TPU v7x, 32 devices: a whole 2x2x4 slice. The times are simulated.
32 devices in a mesh: rows: 16 (over z, y, x), strips: 2 (over core).
Axes of the slice: x: 2, y: 2, z: 4, core: 2. Of those that a mesh axis runs over, the one named last changes fastest.
Arguments:
- left_pixels: int32 [64, 1024], P('rows', 'strips'), may hold values from 2240 to 2368
- right_pixels: int32 [64, 1024], P('rows', 'strips'), may hold values from 2238 to 2370
- valid_mask: int32 [64, 1024], P('rows', 'strips'), may hold values 0 or 1
- first_weight: bfloat16 [64, 1, 3, 3], replicated, may hold values from -6 to 6
- conv_weights: bfloat16 [3, 64, 64, 3, 3], replicated, may hold values from -0.875 to 0.875
Outputs:
- aggregated: float32 [64, 1024, 128], P('rows', 'strips')
All inputs are finite; a program needn't handle non-finite values. No bound on the sum of `valid_mask` on one device may be relied on, other than what follows from the above.
Results may differ from a plain program's by a relative error of at most 0.012.
The roundings to bfloat16 on the way count: a program that leaves them out, or rounds other values in their place, can miss the bound.
Values may be sent and summed in bfloat16 or wider, within the bound.
No kernel may reach another device: no remote copies, remote signals or barrier semaphores. Data moves between devices by JAX's collectives and lax.ppermute only.
A program may use at most 128 MiB of HBM per device.

v0:
```python
import functools
import math

import jax
import jax.numpy as jnp
from jax import lax
from jax.experimental import pallas as pl
from jax.experimental.pallas import tpu as pltpu
from jax.sharding import PartitionSpec as P

DISP = 128
P_SMALL = 0.5
P_LARGE = 2.0
BIG = 3.0e38
CH = 64
EDGE = 8
LANES = 128


def chunking(need):
    best = None
    for size in (128, 144, 160, 176):
        total = -(-need // size) * size
        if best is None or total < best[1]:
            best = (size, total)
    return best


def plan(width):
    steps = [chunking(width)]
    for _ in range(2):
        steps.append(chunking(steps[-1][1] + 2 * EDGE))
    need = steps[-1][1] + 2 * EDGE
    steps.append((128, -(-need // 128) * 128))
    return steps[::-1]


def feature_stack(pix_ref, w1_ref, wt_ref, bufs, sizes, col_of, row_low, row_high, flipped, last_mask_ref):
    def in_image(base, count, lanes, halo, lane0):
        position = lax.broadcasted_iota(jnp.int32, (count, lanes), 0) + base
        row = (lax.broadcasted_iota(jnp.int32, (count, lanes), 1) + lane0) // CH - halo
        low, high = col_of(position)
        return low & high & (row >= row_low) & (row < row_high)

    chunk, total = sizes[0]
    lanes = bufs[0].shape[1]

    def first(index, carry):
        start = pl.multiple_of(index * chunk, chunk)
        value = jnp.dot(pix_ref[pl.ds(start, chunk), :], w1_ref[...], preferred_element_type=jnp.float32)
        inside = in_image(start - 3 * EDGE, chunk, lanes, 3, 0)
        value = jnp.where(inside, jnp.maximum(value, 0.0), 0.0)
        bufs[0][pl.ds(start, chunk), :] = value.astype(jnp.bfloat16)
        return carry

    lax.fori_loop(0, total // chunk, first, 0)

    for layer in range(1, 4):
        source, target = bufs[layer - 1], bufs[layer]
        out_rows = target.shape[1] // CH
        chunk, total = sizes[layer]
        reach = chunk + 2 * EDGE
        for group in range(0, out_rows, 4):
            count = min(4, out_rows - group)
            wide, deep = count * CH, (count + 2) * CH

            def convolve(index, carry, layer=layer, group=group, wide=wide, deep=deep, chunk=chunk, reach=reach, source=source, target=target):
                start = pl.multiple_of(index * chunk, 16)
                block = source[pl.ds(start, reach), group * CH : group * CH + deep]
                parts = [
                    jnp.dot(block, wt_ref[layer - 1, dx, :deep, :wide], preferred_element_type=jnp.float32)
                    for dx in range(3)
                ]
                before, after = (parts[2], parts[0]) if flipped else (parts[0], parts[2])
                value = pltpu.roll(before, 1, 0) + parts[1] + pltpu.roll(after, reach - 1, 0)
                value = value[EDGE : EDGE + chunk]
                halo = 3 - layer
                if layer < 3:
                    value = jnp.maximum(value, 0.0)
                inside = in_image(start - halo * EDGE, chunk, wide, halo, group * CH)
                value = jnp.where(inside, value, 0.0).astype(jnp.bfloat16)
                target[pl.ds(start, chunk), group * CH : group * CH + wide] = value
                return carry

            lax.fori_loop(0, total // chunk, convolve, 0)


def cost_kernel(dims, where_ref, left_ref, right_ref, mask_ref, w1_ref, wt_ref, cost_ref, *bufs):
    rows, cols, total_rows, total_cols = dims
    first_row, first_col = where_ref[0], where_ref[1]
    row_low, row_high = -first_row, total_rows - first_row
    left_bufs, right_bufs = bufs[:4], bufs[4:]

    def left_col(position):
        col = position + first_col
        return col >= 0, col < total_cols

    def right_col(position):
        col = first_col + cols - 1 - position
        return col >= 0, col < total_cols

    feature_stack(left_ref, w1_ref, wt_ref, left_bufs, plan(cols), left_col, row_low, row_high, False, mask_ref)
    feature_stack(right_ref, w1_ref, wt_ref, right_bufs, plan(cols + DISP), right_col, row_low, row_high, True, None)
    left, right = left_bufs[3], right_bufs[3]
    for row in range(rows):
        pair = row // 2 * LANES
        lane = lax.broadcasted_iota(jnp.int32, (LANES, LANES), 1)
        own = (lane // CH) == row % 2

        def block(index, carry, pair=pair, own=own, row=row):
            start = pl.multiple_of(index * LANES, LANES)
            window = pl.multiple_of(cols - LANES - start, LANES)
            scale = mask_ref[pl.ds(start, LANES), pair : pair + LANES]
            a = jnp.where(own, left[pl.ds(start, LANES), pair : pair + LANES] * scale, jnp.zeros((), jnp.bfloat16))
            b = right[pl.ds(window, 2 * LANES), pair : pair + LANES]
            product = lax.dot_general(a, b, (((1,), (1,)), ((), ())), preferred_element_type=jnp.float32)
            skewed = pltpu.roll(product, LANES + 1, 1, stride=1, stride_axis=0)
            cost_ref[row, pl.ds(start, LANES), :] = skewed[:, :LANES]
            return carry

        lax.fori_loop(0, cols // LANES, block, 0)


def cost_volume(left_stack, right_stack, mask, w1, wt, place, rows, cols, total_rows, total_cols):
    bufs = []
    for width in (cols, cols + DISP):
        sizes = plan(width)
        for layer in range(4):
            out_rows = rows + 2 * (3 - layer)
            length = sizes[layer][1]
            bufs.append(pltpu.VMEM((length, out_rows * CH), jnp.bfloat16))
    vmem = pl.BlockSpec(memory_space=pltpu.VMEM)
    return pl.pallas_call(
        functools.partial(cost_kernel, (rows, cols, total_rows, total_cols)),
        out_shape=jax.ShapeDtypeStruct((rows, cols, DISP), jnp.float32),
        in_specs=[pl.BlockSpec(memory_space=pltpu.SMEM)] + [vmem] * 5,
        out_specs=vmem,
        scratch_shapes=bufs,
        compiler_params=pltpu.CompilerParams(vmem_limit_bytes=40 << 20),
        cost_estimate=pl.CostEstimate(flops=8_000_000_000, bytes_accessed=6_000_000, transcendentals=0),
    )(place, left_stack, right_stack, mask, w1, wt)


def row_scan_kernel(dims, has_sum, place_ref, cost_ref, state_ref, *rest):
    rows, cols, flip = dims
    if has_sum:
        lead_ref, out_ref, end_ref, tile_ref, spread_ref, path_ref, low_ref = rest
    else:
        out_ref, end_ref, tile_ref, spread_ref, path_ref, low_ref = rest
    width = LANES // rows
    count = cols // width
    forward = place_ref[2] == (1 if flip else 0)
    lane = lax.broadcasted_iota(jnp.int32, (8, LANES), 1)
    sublane = lax.broadcasted_iota(jnp.int32, (8, LANES), 0)
    lane_base = lane // width * width
    lane_col = lane % width

    def lowest(state):
        level = list(state)
        while len(level) > 1:
            level = [jnp.minimum(level[i], level[i + 1]) for i in range(0, len(level), 2)]
        low = level[0]
        for shift in (4, 2, 1):
            low = jnp.minimum(low, pltpu.roll(low, shift, 0))
        return low

    def one_chunk(index, state):
        chunk = jnp.where(forward, index, count - 1 - index)
        start = pl.multiple_of(chunk * width, width)
        for row in range(rows):
            tile_ref[row * width : (row + 1) * width, :] = cost_ref[row, pl.ds(start, width), :]
        tile_ref[...] = tile_ref[...].T
        planes = [tile_ref[pl.ds(v, 8, stride=16), :] for v in range(16)]

        def spread(step, carry):
            col = jnp.where(forward, step, width - 1 - step)
            index = lane_base + col
            for v in range(16):
                spread_ref[step, v] = jnp.take_along_axis(planes[v], index, axis=1)
            return carry

        lax.fori_loop(0, width, spread, 0, unroll=4)

        def advance(step, state):
            col = jnp.where(forward, step, width - 1 - step)
            mask = lane_col == col
            low = lowest(state)
            bound = low + P_LARGE
            above = jnp.where(sublane == 7, BIG, pltpu.roll(state[0], 7, 0))
            below = jnp.where(sublane == 0, BIG, pltpu.roll(state[15], 1, 0))
            padded = [below] + list(state) + [above]
            fresh = []
            for v in range(16):
                near = jnp.minimum(padded[v], padded[v + 2]) + P_SMALL
                best = jnp.minimum(jnp.minimum(state[v], near), bound)
                value = spread_ref[step, v] + best
                pltpu.store(path_ref.at[v], value, mask=mask)
                fresh.append(value)
            pltpu.store(low_ref, low, mask=mask)
            return tuple(fresh)

        def group(step4, state):
            for k in range(4):
                state = advance(step4 * 4 + k, state)
            return state

        state = lax.fori_loop(0, width // 4, group, state)
        low = low_ref[...]
        for v in range(16):
            tile_ref[pl.ds(v, 8, stride=16), :] = path_ref[v] - low
        done = tile_ref[...].T
        for row in range(rows):
            piece = done[row * width : (row + 1) * width]
            if has_sum:
                piece = piece + lead_ref[row, pl.ds(start, width), :]
            out_ref[row, pl.ds(start, width), :] = piece
        low = lowest(state)
        return tuple(value - low for value in state)

    state = tuple(state_ref[v] for v in range(16))
    state = lax.fori_loop(0, count, one_chunk, state)
    for v in range(16):
        end_ref[v] = state[v]


def row_scan(place, cost, state, lead, flip):
    rows, cols, _ = cost.shape
    width = LANES // rows
    vmem = pl.BlockSpec(memory_space=pltpu.VMEM)
    args = [place, cost, state] + ([] if lead is None else [lead])
    return pl.pallas_call(
        functools.partial(row_scan_kernel, (rows, cols, flip), lead is not None),
        out_shape=(
            jax.ShapeDtypeStruct(cost.shape, jnp.float32),
            jax.ShapeDtypeStruct((16, 8, LANES), jnp.float32),
        ),
        in_specs=[pl.BlockSpec(memory_space=pltpu.SMEM)] + [vmem] * (len(args) - 1),
        out_specs=(vmem, vmem),
        scratch_shapes=[
            pltpu.VMEM((LANES, LANES), jnp.float32),
            pltpu.VMEM((width, 16, 8, LANES), jnp.float32),
            pltpu.VMEM((16, 8, LANES), jnp.float32),
            pltpu.VMEM((8, LANES), jnp.float32),
        ],
        compiler_params=pltpu.CompilerParams(vmem_limit_bytes=24 << 20),
        cost_estimate=pl.CostEstimate(flops=2_000_000_000, bytes_accessed=30_000_000, transcendentals=0),
    )(*args)


def column_kernel(cost_ref, out_ref):
    length, width, _ = cost_ref.shape
    lane = lax.broadcasted_iota(jnp.int32, (width, DISP), 1)

    def step(state, cost):
        low = jnp.min(state, axis=1, keepdims=True)
        above = jnp.where(lane == DISP - 1, BIG, pltpu.roll(state, DISP - 1, 1))
        below = jnp.where(lane == 0, BIG, pltpu.roll(state, 1, 1))
        near = jnp.minimum(above, below) + P_SMALL
        return cost + jnp.minimum(jnp.minimum(state, near), low + P_LARGE) - low

    def first(index, states):
        down = step(states[0], cost_ref[index])
        up = step(states[1], cost_ref[length - 1 - index])
        out_ref[index] = down
        out_ref[length - 1 - index] = up
        return down, up

    def second(index, states):
        down = step(states[0], cost_ref[index])
        up = step(states[1], cost_ref[length - 1 - index])
        out_ref[index] += down
        out_ref[length - 1 - index] += up
        return down, up

    zero = jnp.zeros((width, DISP), jnp.float32)
    states = lax.fori_loop(0, length // 2, first, (zero, zero))
    lax.fori_loop(length // 2, length, second, states)


def column_scan(columns):
    vmem = pl.BlockSpec(memory_space=pltpu.VMEM)
    return pl.pallas_call(
        column_kernel,
        out_shape=jax.ShapeDtypeStruct(columns.shape, jnp.float32),
        in_specs=[vmem],
        out_specs=vmem,
        compiler_params=pltpu.CompilerParams(vmem_limit_bytes=24 << 20),
        cost_estimate=pl.CostEstimate(flops=200_000_000, bytes_accessed=2_000_000, transcendentals=0),
    )(columns)


def normalize(image_pixels):
    return (image_pixels.astype(jnp.float32) / 1024.0 - 2.0).astype(jnp.bfloat16)


def layer_weights(conv_weights, rows_in, rows_out):
    base = jnp.transpose(conv_weights, (0, 4, 3, 2, 1))
    taps = base.shape[2]
    columns = [
        jnp.pad(base, ((0, 0), (0, 0), (row, rows_in - taps - row), (0, 0), (0, 0)))
        for row in range(rows_out)
    ]
    joined = jnp.concatenate(columns, axis=-1)
    return joined.reshape(base.shape[0], base.shape[1], rows_in * base.shape[3], rows_out * base.shape[4])


def neighbours(pair, row_axis, strip_axis):
    groups, strips = lax.axis_size(row_axis), lax.axis_size(strip_axis)
    axes = (row_axis, strip_axis)
    strip = lax.axis_index(strip_axis)

    def moved(up, across):
        route = []
        for r in range(groups):
            for s in range(strips):
                source = (r + up, s ^ across)
                if 0 <= source[0] < groups:
                    route.append((source[0] * strips + source[1], r * strips + s))
        return lax.ppermute(pair, axes, route)

    bands = []
    for up in (-1, 0, 1):
        own = pair if up == 0 else moved(up, 0)
        other = moved(up, 1)
        joined = jnp.where(strip == 0, jnp.concatenate([own, other], 2), jnp.concatenate([other, own], 2))
        bands.append(joined)
    return jnp.concatenate(bands, axis=1)


def stacked(image, start, length, flipped):
    parts = []
    for dx in range(3):
        part = lax.dynamic_slice_in_dim(image, start + dx - 1, length, 1)
        parts.append(part[:, ::-1] if flipped else part)
    joined = jnp.concatenate(parts, axis=0)
    joined = jnp.pad(joined, ((0, LANES - joined.shape[0]), (0, 0)))
    return joined.T


def per_device(left_pixels, right_pixels, valid_mask, first_weight, conv_weights):
    rows, cols = left_pixels.shape
    groups, strips = lax.axis_size("rows"), lax.axis_size("strips")
    group, strip = lax.axis_index("rows"), lax.axis_index("strips")
    total_rows, total_cols = rows * groups, cols * strips

    wt = layer_weights(conv_weights, 6, 4)
    w1 = layer_weights(first_weight[None], rows + 8, rows + 6)[0].reshape(3 * (rows + 8), (rows + 6) * CH)
    w1 = jnp.pad(w1, ((0, LANES - w1.shape[0]), (0, 0)))

    pair = jnp.stack([normalize(left_pixels), normalize(right_pixels)])
    band = neighbours(pair, "rows", "strips")[:, rows - 4 : 2 * rows + 4]
    left_length, right_length = plan(cols)[0][1], plan(cols + DISP)[0][1]
    margin = right_length + 8
    band = jnp.pad(band, ((0, 0), (0, 0), (margin, margin)))
    first_col = strip * cols
    left_stack = stacked(band[0], margin + first_col - 3 * EDGE, left_length, False)
    right_start = first_col + cols - 1 + 3 * EDGE - (right_length - 1)
    right_stack = stacked(band[1], margin + right_start, right_length, True)
    scale = -1.0 / math.sqrt(CH)
    mask = jnp.repeat((valid_mask.astype(jnp.float32) * scale).astype(jnp.bfloat16).T, CH, axis=1)
    place = jnp.stack([group * rows, first_col, strip]).astype(jnp.int32)

    cost = cost_volume(left_stack, right_stack, mask, w1, wt, place, rows, cols, total_rows, total_cols)

    per_group = cols // groups
    grouped = jnp.swapaxes(cost.reshape(rows, groups, per_group, DISP), 0, 1)
    columns = lax.all_to_all(grouped, "rows", split_axis=0, concat_axis=0, tiled=True)
    columns = columns.reshape(total_rows, per_group, DISP)

    zero = jnp.zeros((16, 8, LANES), jnp.float32)
    leading, end = row_scan(place, cost, zero, None, False)
    received = lax.ppermute(end, "strips", [(i, i ^ 1) for i in range(strips)])
    column_sum = column_scan(columns)
    vertical = lax.all_to_all(
        column_sum.reshape(groups, rows, per_group, DISP), "rows", split_axis=0, concat_axis=0, tiled=True
    )
    horizontal, _ = row_scan(place, cost, received, leading, True)
    vertical = jnp.swapaxes(vertical, 0, 1).reshape(rows, cols, DISP)
    return horizontal + vertical


def solution(mesh):
    in_specs = (P("rows", "strips"), P("rows", "strips"), P("rows", "strips"), P(), P())
    out_specs = P("rows", "strips", None)
    return jax.shard_map(
        per_device, mesh=mesh, in_specs=in_specs, out_specs=out_specs, check_vma=False
    )
```

profile of v0, /device:TPU:0, one launch (start us, length us, event | category | flops | bytes accessed | tf_op | source)
XLA Modules:
  0.0 162.2 jit_solution(17931068822740685328)
XLA Ops:
  0.0 0.0 copy-start
  0.0 0.0 copy-start.1
  0.0 0.7 fusion.15
  0.8 4.8 %collective-permute-start = (bf16[2,4,512]{2,1,0:T(4,128)(2,1)S(1)}, bf16[2,4,512]{2,1,0:T(4,128)(2,1)S(1)}, u32[]{:S(2)}, u32[]{:S(2)}) collective-permute-start(bf16[2,4,512]{2,1,0:T(4,128)(2,1)S(1)} %pad_maximum_fusion.2), channel_id=1, source_target_pairs={{0,2},{1,3},{2,4},{3,5},{4,6},{5,7},{6,8},{7,9},{8,10},{9,11},{10,... | collective-permute-start | bytes 24584 | tf_op jit(solution)/shard_map/ppermute | solution.py:319
  5.6 2.6 %collective-permute-start.1 = (bf16[2,4,512]{2,1,0:T(4,128)(2,1)S(1)}, bf16[2,4,512]{2,1,0:T(4,128)(2,1)S(1)}, u32[]{:S(2)}, u32[]{:S(2)}) collective-permute-start(bf16[2,4,512]{2,1,0:T(4,128)(2,1)S(1)} %pad_maximum_fusion.2), channel_id=1, source_target_pairs={{1,2},{0,3},{3,4},{2,5},{5,6},{4,7},{7,8},{6,9},{9,10},{8,11},{11,... | collective-permute-start | bytes 24584 | tf_op jit(solution)/shard_map/ppermute | solution.py:319
  8.2 1.3 collective-permute-start.3
  9.5 1.3 collective-permute-start.4
  10.8 1.0 collective-permute-start.2
  11.8 1.0 fusion.19
  12.8 4.7 %fusion.7 = bf16[3,3,6,64,256]{3,4,1,2,0:T(8,128)(2,1)} fusion(bf16[3,3,3,64,64]{3,4,1,2,0:T(8,128)(2,1)} %bitcast.47), kind=kLoop, calls=%fused_computation.13 | loop fusion | flops 17694720 | bytes 1990656 | tf_op jit(solution)/shard_map/concatenate | solution.py:303
  17.5 0.0 copy-done.1
  17.6 0.1 pad_add_fusion.where_ref.place_ref
  17.6 0.0 copy-done
  17.6 0.2 concatenate.42
  17.9 3.5 %copy.31 = bf16[3,3,6,64,256]{4,3,2,1,0:T(8,128)(2,1)S(1)} copy(bf16[3,3,6,64,256]{3,4,1,2,0:T(8,128)(2,1)} %fusion.7) | data formatting | bytes 3538944 | tf_op jit(solution)/shard_map/concatenate | solution.py:303
  21.5 0.1 copy.32.mask_ref
  21.6 0.0 collective-permute-done.2
  21.6 0.0 collective-permute-done
  21.6 0.0 collective-permute-done.1
  21.7 0.0 collective-permute-done.3
  21.7 0.0 collective-permute-done.4
  21.7 0.1 fusion.14
  21.9 0.1 dynamic-slice_bitcast_fusion.2
  22.0 0.5 rev.10
  22.5 0.5 rev.11
  23.0 0.5 rev.9
  23.5 0.2 copy.29
  23.7 0.1 dynamic-slice_bitcast_fusion.5
  23.8 0.2 copy.28
  24.1 18.7 %shard_map.55.cost_ref = f32[4,512,128]{2,1,0:T(8,128)S(1)} custom-call(s32[3]{0:T(128)S(1)} %pad_add_fusion.where_ref.place_ref, bf16[640,128]{1,0:T(8,128)(2,1)S(1)} %pad_bitcast_fusion.1.left_ref, bf16[768,128]{1,0:T(8,128)(2,1)S(1)} %pad_bitcast_fusion.right_ref, bf16[512,256]{1,0:T(8,128)(2,1)S(1)} %copy.32.mask_ref, bf16[128,640]{1,0:T(8,128)(2,1)S(1)} %pad.84.w1_ref, ...), custom_call_target="tpu_custom_call" | custom-call | flops 8000000000 | bytes 6000000 | tf_op jit(solution)/shard_map/pallas_call | solution.py:133
  42.8 0.1 copy.36
  42.9 35.9 %all_to_all.10 = f32[16,4,32,128]{3,2,1,0:T(8,128)S(1)} all-to-all(f32[16,4,32,128]{3,2,1,0:T(8,128)S(1)} %bitcast.45), channel_id=1, replica_groups=mesh['rows'=16,'strips'=2] {'rows'}, dimensions={0} | all-to-all | bytes 2097152 | tf_op jit(solution)/shard_map/all_to_all | solution.py:367
  78.8 8.6 %shard_map.58 = f32[64,32,128]{2,1,0:T(8,128)} custom-call(f32[64,32,128]{2,1,0:T(8,128)S(1)} %bitcast.42), custom_call_target="tpu_custom_call" | custom-call | flops 200000000 | bytes 2000000 | tf_op jit(solution)/shard_map/pallas_call | solution.py:282
  87.4 4.3 %all-to-all-start.1 = ((f32[16,4,32,128]{3,2,1,0:T(8,128)}), f32[16,4,32,128]{3,2,1,0:T(8,128)}, u32[]{:S(2)}, u32[]{:S(2)}) async-start(f32[16,4,32,128]{3,2,1,0:T(8,128)} %bitcast.23), calls=%async_computation.1 | async-start | bytes 2097152 | tf_op jit(solution)/shard_map/all_to_all | solution.py:374
  91.8 33.0 %shard_map.56 = (f32[4,512,128]{2,1,0:T(8,128)S(1)}, f32[16,8,128]{2,1,0:T(8,128)S(1)}) custom-call(s32[3]{0:T(128)S(1)} %pad_add_fusion.where_ref.place_ref, f32[4,512,128]{2,1,0:T(8,128)S(1)} %shard_map.55.cost_ref, f32[16,8,128]{2,1,0:T(8,128)S(1)} %broadcast_in_dim.11.state_ref), custom_call_target="tpu_custom_call" | custom-call | flops 2000000000 | bytes 30000000 | tf_op jit(solution)/shard_map/pallas_call | solution.py:231
  124.8 0.1 collective-permute-start.5
  124.9 1.2 collective-permute-done.5.state_ref
  126.2 33.6 %shard_map.57 = (f32[4,512,128]{2,1,0:T(8,128)S(1)}, f32[16,8,128]{2,1,0:T(8,128)}) custom-call(s32[3]{0:T(128)S(1)} %pad_add_fusion.where_ref.place_ref, f32[4,512,128]{2,1,0:T(8,128)S(1)} %shard_map.55.cost_ref, f32[16,8,128]{2,1,0:T(8,128)S(1)} %collective-permute-done.5.state_ref, f32[4,512,128]{2,1,0:T(8,128)S(1)} %get-tuple-element.9.rest_0_), custom_call_target="tpu_custom_call" | custom-call | flops 2000000000 | bytes 30000000 | tf_op jit(solution)/shard_map/pallas_call | solution.py:231
  159.8 0.0 all-to-all-done.1
  159.8 1.3 copy.34
  161.1 1.1 bitcast_add_fusion
  (16 shorter events, 0.3 us)
Async XLA Ops:
  0.0 17.6 %copy-start = (bf16[64,1,3,3]{0,3,2,1:T(4,128)(2,1)S(1)}, bf16[64,1,3,3]{0,3,2,1:T(4,128)(2,1)}, u32[]{:S(2)}) copy-start(bf16[64,1,3,3]{0,3,2,1:T(4,128)(2,1)} %param.8) | copy-start | bytes 3460
  0.0 17.5 %copy-start.1 = (s32[4,512]{1,0:T(4,128)S(1)}, s32[4,512]{1,0:T(4,128)}, u32[]{:S(2)}) copy-start(s32[4,512]{1,0:T(4,128)} %param.7) | copy-start | bytes 24580
  0.8 20.9 %collective-permute-start = (bf16[2,4,512]{2,1,0:T(4,128)(2,1)S(1)}, bf16[2,4,512]{2,1,0:T(4,128)(2,1)S(1)}, u32[]{:S(2)}, u32[]{:S(2)}) collective-permute-start(bf16[2,4,512]{2,1,0:T(4,128)(2,1)S(1)} %pad_maximum_fusion.2), channel_id=1, source_target_pairs={{0,2},{1,3},{2,4},{3,5},{4,6},{5,7},{6,8},{7,9},{8,10},{9,11},{10,... | collective-permute-start | bytes 24584 | tf_op jit(solution)/shard_map/ppermute | solution.py:319
  5.6 16.0 %collective-permute-start.1 = (bf16[2,4,512]{2,1,0:T(4,128)(2,1)S(1)}, bf16[2,4,512]{2,1,0:T(4,128)(2,1)S(1)}, u32[]{:S(2)}, u32[]{:S(2)}) collective-permute-start(bf16[2,4,512]{2,1,0:T(4,128)(2,1)S(1)} %pad_maximum_fusion.2), channel_id=1, source_target_pairs={{1,2},{0,3},{3,4},{2,5},{5,6},{4,7},{7,8},{6,9},{9,10},{8,11},{11,... | collective-permute-start | bytes 24584 | tf_op jit(solution)/shard_map/ppermute | solution.py:319
  8.2 13.5 %collective-permute-start.3 = (bf16[2,4,512]{2,1,0:T(4,128)(2,1)S(1)}, bf16[2,4,512]{2,1,0:T(4,128)(2,1)S(1)}, u32[]{:S(2)}, u32[]{:S(2)}) collective-permute-start(bf16[2,4,512]{2,1,0:T(4,128)(2,1)S(1)} %pad_maximum_fusion.2), channel_id=1, source_target_pairs={{2,0},{3,1},{4,2},{5,3},{6,4},{7,5},{8,6},{9,7},{10,8},{11,9},{12,... | collective-permute-start | bytes 24584 | tf_op jit(solution)/shard_map/ppermute | solution.py:319
  9.5 12.2 %collective-permute-start.4 = (bf16[2,4,512]{2,1,0:T(4,128)(2,1)S(1)}, bf16[2,4,512]{2,1,0:T(4,128)(2,1)S(1)}, u32[]{:S(2)}, u32[]{:S(2)}) collective-permute-start(bf16[2,4,512]{2,1,0:T(4,128)(2,1)S(1)} %pad_maximum_fusion.2), channel_id=1, source_target_pairs={{3,0},{2,1},{5,2},{4,3},{7,4},{6,5},{9,6},{8,7},{11,8},{10,9},{13,... | collective-permute-start | bytes 24584 | tf_op jit(solution)/shard_map/ppermute | solution.py:319
  10.8 10.8 %collective-permute-start.2 = (bf16[2,4,512]{2,1,0:T(4,128)(2,1)S(1)}, bf16[2,4,512]{2,1,0:T(4,128)(2,1)S(1)}, u32[]{:S(2)}, u32[]{:S(2)}) collective-permute-start(bf16[2,4,512]{2,1,0:T(4,128)(2,1)S(1)} %pad_maximum_fusion.2), channel_id=1, source_target_pairs={{1,0},{0,1},{3,2},{2,3},{5,4},{4,5},{7,6},{6,7},{9,8},{8,9},{11,10... | collective-permute-start | bytes 24584 | tf_op jit(solution)/shard_map/ppermute | solution.py:319
  87.4 72.3 %all-to-all-start.1 = ((f32[16,4,32,128]{3,2,1,0:T(8,128)}), f32[16,4,32,128]{3,2,1,0:T(8,128)}, u32[]{:S(2)}, u32[]{:S(2)}) async-start(f32[16,4,32,128]{3,2,1,0:T(8,128)} %bitcast.23), calls=%async_computation.1 | async-start | bytes 2097152 | tf_op jit(solution)/shard_map/all_to_all | solution.py:374
  124.8 1.3 collective-permute-start.5
where the time goes:
time: 163 us; the launch traced here: 162 us
  Pallas kernels  94 us (58%)
  blocking collectives  35.9 us (22%)
  starting transfers between devices  15.4 us (9%)
  local copies, waits for them, and re-layouts  8.49 us (5%)
  other arithmetic  6.8 us (4%)
    pallas_call x2, Pallas kernels, row_scan(): pl.pallas_call(functools.partial(row_scan_kernel, (rows, cols, flip), lea...  66.7 us
    all_to_all x1, blocking collectives, per_device(): lax.all_to_all(grouped, 'rows', split_axis=0, concat_axis=0, tiled=True)  35.9 us
    pallas_call x1, Pallas kernels, cost_volume(): pl.pallas_call(functools.partial(cost_kernel, (rows, cols, total_rows, to...  18.7 us
    ppermute x5, starting transfers between devices, moved(): return lax.ppermute(pair, axes, route)  11 us
    pallas_call x1, Pallas kernels, column_scan(): pl.pallas_call(column_kernel, out_shape=jax.ShapeDtypeStruct(columns.shap...  8.63 us
    concatenate x1, other arithmetic, layer_weights(): joined = jnp.concatenate(columns, axis=-1)  4.69 us
    all_to_all x1, starting transfers between devices, per_device(): lax.all_to_all(column_sum.reshape(groups, rows, per_group, DISP), 'rows',...  4.34 us
    concatenate x3, local copies, waits for them, and re-layouts, layer_weights(): joined = jnp.concatenate(columns, axis=-1)  3.72 us
  transfers between devices with their start and end apart: 7, of which 1 were waited for; matrix products, arithmetic and copies ran while one was open for 6% of the time, Pallas kernels for 41%

commit v1 on v0

--- a/solution.py
+++ b/solution.py
@@ -15,6 +15,7 @@
 CH = 64
 EDGE = 8
 LANES = 128
+BATCH = 4
 
 
 def chunking(need):
@@ -142,18 +143,25 @@
 
 
 def row_scan_kernel(dims, has_sum, place_ref, cost_ref, state_ref, *rest):
-    rows, cols, flip = dims
+    rows, cols, flip, batch = dims
     if has_sum:
-        lead_ref, out_ref, end_ref, tile_ref, spread_ref, path_ref, low_ref = rest
-    else:
-        out_ref, end_ref, tile_ref, spread_ref, path_ref, low_ref = rest
+        lead_ref, rest = rest[0], rest[1:]
+    out_ref, end_ref, tile_ref, turn_ref, pick_ref, split_ref, even_ref, odd_ref, path_ref, low_ref = rest
     width = LANES // rows
     count = cols // width
     forward = place_ref[2] == (1 if flip else 0)
     lane = lax.broadcasted_iota(jnp.int32, (8, LANES), 1)
     sublane = lax.broadcasted_iota(jnp.int32, (8, LANES), 0)
-    lane_base = lane // width * width
     lane_col = lane % width
+
+    def build_pick(pair, carry):
+        k = lax.broadcasted_iota(jnp.int32, (2 * LANES, 2 * LANES), 0) % LANES
+        n = lax.broadcasted_iota(jnp.int32, (2 * LANES, 2 * LANES), 1)
+        wanted = n % LANES // width * width + 2 * pair + n // LANES
+        pick_ref[pair] = jnp.where(k == wanted, 1.0, 0.0).astype(jnp.bfloat16)
+        return carry
+
+    lax.fori_loop(0, width // 2, build_pick, 0)
 
     def lowest(state):
         level = list(state)
@@ -164,61 +172,94 @@
             low = jnp.minimum(low, pltpu.roll(low, shift, 0))
         return low
 
-    def one_chunk(index, state):
+    def chunk_start(index):
         chunk = jnp.where(forward, index, count - 1 - index)
-        start = pl.multiple_of(chunk * width, width)
+        return pl.multiple_of(chunk * width, width)
+
+    def split(base, slot):
+        start = chunk_start(base + slot)
         for row in range(rows):
-            tile_ref[row * width : (row + 1) * width, :] = cost_ref[row, pl.ds(start, width), :]
-        tile_ref[...] = tile_ref[...].T
-        planes = [tile_ref[pl.ds(v, 8, stride=16), :] for v in range(16)]
-
-        def spread(step, carry):
-            col = jnp.where(forward, step, width - 1 - step)
-            index = lane_base + col
+            tile_ref[slot, row * width : (row + 1) * width, :] = cost_ref[row, pl.ds(start, width), :]
+        tile_ref[slot] = tile_ref[slot].T
+        for v in range(0, 16, 2):
+            plane = jnp.concatenate(
+                [tile_ref[slot, pl.ds(v, 8, stride=16), :], tile_ref[slot, pl.ds(v + 1, 8, stride=16), :]], axis=0
+            )
+            high = plane.astype(jnp.bfloat16)
+            split_ref[slot * LANES + v * 8 : slot * LANES + v * 8 + 16, :LANES] = high
+            split_ref[slot * LANES + v * 8 : slot * LANES + v * 8 + 16, LANES:] = (plane - high.astype(jnp.float32)).astype(jnp.bfloat16)
+
+    def spread(target, pair):
+        weight = pick_ref[pair]
+        both = jnp.dot(split_ref[...], weight, preferred_element_type=jnp.float32)
+        for slot in range(batch):
+            target[slot, 2 * pair] = both[slot * LANES : slot * LANES + LANES, :LANES]
+            target[slot, 2 * pair + 1] = both[slot * LANES : slot * LANES + LANES, LANES:]
+
+    def one_batch(number, state, current, coming):
+        base = number * batch
+        later = jnp.minimum(base + batch, count - batch)
+        for slot in range(batch):
+            split(later, slot)
+
+        def one_chunk(slot, state):
+            def advance(step, state):
+                col = jnp.where(forward, step, width - 1 - step)
+                mask = lane_col == col
+                low = lowest(state)
+                bound = low + P_LARGE
+                above = jnp.where(sublane == 7, BIG, pltpu.roll(state[0], 7, 0))
+                below = jnp.where(sublane == 0, BIG, pltpu.roll(state[15], 1, 0))
+                padded = [below] + list(state) + [above]
+                fresh = []
+                for v in range(16):
+                    near = jnp.minimum(padded[v], padded[v + 2]) + P_SMALL
+                    best = jnp.minimum(jnp.minimum(state[v], near), bound)
+                    value = current[slot, col, v * 8 : v * 8 + 8, :] + best
+                    pltpu.store(path_ref.at[v], value, mask=mask)
+                    fresh.append(value)
+                pltpu.store(low_ref, low, mask=mask)
+                return tuple(fresh)
+
+            per_pair = 2 * batch
+
+            def group(index, state):
+                spread(coming, slot * (width // per_pair) + index)
+                for k in range(per_pair):
+                    state = advance(index * per_pair + k, state)
+                return state
+
+            state = lax.fori_loop(0, width // per_pair, group, state)
+            start = chunk_start(base + slot)
+            low = low_ref[...]
             for v in range(16):
-                spread_ref[step, v] = jnp.take_along_axis(planes[v], index, axis=1)
-            return carry
-
-        lax.fori_loop(0, width, spread, 0, unroll=4)
-
-        def advance(step, state):
-            col = jnp.where(forward, step, width - 1 - step)
-            mask = lane_col == col
+                turn_ref[pl.ds(v, 8, stride=16), :] = path_ref[v] - low
+            done = turn_ref[...].T
+            for row in range(rows):
+                piece = done[row * width : (row + 1) * width]
+                if has_sum:
+                    piece = piece + lead_ref[row, pl.ds(start, width), :]
+                out_ref[row, pl.ds(start, width), :] = piece
             low = lowest(state)
-            bound = low + P_LARGE
-            above = jnp.where(sublane == 7, BIG, pltpu.roll(state[0], 7, 0))
-            below = jnp.where(sublane == 0, BIG, pltpu.roll(state[15], 1, 0))
-            padded = [below] + list(state) + [above]
-            fresh = []
-            for v in range(16):
-                near = jnp.minimum(padded[v], padded[v + 2]) + P_SMALL
-                best = jnp.minimum(jnp.minimum(state[v], near), bound)
-                value = spread_ref[step, v] + best
-                pltpu.store(path_ref.at[v], value, mask=mask)
-                fresh.append(value)
-            pltpu.store(low_ref, low, mask=mask)
-            return tuple(fresh)
-
-        def group(step4, state):
-            for k in range(4):
-                state = advance(step4 * 4 + k, state)
-            return state
-
-        state = lax.fori_loop(0, width // 4, group, state)
-        low = low_ref[...]
-        for v in range(16):
-            tile_ref[pl.ds(v, 8, stride=16), :] = path_ref[v] - low
-        done = tile_ref[...].T
-        for row in range(rows):
-            piece = done[row * width : (row + 1) * width]
-            if has_sum:
-                piece = piece + lead_ref[row, pl.ds(start, width), :]
-            out_ref[row, pl.ds(start, width), :] = piece
-        low = lowest(state)
-        return tuple(value - low for value in state)
+            return tuple(value - low for value in state)
+
+        return lax.fori_loop(0, batch, one_chunk, state)
+
+    for slot in range(batch):
+        split(0, slot)
+
+    def first(pair, carry):
+        spread(even_ref, pair)
+        return carry
+
+    lax.fori_loop(0, width // 2, first, 0)
+
+    def two_batches(index, state):
+        state = one_batch(2 * index, state, even_ref, odd_ref)
+        return one_batch(2 * index + 1, state, odd_ref, even_ref)
 
     state = tuple(state_ref[v] for v in range(16))
-    state = lax.fori_loop(0, count, one_chunk, state)
+    state = lax.fori_loop(0, count // batch // 2, two_batches, state)
     for v in range(16):
         end_ref[v] = state[v]
 
@@ -226,10 +267,11 @@
 def row_scan(place, cost, state, lead, flip):
     rows, cols, _ = cost.shape
     width = LANES // rows
+    batch = math.gcd(cols // width // 2, BATCH)
     vmem = pl.BlockSpec(memory_space=pltpu.VMEM)
     args = [place, cost, state] + ([] if lead is None else [lead])
     return pl.pallas_call(
-        functools.partial(row_scan_kernel, (rows, cols, flip), lead is not None),
+        functools.partial(row_scan_kernel, (rows, cols, flip, batch), lead is not None),
         out_shape=(
             jax.ShapeDtypeStruct(cost.shape, jnp.float32),
             jax.ShapeDtypeStruct((16, 8, LANES), jnp.float32),
@@ -237,12 +279,16 @@
         in_specs=[pl.BlockSpec(memory_space=pltpu.SMEM)] + [vmem] * (len(args) - 1),
         out_specs=(vmem, vmem),
         scratch_shapes=[
+            pltpu.VMEM((batch, LANES, LANES), jnp.float32),
             pltpu.VMEM((LANES, LANES), jnp.float32),
-            pltpu.VMEM((width, 16, 8, LANES), jnp.float32),
+            pltpu.VMEM((width // 2, 2 * LANES, 2 * LANES), jnp.bfloat16),
+            pltpu.VMEM((batch * LANES, 2 * LANES), jnp.bfloat16),
+            pltpu.VMEM((batch, width, LANES, LANES), jnp.float32),
+            pltpu.VMEM((batch, width, LANES, LANES), jnp.float32),
             pltpu.VMEM((16, 8, LANES), jnp.float32),
             pltpu.VMEM((8, LANES), jnp.float32),
         ],
-        compiler_params=pltpu.CompilerParams(vmem_limit_bytes=24 << 20),
+        compiler_params=pltpu.CompilerParams(vmem_limit_bytes=40 << 20),
         cost_estimate=pl.CostEstimate(flops=2_000_000_000, bytes_accessed=30_000_000, transcendentals=0),
     )(*args)
 
@@ -369,8 +415,9 @@
 
     zero = jnp.zeros((16, 8, LANES), jnp.float32)
     leading, end = row_scan(place, cost, zero, None, False)
+    columns, end = lax.optimization_barrier((columns, end))
+    column_sum = column_scan(columns)
     received = lax.ppermute(end, "strips", [(i, i ^ 1) for i in range(strips)])
-    column_sum = column_scan(columns)
     vertical = lax.all_to_all(
         column_sum.reshape(groups, rows, per_group, DISP), "rows", split_axis=0, concat_axis=0, tiled=True
     )

time: 163 us -> 124 us (0.76)
  blocking collectives: 35.9 us -> 0 us
  Pallas kernels: 94 us -> 75.4 us
  starting transfers between devices: 15.4 us -> 27.3 us
  local copies, waits for them, and re-layouts: 8.49 us -> 11.7 us
    all_to_all x1 -> x0, blocking collectives: 35.9 us -> none  [per_device(): lax.all_to_all(grouped, 'rows', split_axis=0, concat_axis=0, tiled=True)]
    pallas_call x2, Pallas kernels: 66.7 us -> 48.1 us  [row_scan(): pl.pallas_call(functools.partial(row_scan_kernel, (rows, cols, flip, batc...]
    all_to_all x0 -> x1, starting transfers between devices: none -> 9.41 us  [per_device(): lax.all_to_all(grouped, 'rows', split_axis=0, concat_axis=0, tiled=True)]
    all_to_all x1, starting transfers between devices: 4.34 us -> 6.85 us  [per_device(): lax.all_to_all(column_sum.reshape(groups, rows, per_group, DISP), 'rows',...]
    unnamed x4 -> x8, local copies, waits for them, and re-layouts: 0.01 us -> 2.2 us
  transfers between devices with their start and end apart: 7 -> 8, of which waited for: 1 -> 2; matrix products, arithmetic and copies ran while one was open for 6% -> 8% of each run, Pallas kernels for 41% -> 39%
where the time goes in v1:
time: 124 us; the launch traced here: 123 us
  Pallas kernels  75.4 us (61%)
  starting transfers between devices  27.3 us (22%)
  local copies, waits for them, and re-layouts  11.7 us (9%)
  other arithmetic  6.82 us (6%)
  waiting for transfers between devices  1.37 us (1%)
    pallas_call x2, Pallas kernels, row_scan(): pl.pallas_call(functools.partial(row_scan_kernel, (rows, cols, flip, batc...  48.1 us
    pallas_call x1, Pallas kernels, cost_volume(): pl.pallas_call(functools.partial(cost_kernel, (rows, cols, total_rows, to...  18.7 us
    ppermute x5, starting transfers between devices, moved(): return lax.ppermute(pair, axes, route)  11 us
    all_to_all x1, starting transfers between devices, per_device(): lax.all_to_all(grouped, 'rows', split_axis=0, concat_axis=0, tiled=True)  9.41 us
    pallas_call x1, Pallas kernels, column_scan(): pl.pallas_call(column_kernel, out_shape=jax.ShapeDtypeStruct(columns.shap...  8.64 us
    all_to_all x1, starting transfers between devices, per_device(): lax.all_to_all(column_sum.reshape(groups, rows, per_group, DISP), 'rows',...  6.85 us
    concatenate x1, other arithmetic, layer_weights(): joined = jnp.concatenate(columns, axis=-1)  4.7 us
    concatenate x3, local copies, waits for them, and re-layouts, layer_weights(): joined = jnp.concatenate(columns, axis=-1)  3.71 us
  transfers between devices with their start and end apart: 8, of which 2 were waited for; matrix products, arithmetic and copies ran while one was open for 8% of the time, Pallas kernels for 39%

profile of v1, /device:TPU:0, one launch (start us, length us, event | category | flops | bytes accessed | tf_op | source)
XLA Modules:
  0.0 122.9 jit_solution(382309757092462032)
XLA Ops:
  0.0 0.0 copy-start.2
  0.0 0.0 copy-start.3
  0.0 0.7 fusion.15
  0.8 4.8 %collective-permute-start = (bf16[2,4,512]{2,1,0:T(4,128)(2,1)S(1)}, bf16[2,4,512]{2,1,0:T(4,128)(2,1)S(1)}, u32[]{:S(2)}, u32[]{:S(2)}) collective-permute-start(bf16[2,4,512]{2,1,0:T(4,128)(2,1)S(1)} %pad_maximum_fusion.2), channel_id=1, source_target_pairs={{0,2},{1,3},{2,4},{3,5},{4,6},{5,7},{6,8},{7,9},{8,10},{9,11},{10,... | collective-permute-start | bytes 24584 | tf_op jit(solution)/shard_map/ppermute | solution.py:365
  5.6 2.6 %collective-permute-start.1 = (bf16[2,4,512]{2,1,0:T(4,128)(2,1)S(1)}, bf16[2,4,512]{2,1,0:T(4,128)(2,1)S(1)}, u32[]{:S(2)}, u32[]{:S(2)}) collective-permute-start(bf16[2,4,512]{2,1,0:T(4,128)(2,1)S(1)} %pad_maximum_fusion.2), channel_id=1, source_target_pairs={{1,2},{0,3},{3,4},{2,5},{5,6},{4,7},{7,8},{6,9},{9,10},{8,11},{11,... | collective-permute-start | bytes 24584 | tf_op jit(solution)/shard_map/ppermute | solution.py:365
  8.2 1.3 %collective-permute-start.3 = (bf16[2,4,512]{2,1,0:T(4,128)(2,1)S(1)}, bf16[2,4,512]{2,1,0:T(4,128)(2,1)S(1)}, u32[]{:S(2)}, u32[]{:S(2)}) collective-permute-start(bf16[2,4,512]{2,1,0:T(4,128)(2,1)S(1)} %pad_maximum_fusion.2), channel_id=1, source_target_pairs={{2,0},{3,1},{4,2},{5,3},{6,4},{7,5},{8,6},{9,7},{10,8},{11,9},{12,... | collective-permute-start | bytes 24584 | tf_op jit(solution)/shard_map/ppermute | solution.py:365
  9.5 1.3 %collective-permute-start.4 = (bf16[2,4,512]{2,1,0:T(4,128)(2,1)S(1)}, bf16[2,4,512]{2,1,0:T(4,128)(2,1)S(1)}, u32[]{:S(2)}, u32[]{:S(2)}) collective-permute-start(bf16[2,4,512]{2,1,0:T(4,128)(2,1)S(1)} %pad_maximum_fusion.2), channel_id=1, source_target_pairs={{3,0},{2,1},{5,2},{4,3},{7,4},{6,5},{9,6},{8,7},{11,8},{10,9},{13,... | collective-permute-start | bytes 24584 | tf_op jit(solution)/shard_map/ppermute | solution.py:365
  10.8 1.0 collective-permute-start.2
  11.8 1.0 fusion.19
  12.8 4.7 %fusion.7 = bf16[3,3,6,64,256]{3,4,1,2,0:T(8,128)(2,1)} fusion(bf16[3,3,3,64,64]{3,4,1,2,0:T(8,128)(2,1)} %bitcast.46), kind=kLoop, calls=%fused_computation.13 | loop fusion | flops 17694720 | bytes 1990656 | tf_op jit(solution)/shard_map/concatenate | solution.py:349
  17.6 0.0 copy-done.3
  17.6 0.1 pad_add_fusion.where_ref.place_ref
  17.6 0.0 copy-done.2
  17.7 0.2 concatenate.42
  17.9 3.5 %copy.31 = bf16[3,3,6,64,256]{4,3,2,1,0:T(8,128)(2,1)S(1)} copy(bf16[3,3,6,64,256]{3,4,1,2,0:T(8,128)(2,1)} %fusion.7) | data formatting | bytes 3538944 | tf_op jit(solution)/shard_map/concatenate | solution.py:349
  21.5 0.1 copy.32.mask_ref
  21.6 0.0 collective-permute-done.2
  21.6 0.0 collective-permute-done
  21.7 0.0 collective-permute-done.1
  21.7 0.0 collective-permute-done.3
  21.7 0.0 collective-permute-done.4
  21.7 0.1 fusion.14
  21.9 0.1 dynamic-slice_bitcast_fusion.2
  22.0 0.5 rev.10
  22.5 0.5 rev.11
  23.0 0.5 rev.9
  23.5 0.2 copy.29
  23.7 0.1 dynamic-slice_bitcast_fusion.5
  23.8 0.2 copy.28
  24.1 18.7 %shard_map.55.cost_ref = f32[4,512,128]{2,1,0:T(8,128)S(1)} custom-call(s32[3]{0:T(128)S(1)} %pad_add_fusion.where_ref.place_ref, bf16[640,128]{1,0:T(8,128)(2,1)S(1)} %pad_bitcast_fusion.1.left_ref, bf16[768,128]{1,0:T(8,128)(2,1)S(1)} %pad_bitcast_fusion.right_ref, bf16[512,256]{1,0:T(8,128)(2,1)S(1)} %copy.32.mask_ref, bf16[128,640]{1,0:T(8,128)(2,1)S(1)} %pad.84.w1_ref, ...), custom_call_target="tpu_custom_call" | custom-call | flops 8000000000 | bytes 6000000 | tf_op jit(solution)/shard_map/pallas_call | solution.py:134
  42.8 1.1 copy.36
  43.9 9.4 %all-to-all-start = ((f32[16,4,32,128]{3,2,1,0:T(8,128)}), f32[16,4,32,128]{3,2,1,0:T(8,128)S(1)}, u32[]{:S(2)}, u32[]{:S(2)}) async-start(f32[16,4,32,128]{3,2,1,0:T(8,128)} %bitcast.41), calls=%async_computation | async-start | bytes 2097152 | tf_op jit(solution)/shard_map/all_to_all | solution.py:413
  53.3 23.7 %shard_map.56 = (f32[4,512,128]{2,1,0:T(8,128)S(1)}, f32[16,8,128]{2,1,0:T(8,128)S(1)}) custom-call(s32[3]{0:T(128)S(1)} %pad_add_fusion.where_ref.place_ref, f32[4,512,128]{2,1,0:T(8,128)S(1)} %shard_map.55.cost_ref, f32[16,8,128]{2,1,0:T(8,128)S(1)} %broadcast_in_dim.11.state_ref), custom_call_target="tpu_custom_call" | custom-call | flops 2000000000 | bytes 30000000 | tf_op jit(solution)/shard_map/pallas_call | solution.py:273
  77.0 0.0 copy-start
  77.0 1.0 copy-done
  78.0 0.1 all-to-all-done
  78.1 8.6 %shard_map.58 = f32[64,32,128]{2,1,0:T(8,128)} custom-call(f32[64,32,128]{2,1,0:T(8,128)S(1)} %bitcast.42), custom_call_target="tpu_custom_call" | custom-call | flops 200000000 | bytes 2000000 | tf_op jit(solution)/shard_map/pallas_call | solution.py:328
  86.7 6.8 %all-to-all-start.1 = ((f32[16,4,32,128]{3,2,1,0:T(8,128)}), f32[16,4,32,128]{3,2,1,0:T(8,128)}, u32[]{:S(2)}, u32[]{:S(2)}) async-start(f32[16,4,32,128]{3,2,1,0:T(8,128)} %bitcast.23), calls=%async_computation.1 | async-start | bytes 2097152 | tf_op jit(solution)/shard_map/all_to_all | solution.py:421
  93.6 0.1 collective-permute-start.5
  93.7 1.2 %collective-permute-done.5.state_ref = f32[16,8,128]{2,1,0:T(8,128)S(1)} collective-permute-done((f32[16,8,128]{2,1,0:T(8,128)S(1)}, f32[16,8,128]{2,1,0:T(8,128)S(1)}, u32[]{:S(2)}, u32[]{:S(2)}) %collective-permute-start.5) | collective-permute-done | bytes 65568 | tf_op jit(solution)/shard_map/ppermute | solution.py:420
  94.9 0.0 copy-start.1
  94.9 1.2 copy-done.1
  96.1 24.4 %shard_map.57 = (f32[4,512,128]{2,1,0:T(8,128)S(1)}, f32[16,8,128]{2,1,0:T(8,128)}) custom-call(s32[3]{0:T(128)S(1)} %pad_add_fusion.where_ref.place_ref, f32[4,512,128]{2,1,0:T(8,128)S(1)} %shard_map.55.cost_ref, f32[16,8,128]{2,1,0:T(8,128)S(1)} %collective-permute-done.5.state_ref, f32[4,512,128]{2,1,0:T(8,128)S(1)} %copy-done.1), custom_call_target="tpu_custom_call" | custom-call | flops 2000000000 | bytes 30000000 | tf_op jit(solution)/shard_map/pallas_call | solution.py:273
  120.5 0.0 all-to-all-done.1
  120.5 1.3 %copy.34 = f32[4,16,32,128]{3,2,1,0:T(8,128)S(1)} copy(f32[4,16,32,128]{3,2,0,1:T(8,128)} %bitcast.24) | data formatting | bytes 2097152 | tf_op jit(solution)/shard_map/transpose | solution.py:425
  121.8 1.1 bitcast_add_fusion
  (16 shorter events, 0.3 us)
Async XLA Ops:
  0.0 17.6 %copy-start.2 = (bf16[64,1,3,3]{0,3,2,1:T(4,128)(2,1)S(1)}, bf16[64,1,3,3]{0,3,2,1:T(4,128)(2,1)}, u32[]{:S(2)}) copy-start(bf16[64,1,3,3]{0,3,2,1:T(4,128)(2,1)} %param.8) | copy-start | bytes 3460
  0.0 17.6 %copy-start.3 = (s32[4,512]{1,0:T(4,128)S(1)}, s32[4,512]{1,0:T(4,128)}, u32[]{:S(2)}) copy-start(s32[4,512]{1,0:T(4,128)} %param.7) | copy-start | bytes 24580
  0.8 20.9 %collective-permute-start = (bf16[2,4,512]{2,1,0:T(4,128)(2,1)S(1)}, bf16[2,4,512]{2,1,0:T(4,128)(2,1)S(1)}, u32[]{:S(2)}, u32[]{:S(2)}) collective-permute-start(bf16[2,4,512]{2,1,0:T(4,128)(2,1)S(1)} %pad_maximum_fusion.2), channel_id=1, source_target_pairs={{0,2},{1,3},{2,4},{3,5},{4,6},{5,7},{6,8},{7,9},{8,10},{9,11},{10,... | collective-permute-start | bytes 24584 | tf_op jit(solution)/shard_map/ppermute | solution.py:365
  5.6 16.0 %collective-permute-start.1 = (bf16[2,4,512]{2,1,0:T(4,128)(2,1)S(1)}, bf16[2,4,512]{2,1,0:T(4,128)(2,1)S(1)}, u32[]{:S(2)}, u32[]{:S(2)}) collective-permute-start(bf16[2,4,512]{2,1,0:T(4,128)(2,1)S(1)} %pad_maximum_fusion.2), channel_id=1, source_target_pairs={{1,2},{0,3},{3,4},{2,5},{5,6},{4,7},{7,8},{6,9},{9,10},{8,11},{11,... | collective-permute-start | bytes 24584 | tf_op jit(solution)/shard_map/ppermute | solution.py:365
  8.2 13.5 %collective-permute-start.3 = (bf16[2,4,512]{2,1,0:T(4,128)(2,1)S(1)}, bf16[2,4,512]{2,1,0:T(4,128)(2,1)S(1)}, u32[]{:S(2)}, u32[]{:S(2)}) collective-permute-start(bf16[2,4,512]{2,1,0:T(4,128)(2,1)S(1)} %pad_maximum_fusion.2), channel_id=1, source_target_pairs={{2,0},{3,1},{4,2},{5,3},{6,4},{7,5},{8,6},{9,7},{10,8},{11,9},{12,... | collective-permute-start | bytes 24584 | tf_op jit(solution)/shard_map/ppermute | solution.py:365
  9.5 12.2 %collective-permute-start.4 = (bf16[2,4,512]{2,1,0:T(4,128)(2,1)S(1)}, bf16[2,4,512]{2,1,0:T(4,128)(2,1)S(1)}, u32[]{:S(2)}, u32[]{:S(2)}) collective-permute-start(bf16[2,4,512]{2,1,0:T(4,128)(2,1)S(1)} %pad_maximum_fusion.2), channel_id=1, source_target_pairs={{3,0},{2,1},{5,2},{4,3},{7,4},{6,5},{9,6},{8,7},{11,8},{10,9},{13,... | collective-permute-start | bytes 24584 | tf_op jit(solution)/shard_map/ppermute | solution.py:365
  10.8 10.8 %collective-permute-start.2 = (bf16[2,4,512]{2,1,0:T(4,128)(2,1)S(1)}, bf16[2,4,512]{2,1,0:T(4,128)(2,1)S(1)}, u32[]{:S(2)}, u32[]{:S(2)}) collective-permute-start(bf16[2,4,512]{2,1,0:T(4,128)(2,1)S(1)} %pad_maximum_fusion.2), channel_id=1, source_target_pairs={{1,0},{0,1},{3,2},{2,3},{5,4},{4,5},{7,6},{6,7},{9,8},{8,9},{11,10... | collective-permute-start | bytes 24584 | tf_op jit(solution)/shard_map/ppermute | solution.py:365
  43.9 34.2 %all-to-all-start = ((f32[16,4,32,128]{3,2,1,0:T(8,128)}), f32[16,4,32,128]{3,2,1,0:T(8,128)S(1)}, u32[]{:S(2)}, u32[]{:S(2)}) async-start(f32[16,4,32,128]{3,2,1,0:T(8,128)} %bitcast.41), calls=%async_computation | async-start | bytes 2097152 | tf_op jit(solution)/shard_map/all_to_all | solution.py:413
  77.0 1.0 copy-start
  86.7 33.8 %all-to-all-start.1 = ((f32[16,4,32,128]{3,2,1,0:T(8,128)}), f32[16,4,32,128]{3,2,1,0:T(8,128)}, u32[]{:S(2)}, u32[]{:S(2)}) async-start(f32[16,4,32,128]{3,2,1,0:T(8,128)} %bitcast.23), calls=%async_computation.1 | async-start | bytes 2097152 | tf_op jit(solution)/shard_map/all_to_all | solution.py:421
  93.6 1.3 %collective-permute-start.5 = (f32[16,8,128]{2,1,0:T(8,128)S(1)}, f32[16,8,128]{2,1,0:T(8,128)S(1)}, u32[]{:S(2)}, u32[]{:S(2)}) collective-permute-start(f32[16,8,128]{2,1,0:T(8,128)S(1)} %get-tuple-element.11), channel_id=1, source_target_pairs={{0,1},{1,0},{2,3},{3,2},{4,5},{5,4},{6,7},{7,6},{8,9},{9,8},{10,11... | collective-permute-start | bytes 196616 | tf_op jit(solution)/shard_map/ppermute | solution.py:420
  94.9 1.2 copy-start.1

commit v2 on v1

--- a/solution.py
+++ b/solution.py
@@ -16,74 +16,64 @@
 EDGE = 8
 LANES = 128
 BATCH = 4
-
-
-def chunking(need):
-    best = None
-    for size in (128, 144, 160, 176):
-        total = -(-need // size) * size
-        if best is None or total < best[1]:
-            best = (size, total)
-    return best
+PARTS = 1
+BLOCKS = 4
 
 
 def plan(width):
-    steps = [chunking(width)]
-    for _ in range(2):
-        steps.append(chunking(steps[-1][1] + 2 * EDGE))
-    need = steps[-1][1] + 2 * EDGE
-    steps.append((128, -(-need // 128) * 128))
-    return steps[::-1]
-
-
-def feature_stack(pix_ref, w1_ref, wt_ref, bufs, sizes, col_of, row_low, row_high, flipped, last_mask_ref):
-    def in_image(base, count, lanes, halo, lane0):
+    unit = 16 * PARTS
+    totals = [-(-width // unit) * unit]
+    for _ in range(3):
+        totals.append(-(-(totals[-1] + 2 * EDGE) // unit) * unit)
+    return totals[::-1]
+
+
+def feature_stacks(stacks, w1_ref, wt_ref, row_low, row_high):
+    def inside(test, base, count, lanes, halo, lane0):
         position = lax.broadcasted_iota(jnp.int32, (count, lanes), 0) + base
         row = (lax.broadcasted_iota(jnp.int32, (count, lanes), 1) + lane0) // CH - halo
-        low, high = col_of(position)
-        return low & high & (row >= row_low) & (row < row_high)
-
-    chunk, total = sizes[0]
-    lanes = bufs[0].shape[1]
+        return test(position) & (row >= row_low) & (row < row_high)
 
     def first(index, carry):
-        start = pl.multiple_of(index * chunk, chunk)
-        value = jnp.dot(pix_ref[pl.ds(start, chunk), :], w1_ref[...], preferred_element_type=jnp.float32)
-        inside = in_image(start - 3 * EDGE, chunk, lanes, 3, 0)
-        value = jnp.where(inside, jnp.maximum(value, 0.0), 0.0)
-        bufs[0][pl.ds(start, chunk), :] = value.astype(jnp.bfloat16)
+        for pix_ref, bufs, test, flipped in stacks:
+            chunk = bufs[0].shape[0] // PARTS
+            start = pl.multiple_of(index * chunk, 16)
+            value = jnp.dot(pix_ref[pl.ds(start, chunk), :], w1_ref[...], preferred_element_type=jnp.float32)
+            keep = inside(test, start - 3 * EDGE, chunk, bufs[0].shape[1], 3, 0)
+            bufs[0][pl.ds(start, chunk), :] = jnp.where(keep, jnp.maximum(value, 0.0), 0.0).astype(jnp.bfloat16)
         return carry
 
-    lax.fori_loop(0, total // chunk, first, 0)
+    lax.fori_loop(0, PARTS, first, 0)
 
     for layer in range(1, 4):
-        source, target = bufs[layer - 1], bufs[layer]
-        out_rows = target.shape[1] // CH
-        chunk, total = sizes[layer]
-        reach = chunk + 2 * EDGE
-        for group in range(0, out_rows, 4):
-            count = min(4, out_rows - group)
-            wide, deep = count * CH, (count + 2) * CH
-
-            def convolve(index, carry, layer=layer, group=group, wide=wide, deep=deep, chunk=chunk, reach=reach, source=source, target=target):
+
+        def convolve(index, carry, layer=layer):
+            halo = 3 - layer
+            for pix_ref, bufs, test, flipped in stacks:
+                source, target = bufs[layer - 1], bufs[layer]
+                out_rows = target.shape[1] // CH
+                chunk = target.shape[0] // PARTS
+                reach = chunk + 2 * EDGE
                 start = pl.multiple_of(index * chunk, 16)
-                block = source[pl.ds(start, reach), group * CH : group * CH + deep]
-                parts = [
-                    jnp.dot(block, wt_ref[layer - 1, dx, :deep, :wide], preferred_element_type=jnp.float32)
-                    for dx in range(3)
-                ]
-                before, after = (parts[2], parts[0]) if flipped else (parts[0], parts[2])
-                value = pltpu.roll(before, 1, 0) + parts[1] + pltpu.roll(after, reach - 1, 0)
-                value = value[EDGE : EDGE + chunk]
-                halo = 3 - layer
-                if layer < 3:
-                    value = jnp.maximum(value, 0.0)
-                inside = in_image(start - halo * EDGE, chunk, wide, halo, group * CH)
-                value = jnp.where(inside, value, 0.0).astype(jnp.bfloat16)
-                target[pl.ds(start, chunk), group * CH : group * CH + wide] = value
-                return carry
-
-            lax.fori_loop(0, total // chunk, convolve, 0)
+                for group in range(0, out_rows, 4):
+                    count = min(4, out_rows - group)
+                    wide, deep = count * CH, (count + 2) * CH
+                    block = source[pl.ds(start, reach), group * CH : group * CH + deep]
+                    parts = [
+                        jnp.dot(block, wt_ref[layer - 1, dx, :deep, :wide], preferred_element_type=jnp.float32)
+                        for dx in range(3)
+                    ]
+                    before, after = (parts[2], parts[0]) if flipped else (parts[0], parts[2])
+                    value = pltpu.roll(before, 1, 0) + parts[1] + pltpu.roll(after, reach - 1, 0)
+                    value = value[EDGE : EDGE + chunk]
+                    if layer < 3:
+                        value = jnp.maximum(value, 0.0)
+                    keep = inside(test, start - halo * EDGE, chunk, wide, halo, group * CH)
+                    value = jnp.where(keep, value, 0.0).astype(jnp.bfloat16)
+                    target[pl.ds(start, chunk), group * CH : group * CH + wide] = value
+            return carry
+
+        lax.fori_loop(0, PARTS, convolve, 0)
 
 
 def cost_kernel(dims, where_ref, left_ref, right_ref, mask_ref, w1_ref, wt_ref, cost_ref, *bufs):
@@ -94,14 +84,16 @@
 
     def left_col(position):
         col = position + first_col
-        return col >= 0, col < total_cols
+        return (col >= 0) & (col < total_cols)
 
     def right_col(position):
         col = first_col + cols - 1 - position
-        return col >= 0, col < total_cols
-
-    feature_stack(left_ref, w1_ref, wt_ref, left_bufs, plan(cols), left_col, row_low, row_high, False, mask_ref)
-    feature_stack(right_ref, w1_ref, wt_ref, right_bufs, plan(cols + DISP), right_col, row_low, row_high, True, None)
+        return (col >= 0) & (col < total_cols)
+
+    feature_stacks(
+        [(left_ref, left_bufs, left_col, False), (right_ref, right_bufs, right_col, True)],
+        w1_ref, wt_ref, row_low, row_high,
+    )
     left, right = left_bufs[3], right_bufs[3]
     for row in range(rows):
         pair = row // 2 * LANES
@@ -119,7 +111,7 @@
             cost_ref[row, pl.ds(start, LANES), :] = skewed[:, :LANES]
             return carry
 
-        lax.fori_loop(0, cols // LANES, block, 0)
+        lax.fori_loop(0, cols // LANES, block, 0, unroll=BLOCKS)
 
 
 def cost_volume(left_stack, right_stack, mask, w1, wt, place, rows, cols, total_rows, total_cols):
@@ -128,7 +120,7 @@
         sizes = plan(width)
         for layer in range(4):
             out_rows = rows + 2 * (3 - layer)
-            length = sizes[layer][1]
+            length = sizes[layer]
             bufs.append(pltpu.VMEM((length, out_rows * CH), jnp.bfloat16))
     vmem = pl.BlockSpec(memory_space=pltpu.VMEM)
     return pl.pallas_call(
@@ -146,7 +138,7 @@
     rows, cols, flip, batch = dims
     if has_sum:
         lead_ref, rest = rest[0], rest[1:]
-    out_ref, end_ref, tile_ref, turn_ref, pick_ref, split_ref, even_ref, odd_ref, path_ref, low_ref = rest
+    out_ref, end_ref, tile_ref, turn_ref, pick_ref, split_a, split_b, even_ref, odd_ref, path_ref, low_ref = rest
     width = LANES // rows
     count = cols // width
     forward = place_ref[2] == (1 if flip else 0)
@@ -176,90 +168,92 @@
         chunk = jnp.where(forward, index, count - 1 - index)
         return pl.multiple_of(chunk * width, width)
 
-    def split(base, slot):
-        start = chunk_start(base + slot)
-        for row in range(rows):
-            tile_ref[slot, row * width : (row + 1) * width, :] = cost_ref[row, pl.ds(start, width), :]
-        tile_ref[slot] = tile_ref[slot].T
+    def split(index, target):
+        start = chunk_start(jnp.minimum(index, count - 1))
+        tile = jnp.concatenate([cost_ref[row, pl.ds(start, width), :] for row in range(rows)], axis=0)
+        tile_ref[...] = tile.T
         for v in range(0, 16, 2):
             plane = jnp.concatenate(
-                [tile_ref[slot, pl.ds(v, 8, stride=16), :], tile_ref[slot, pl.ds(v + 1, 8, stride=16), :]], axis=0
+                [tile_ref[pl.ds(v, 8, stride=16), :], tile_ref[pl.ds(v + 1, 8, stride=16), :]], axis=0
             )
             high = plane.astype(jnp.bfloat16)
-            split_ref[slot * LANES + v * 8 : slot * LANES + v * 8 + 16, :LANES] = high
-            split_ref[slot * LANES + v * 8 : slot * LANES + v * 8 + 16, LANES:] = (plane - high.astype(jnp.float32)).astype(jnp.bfloat16)
-
-    def spread(target, pair):
-        weight = pick_ref[pair]
-        both = jnp.dot(split_ref[...], weight, preferred_element_type=jnp.float32)
+            low = (plane - high.astype(jnp.float32)).astype(jnp.bfloat16)
+            target[v * 8 : v * 8 + 16, :LANES] = high
+            target[v * 8 : v * 8 + 16, LANES:] = low
+
+    def spread(source, target, pair):
+        both = jnp.dot(source[...], pick_ref[pair], preferred_element_type=jnp.float32)
         for slot in range(batch):
             target[slot, 2 * pair] = both[slot * LANES : slot * LANES + LANES, :LANES]
             target[slot, 2 * pair + 1] = both[slot * LANES : slot * LANES + LANES, LANES:]
 
-    def one_batch(number, state, current, coming):
+    def emit(index):
+        start = chunk_start(jnp.maximum(index, 0))
+        low = low_ref[...]
+        for v in range(16):
+            turn_ref[pl.ds(v, 8, stride=16), :] = path_ref[v] - low
+        done = turn_ref[...].T
+        for row in range(rows):
+            piece = done[row * width : (row + 1) * width]
+            if has_sum:
+                piece = piece + lead_ref[row, pl.ds(start, width), :]
+            out_ref[row, pl.ds(start, width), :] = piece
+
+    def advance(state, low, slot, step, current):
+        col = jnp.where(forward, step, width - 1 - step)
+        mask = lane_col == col
+        bound = low + P_LARGE
+        above = jnp.where(sublane == 7, BIG, pltpu.roll(state[0], 7, 0))
+        below = jnp.where(sublane == 0, BIG, pltpu.roll(state[15], 1, 0))
+        padded = [below] + list(state) + [above]
+        fresh = []
+        for v in range(16):
+            near = jnp.minimum(padded[v], padded[v + 2]) + P_SMALL
+            best = jnp.minimum(jnp.minimum(state[v], near), bound)
+            value = current[slot, col, v * 8 : v * 8 + 8, :] + best
+            pltpu.store(path_ref.at[v], value, mask=mask)
+            fresh.append(value)
+        pltpu.store(low_ref, low, mask=mask)
+        return fresh
+
+    def one_batch(number, state, current, coming, ready, filling):
         base = number * batch
-        later = jnp.minimum(base + batch, count - batch)
-        for slot in range(batch):
-            split(later, slot)
+        pairs = width // 2 // batch
 
         def one_chunk(slot, state):
-            def advance(step, state):
-                col = jnp.where(forward, step, width - 1 - step)
-                mask = lane_col == col
-                low = lowest(state)
-                bound = low + P_LARGE
-                above = jnp.where(sublane == 7, BIG, pltpu.roll(state[0], 7, 0))
-                below = jnp.where(sublane == 0, BIG, pltpu.roll(state[15], 1, 0))
-                padded = [below] + list(state) + [above]
-                fresh = []
-                for v in range(16):
-                    near = jnp.minimum(padded[v], padded[v + 2]) + P_SMALL
-                    best = jnp.minimum(jnp.minimum(state[v], near), bound)
-                    value = current[slot, col, v * 8 : v * 8 + 8, :] + best
-                    pltpu.store(path_ref.at[v], value, mask=mask)
-                    fresh.append(value)
-                pltpu.store(low_ref, low, mask=mask)
-                return tuple(fresh)
-
-            per_pair = 2 * batch
-
-            def group(index, state):
-                spread(coming, slot * (width // per_pair) + index)
-                for k in range(per_pair):
-                    state = advance(index * per_pair + k, state)
-                return state
-
-            state = lax.fori_loop(0, width // per_pair, group, state)
-            start = chunk_start(base + slot)
-            low = low_ref[...]
-            for v in range(16):
-                turn_ref[pl.ds(v, 8, stride=16), :] = path_ref[v] - low
-            done = turn_ref[...].T
-            for row in range(rows):
-                piece = done[row * width : (row + 1) * width]
-                if has_sum:
-                    piece = piece + lead_ref[row, pl.ds(start, width), :]
-                out_ref[row, pl.ds(start, width), :] = piece
+            emit(base + slot - 1)
+            split(base + 2 * batch + slot, filling.at[pl.ds(pl.multiple_of(slot * LANES, LANES), LANES)])
             low = lowest(state)
-            return tuple(value - low for value in state)
+            state = [value - low for value in state]
+            low = jnp.zeros_like(low)
+            for step in range(width):
+                if step % (2 * batch) == 0:
+                    spread(ready, coming, slot * pairs + step // (2 * batch))
+                if step:
+                    low = lowest(state)
+                state = advance(state, low, slot, step, current)
+            return tuple(state)
 
         return lax.fori_loop(0, batch, one_chunk, state)
 
     for slot in range(batch):
-        split(0, slot)
-
-    def first(pair, carry):
-        spread(even_ref, pair)
+        split(slot, split_a.at[pl.ds(slot * LANES, LANES)])
+        split(batch + slot, split_b.at[pl.ds(slot * LANES, LANES)])
+
+    def first(group, carry):
+        for k in range(4):
+            spread(split_a, even_ref, group * 4 + k)
         return carry
 
-    lax.fori_loop(0, width // 2, first, 0)
+    lax.fori_loop(0, width // 8, first, 0)
 
     def two_batches(index, state):
-        state = one_batch(2 * index, state, even_ref, odd_ref)
-        return one_batch(2 * index + 1, state, odd_ref, even_ref)
+        state = one_batch(2 * index, state, even_ref, odd_ref, split_b, split_a)
+        return one_batch(2 * index + 1, state, odd_ref, even_ref, split_a, split_b)
 
     state = tuple(state_ref[v] for v in range(16))
     state = lax.fori_loop(0, count // batch // 2, two_batches, state)
+    emit(count - 1)
     for v in range(16):
         end_ref[v] = state[v]
 
@@ -279,9 +273,10 @@
         in_specs=[pl.BlockSpec(memory_space=pltpu.SMEM)] + [vmem] * (len(args) - 1),
         out_specs=(vmem, vmem),
         scratch_shapes=[
-            pltpu.VMEM((batch, LANES, LANES), jnp.float32),
+            pltpu.VMEM((LANES, LANES), jnp.float32),
             pltpu.VMEM((LANES, LANES), jnp.float32),
             pltpu.VMEM((width // 2, 2 * LANES, 2 * LANES), jnp.bfloat16),
+            pltpu.VMEM((batch * LANES, 2 * LANES), jnp.bfloat16),
             pltpu.VMEM((batch * LANES, 2 * LANES), jnp.bfloat16),
             pltpu.VMEM((batch, width, LANES, LANES), jnp.float32),
             pltpu.VMEM((batch, width, LANES, LANES), jnp.float32),
@@ -395,7 +390,7 @@
 
     pair = jnp.stack([normalize(left_pixels), normalize(right_pixels)])
     band = neighbours(pair, "rows", "strips")[:, rows - 4 : 2 * rows + 4]
-    left_length, right_length = plan(cols)[0][1], plan(cols + DISP)[0][1]
+    left_length, right_length = plan(cols)[0], plan(cols + DISP)[0]
     margin = right_length + 8
     band = jnp.pad(band, ((0, 0), (0, 0), (margin, margin)))
     first_col = strip * cols

time: 124 us -> 109 us (0.88)
  Pallas kernels: 75.4 us -> 47 us
  waiting for transfers between devices: 1.37 us -> 14.8 us
    pallas_call x2, Pallas kernels: 48.1 us -> 31.5 us  [row_scan(): pl.pallas_call(functools.partial(row_scan_kernel, (rows, cols, flip, batc...]
    pallas_call x1, Pallas kernels: 18.7 us -> 6.84 us  [cost_volume(): pl.pallas_call(functools.partial(cost_kernel, (rows, cols, total_rows, to...]
    all_to_all x1, waiting for transfers between devices: 0.12 us -> 8.38 us  [per_device(): lax.all_to_all(grouped, 'rows', split_axis=0, concat_axis=0, tiled=True)]
    all_to_all x1, waiting for transfers between devices: 0.01 us -> 5.14 us  [per_device(): lax.all_to_all(column_sum.reshape(groups, rows, per_group, DISP), 'rows',...]
    unnamed x8 -> x14, local copies, waits for them, and re-layouts: 2.2 us -> 3.91 us
    rev x3 -> x0, local copies, waits for them, and re-layouts: 1.47 us -> none  [stacked(): parts.append(part[:, ::-1] if flipped else part)]
  transfers between devices with their start and end apart: 8 -> 8, of which waited for: 2 -> 3; matrix products, arithmetic and copies ran while one was open for 8% -> 9% of each run, Pallas kernels for 39% -> 29%
where the time goes in v2:
time: 109 us; the launch traced here: 108 us
  Pallas kernels  47 us (43%)
  starting transfers between devices  27.4 us (25%)
  waiting for transfers between devices  14.8 us (14%)
  local copies, waits for them, and re-layouts  11.9 us (11%)
  other arithmetic  6.78 us (6%)
    pallas_call x2, Pallas kernels, row_scan(): pl.pallas_call(functools.partial(row_scan_kernel, (rows, cols, flip, batc...  31.5 us
    ppermute x5, starting transfers between devices, moved(): return lax.ppermute(pair, axes, route)  11 us
    all_to_all x1, starting transfers between devices, per_device(): lax.all_to_all(grouped, 'rows', split_axis=0, concat_axis=0, tiled=True)  9.41 us
    pallas_call x1, Pallas kernels, column_scan(): pl.pallas_call(column_kernel, out_shape=jax.ShapeDtypeStruct(columns.shap...  8.64 us
    all_to_all x1, waiting for transfers between devices, per_device(): lax.all_to_all(grouped, 'rows', split_axis=0, concat_axis=0, tiled=True)  8.38 us
    all_to_all x1, starting transfers between devices, per_device(): lax.all_to_all(column_sum.reshape(groups, rows, per_group, DISP), 'rows',...  6.86 us
    pallas_call x1, Pallas kernels, cost_volume(): pl.pallas_call(functools.partial(cost_kernel, (rows, cols, total_rows, to...  6.84 us
    all_to_all x1, waiting for transfers between devices, per_device(): lax.all_to_all(column_sum.reshape(groups, rows, per_group, DISP), 'rows',...  5.14 us
  transfers between devices with their start and end apart: 8, of which 3 were waited for; matrix products, arithmetic and copies ran while one was open for 9% of the time, Pallas kernels for 29%

profile of v2, /device:TPU:0, one launch (start us, length us, event | category | flops | bytes accessed | tf_op | source)
XLA Modules:
  0.0 108.1 jit_solution(16651493133627696805)
XLA Ops:
  0.0 0.0 copy-start.2
  0.0 0.0 copy-start.3
  0.0 0.7 fusion.15
  0.8 4.8 %collective-permute-start = (bf16[2,4,512]{2,1,0:T(4,128)(2,1)S(1)}, bf16[2,4,512]{2,1,0:T(4,128)(2,1)S(1)}, u32[]{:S(2)}, u32[]{:S(2)}) collective-permute-start(bf16[2,4,512]{2,1,0:T(4,128)(2,1)S(1)} %pad_maximum_fusion.2), channel_id=1, source_target_pairs={{0,2},{1,3},{2,4},{3,5},{4,6},{5,7},{6,8},{7,9},{8,10},{9,11},{10,... | collective-permute-start | bytes 24584 | tf_op jit(solution)/shard_map/ppermute | solution.py:360
  5.6 2.6 %collective-permute-start.1 = (bf16[2,4,512]{2,1,0:T(4,128)(2,1)S(1)}, bf16[2,4,512]{2,1,0:T(4,128)(2,1)S(1)}, u32[]{:S(2)}, u32[]{:S(2)}) collective-permute-start(bf16[2,4,512]{2,1,0:T(4,128)(2,1)S(1)} %pad_maximum_fusion.2), channel_id=1, source_target_pairs={{1,2},{0,3},{3,4},{2,5},{5,6},{4,7},{7,8},{6,9},{9,10},{8,11},{11,... | collective-permute-start | bytes 24584 | tf_op jit(solution)/shard_map/ppermute | solution.py:360
  8.2 1.3 %collective-permute-start.3 = (bf16[2,4,512]{2,1,0:T(4,128)(2,1)S(1)}, bf16[2,4,512]{2,1,0:T(4,128)(2,1)S(1)}, u32[]{:S(2)}, u32[]{:S(2)}) collective-permute-start(bf16[2,4,512]{2,1,0:T(4,128)(2,1)S(1)} %pad_maximum_fusion.2), channel_id=1, source_target_pairs={{2,0},{3,1},{4,2},{5,3},{6,4},{7,5},{8,6},{9,7},{10,8},{11,9},{12,... | collective-permute-start | bytes 24584 | tf_op jit(solution)/shard_map/ppermute | solution.py:360
  9.5 1.3 %collective-permute-start.4 = (bf16[2,4,512]{2,1,0:T(4,128)(2,1)S(1)}, bf16[2,4,512]{2,1,0:T(4,128)(2,1)S(1)}, u32[]{:S(2)}, u32[]{:S(2)}) collective-permute-start(bf16[2,4,512]{2,1,0:T(4,128)(2,1)S(1)} %pad_maximum_fusion.2), channel_id=1, source_target_pairs={{3,0},{2,1},{5,2},{4,3},{7,4},{6,5},{9,6},{8,7},{11,8},{10,9},{13,... | collective-permute-start | bytes 24584 | tf_op jit(solution)/shard_map/ppermute | solution.py:360
  10.8 1.0 collective-permute-start.2
  11.8 1.0 fusion.19
  12.8 4.7 %fusion.7 = bf16[3,3,6,64,256]{3,4,1,2,0:T(8,128)(2,1)} fusion(bf16[3,3,3,64,64]{3,4,1,2,0:T(8,128)(2,1)} %bitcast.49), kind=kLoop, calls=%fused_computation.13 | loop fusion | flops 17694720 | bytes 1990656 | tf_op jit(solution)/shard_map/concatenate | solution.py:344
  17.5 0.0 copy-done.3
  17.5 0.1 pad_add_fusion.where_ref.place_ref
  17.6 0.0 copy-done.2
  17.6 0.2 concatenate.42
  17.9 3.5 %copy.31 = bf16[3,3,6,64,256]{4,3,2,1,0:T(8,128)(2,1)S(1)} copy(bf16[3,3,6,64,256]{3,4,1,2,0:T(8,128)(2,1)} %fusion.7) | data formatting | bytes 3538944 | tf_op jit(solution)/shard_map/concatenate | solution.py:344
  21.4 0.1 copy.32.mask_ref
  21.6 0.0 collective-permute-done.2
  21.6 0.0 collective-permute-done
  21.6 0.0 collective-permute-done.1
  21.7 0.0 collective-permute-done.3
  21.7 0.0 collective-permute-done.4
  21.7 0.1 fusion.14
  21.8 0.1 dynamic-slice_bitcast_fusion.2
  21.9 0.5 reverse
  22.5 0.1 slice.10
  22.5 0.5 reverse.1
  23.0 0.1 slice.11
  23.1 0.5 reverse.2
  23.6 0.1 slice.12
  23.7 0.2 copy.29
  23.9 0.1 dynamic-slice_bitcast_fusion.5
  24.1 0.1 copy.28
  24.2 6.8 %shard_map.55.cost_ref = f32[4,512,128]{2,1,0:T(8,128)S(1)} custom-call(s32[3]{0:T(128)S(1)} %pad_add_fusion.where_ref.place_ref, bf16[560,128]{1,0:T(8,128)(2,1)S(1)} %pad_bitcast_fusion.1.left_ref, bf16[688,128]{1,0:T(8,128)(2,1)S(1)} %pad_bitcast_fusion.right_ref, bf16[512,256]{1,0:T(8,128)(2,1)S(1)} %copy.32.mask_ref, bf16[128,640]{1,0:T(8,128)(2,1)S(1)} %pad.85.w1_ref, ...), custom_call_target="tpu_custom_call" | custom-call | flops 8000000000 | bytes 6000000 | tf_op jit(solution)/shard_map/pallas_call | solution.py:126
  31.1 1.1 %copy.36 = f32[4,16,32,128]{3,2,0,1:T(8,128)} copy(f32[4,16,32,128]{3,2,1,0:T(8,128)S(1)} %bitcast.47) | data formatting | bytes 2097152 | tf_op jit(solution)/shard_map/reshape | solution.py:407
  32.2 9.4 %all-to-all-start = ((f32[16,4,32,128]{3,2,1,0:T(8,128)}), f32[16,4,32,128]{3,2,1,0:T(8,128)S(1)}, u32[]{:S(2)}, u32[]{:S(2)}) async-start(f32[16,4,32,128]{3,2,1,0:T(8,128)} %bitcast.44), calls=%async_computation | async-start | bytes 2097152 | tf_op jit(solution)/shard_map/all_to_all | solution.py:408
  41.6 15.4 %shard_map.56 = (f32[4,512,128]{2,1,0:T(8,128)S(1)}, f32[16,8,128]{2,1,0:T(8,128)S(1)}) custom-call(s32[3]{0:T(128)S(1)} %pad_add_fusion.where_ref.place_ref, f32[4,512,128]{2,1,0:T(8,128)S(1)} %shard_map.55.cost_ref, f32[16,8,128]{2,1,0:T(8,128)S(1)} %broadcast_in_dim.11.state_ref), custom_call_target="tpu_custom_call" | custom-call | flops 2000000000 | bytes 30000000 | tf_op jit(solution)/shard_map/pallas_call | solution.py:267
  57.1 0.0 copy-start
  57.1 1.0 copy-done
  58.0 8.4 %all-to-all-done = f32[16,4,32,128]{3,2,1,0:T(8,128)S(1)} async-done(((f32[16,4,32,128]{3,2,1,0:T(8,128)}), f32[16,4,32,128]{3,2,1,0:T(8,128)S(1)}, u32[]{:S(2)}, u32[]{:S(2)}) %all-to-all-start) | async-done | bytes 1048608 | tf_op jit(solution)/shard_map/all_to_all | solution.py:408
  66.4 8.6 %shard_map.58 = f32[64,32,128]{2,1,0:T(8,128)} custom-call(f32[64,32,128]{2,1,0:T(8,128)S(1)} %bitcast.45), custom_call_target="tpu_custom_call" | custom-call | flops 200000000 | bytes 2000000 | tf_op jit(solution)/shard_map/pallas_call | solution.py:323
  75.1 6.9 %all-to-all-start.1 = ((f32[16,4,32,128]{3,2,1,0:T(8,128)}), f32[16,4,32,128]{3,2,1,0:T(8,128)}, u32[]{:S(2)}, u32[]{:S(2)}) async-start(f32[16,4,32,128]{3,2,1,0:T(8,128)} %bitcast.23), calls=%async_computation.1 | async-start | bytes 2097152 | tf_op jit(solution)/shard_map/all_to_all | solution.py:416
  81.9 0.1 collective-permute-start.5
  82.0 1.2 %collective-permute-done.5.state_ref = f32[16,8,128]{2,1,0:T(8,128)S(1)} collective-permute-done((f32[16,8,128]{2,1,0:T(8,128)S(1)}, f32[16,8,128]{2,1,0:T(8,128)S(1)}, u32[]{:S(2)}, u32[]{:S(2)}) %collective-permute-start.5) | collective-permute-done | bytes 65568 | tf_op jit(solution)/shard_map/ppermute | solution.py:415
  83.3 0.0 copy-start.1
  83.3 1.2 %copy-done.1 = f32[4,512,128]{2,1,0:T(8,128)S(1)} copy-done((f32[4,512,128]{2,1,0:T(8,128)S(1)}, f32[4,512,128]{2,1,0:T(8,128)}, u32[]{:S(2)}) %copy-start.1) | copy-done | bytes 1048600
  84.5 16.1 %shard_map.57 = (f32[4,512,128]{2,1,0:T(8,128)S(1)}, f32[16,8,128]{2,1,0:T(8,128)}) custom-call(s32[3]{0:T(128)S(1)} %pad_add_fusion.where_ref.place_ref, f32[4,512,128]{2,1,0:T(8,128)S(1)} %shard_map.55.cost_ref, f32[16,8,128]{2,1,0:T(8,128)S(1)} %collective-permute-done.5.state_ref, f32[4,512,128]{2,1,0:T(8,128)S(1)} %copy-done.1), custom_call_target="tpu_custom_call" | custom-call | flops 2000000000 | bytes 30000000 | tf_op jit(solution)/shard_map/pallas_call | solution.py:267
  100.6 5.1 %all-to-all-done.1 = f32[16,4,32,128]{3,2,1,0:T(8,128)} async-done(((f32[16,4,32,128]{3,2,1,0:T(8,128)}), f32[16,4,32,128]{3,2,1,0:T(8,128)}, u32[]{:S(2)}, u32[]{:S(2)}) %all-to-all-start.1) | async-done | bytes 1048608 | tf_op jit(solution)/shard_map/all_to_all | solution.py:416
  105.7 1.3 %copy.34 = f32[4,16,32,128]{3,2,1,0:T(8,128)S(1)} copy(f32[4,16,32,128]{3,2,0,1:T(8,128)} %bitcast.24) | data formatting | bytes 2097152 | tf_op jit(solution)/shard_map/transpose | solution.py:420
  107.0 1.1 bitcast_add_fusion
  (16 shorter events, 0.3 us)
Async XLA Ops:
  0.0 17.6 %copy-start.2 = (bf16[64,1,3,3]{0,3,2,1:T(4,128)(2,1)S(1)}, bf16[64,1,3,3]{0,3,2,1:T(4,128)(2,1)}, u32[]{:S(2)}) copy-start(bf16[64,1,3,3]{0,3,2,1:T(4,128)(2,1)} %param.8) | copy-start | bytes 3460
  0.0 17.5 %copy-start.3 = (s32[4,512]{1,0:T(4,128)S(1)}, s32[4,512]{1,0:T(4,128)}, u32[]{:S(2)}) copy-start(s32[4,512]{1,0:T(4,128)} %param.7) | copy-start | bytes 24580
  0.8 20.9 %collective-permute-start = (bf16[2,4,512]{2,1,0:T(4,128)(2,1)S(1)}, bf16[2,4,512]{2,1,0:T(4,128)(2,1)S(1)}, u32[]{:S(2)}, u32[]{:S(2)}) collective-permute-start(bf16[2,4,512]{2,1,0:T(4,128)(2,1)S(1)} %pad_maximum_fusion.2), channel_id=1, source_target_pairs={{0,2},{1,3},{2,4},{3,5},{4,6},{5,7},{6,8},{7,9},{8,10},{9,11},{10,... | collective-permute-start | bytes 24584 | tf_op jit(solution)/shard_map/ppermute | solution.py:360
  5.6 16.0 %collective-permute-start.1 = (bf16[2,4,512]{2,1,0:T(4,128)(2,1)S(1)}, bf16[2,4,512]{2,1,0:T(4,128)(2,1)S(1)}, u32[]{:S(2)}, u32[]{:S(2)}) collective-permute-start(bf16[2,4,512]{2,1,0:T(4,128)(2,1)S(1)} %pad_maximum_fusion.2), channel_id=1, source_target_pairs={{1,2},{0,3},{3,4},{2,5},{5,6},{4,7},{7,8},{6,9},{9,10},{8,11},{11,... | collective-permute-start | bytes 24584 | tf_op jit(solution)/shard_map/ppermute | solution.py:360
  8.2 13.5 %collective-permute-start.3 = (bf16[2,4,512]{2,1,0:T(4,128)(2,1)S(1)}, bf16[2,4,512]{2,1,0:T(4,128)(2,1)S(1)}, u32[]{:S(2)}, u32[]{:S(2)}) collective-permute-start(bf16[2,4,512]{2,1,0:T(4,128)(2,1)S(1)} %pad_maximum_fusion.2), channel_id=1, source_target_pairs={{2,0},{3,1},{4,2},{5,3},{6,4},{7,5},{8,6},{9,7},{10,8},{11,9},{12,... | collective-permute-start | bytes 24584 | tf_op jit(solution)/shard_map/ppermute | solution.py:360
  9.5 12.2 %collective-permute-start.4 = (bf16[2,4,512]{2,1,0:T(4,128)(2,1)S(1)}, bf16[2,4,512]{2,1,0:T(4,128)(2,1)S(1)}, u32[]{:S(2)}, u32[]{:S(2)}) collective-permute-start(bf16[2,4,512]{2,1,0:T(4,128)(2,1)S(1)} %pad_maximum_fusion.2), channel_id=1, source_target_pairs={{3,0},{2,1},{5,2},{4,3},{7,4},{6,5},{9,6},{8,7},{11,8},{10,9},{13,... | collective-permute-start | bytes 24584 | tf_op jit(solution)/shard_map/ppermute | solution.py:360
  10.8 10.8 %collective-permute-start.2 = (bf16[2,4,512]{2,1,0:T(4,128)(2,1)S(1)}, bf16[2,4,512]{2,1,0:T(4,128)(2,1)S(1)}, u32[]{:S(2)}, u32[]{:S(2)}) collective-permute-start(bf16[2,4,512]{2,1,0:T(4,128)(2,1)S(1)} %pad_maximum_fusion.2), channel_id=1, source_target_pairs={{1,0},{0,1},{3,2},{2,3},{5,4},{4,5},{7,6},{6,7},{9,8},{8,9},{11,10... | collective-permute-start | bytes 24584 | tf_op jit(solution)/shard_map/ppermute | solution.py:360
  32.2 34.2 %all-to-all-start = ((f32[16,4,32,128]{3,2,1,0:T(8,128)}), f32[16,4,32,128]{3,2,1,0:T(8,128)S(1)}, u32[]{:S(2)}, u32[]{:S(2)}) async-start(f32[16,4,32,128]{3,2,1,0:T(8,128)} %bitcast.44), calls=%async_computation | async-start | bytes 2097152 | tf_op jit(solution)/shard_map/all_to_all | solution.py:408
  57.1 1.0 copy-start
  75.1 30.6 %all-to-all-start.1 = ((f32[16,4,32,128]{3,2,1,0:T(8,128)}), f32[16,4,32,128]{3,2,1,0:T(8,128)}, u32[]{:S(2)}, u32[]{:S(2)}) async-start(f32[16,4,32,128]{3,2,1,0:T(8,128)} %bitcast.23), calls=%async_computation.1 | async-start | bytes 2097152 | tf_op jit(solution)/shard_map/all_to_all | solution.py:416
  81.9 1.3 %collective-permute-start.5 = (f32[16,8,128]{2,1,0:T(8,128)S(1)}, f32[16,8,128]{2,1,0:T(8,128)S(1)}, u32[]{:S(2)}, u32[]{:S(2)}) collective-permute-start(f32[16,8,128]{2,1,0:T(8,128)S(1)} %get-tuple-element.11), channel_id=1, source_target_pairs={{0,1},{1,0},{2,3},{3,2},{4,5},{5,4},{6,7},{7,6},{8,9},{9,8},{10,11... | collective-permute-start | bytes 196616 | tf_op jit(solution)/shard_map/ppermute | solution.py:415
  83.3 1.2 %copy-start.1 = (f32[4,512,128]{2,1,0:T(8,128)S(1)}, f32[4,512,128]{2,1,0:T(8,128)}, u32[]{:S(2)}) copy-start(f32[4,512,128]{2,1,0:T(8,128)} %copy-done) | copy-start | bytes 3145732

commit v3 on v2

--- a/solution.py
+++ b/solution.py
@@ -15,7 +15,7 @@
 CH = 64
 EDGE = 8
 LANES = 128
-BATCH = 4
+BATCH = 2
 PARTS = 1
 BLOCKS = 4
 
@@ -76,8 +76,13 @@
         lax.fori_loop(0, PARTS, convolve, 0)
 
 
-def cost_kernel(dims, where_ref, left_ref, right_ref, mask_ref, w1_ref, wt_ref, cost_ref, *bufs):
-    rows, cols, total_rows, total_cols = dims
+def packs(per_group):
+    return per_group % 16 == 0 and LANES % per_group == 0
+
+
+def cost_kernel(dims, where_ref, left_ref, right_ref, mask_ref, w1_ref, wt_ref, cost_ref, *rest):
+    rows, cols, total_rows, total_cols, per_group = dims
+    payload_ref, bufs = (rest[0], rest[1:]) if len(rest) % 2 else (None, rest)
     first_row, first_col = where_ref[0], where_ref[1]
     row_low, row_high = -first_row, total_rows - first_row
     left_bufs, right_bufs = bufs[:4], bufs[4:]
@@ -108,13 +113,19 @@
             b = right[pl.ds(window, 2 * LANES), pair : pair + LANES]
             product = lax.dot_general(a, b, (((1,), (1,)), ((), ())), preferred_element_type=jnp.float32)
             skewed = pltpu.roll(product, LANES + 1, 1, stride=1, stride_axis=0)
-            cost_ref[row, pl.ds(start, LANES), :] = skewed[:, :LANES]
+            skewed = skewed[:, :LANES]
+            cost_ref[row, pl.ds(start, LANES), :] = skewed
+            if payload_ref is not None:
+                for k in range(LANES // per_group):
+                    piece = skewed[k * per_group : (k + 1) * per_group].astype(jnp.bfloat16)
+                    group = index * (LANES // per_group) + k
+                    payload_ref[group, row * per_group : (row + 1) * per_group, :] = piece
             return carry
 
         lax.fori_loop(0, cols // LANES, block, 0, unroll=BLOCKS)
 
 
-def cost_volume(left_stack, right_stack, mask, w1, wt, place, rows, cols, total_rows, total_cols):
+def cost_volume(left_stack, right_stack, mask, w1, wt, place, rows, cols, total_rows, total_cols, per_group):
     bufs = []
     for width in (cols, cols + DISP):
         sizes = plan(width)
@@ -123,11 +134,14 @@
             length = sizes[layer]
             bufs.append(pltpu.VMEM((length, out_rows * CH), jnp.bfloat16))
     vmem = pl.BlockSpec(memory_space=pltpu.VMEM)
+    shapes = [jax.ShapeDtypeStruct((rows, cols, DISP), jnp.float32)]
+    if packs(per_group):
+        shapes.append(jax.ShapeDtypeStruct((cols // per_group, rows * per_group, DISP), jnp.bfloat16))
     return pl.pallas_call(
-        functools.partial(cost_kernel, (rows, cols, total_rows, total_cols)),
-        out_shape=jax.ShapeDtypeStruct((rows, cols, DISP), jnp.float32),
+        functools.partial(cost_kernel, (rows, cols, total_rows, total_cols, per_group)),
+        out_shape=tuple(shapes),
         in_specs=[pl.BlockSpec(memory_space=pltpu.SMEM)] + [vmem] * 5,
-        out_specs=vmem,
+        out_specs=(vmem,) * len(shapes),
         scratch_shapes=bufs,
         compiler_params=pltpu.CompilerParams(vmem_limit_bytes=40 << 20),
         cost_estimate=pl.CostEstimate(flops=8_000_000_000, bytes_accessed=6_000_000, transcendentals=0),
@@ -283,16 +297,17 @@
             pltpu.VMEM((16, 8, LANES), jnp.float32),
             pltpu.VMEM((8, LANES), jnp.float32),
         ],
-        compiler_params=pltpu.CompilerParams(vmem_limit_bytes=40 << 20),
+        compiler_params=pltpu.CompilerParams(vmem_limit_bytes=20 << 20),
         cost_estimate=pl.CostEstimate(flops=2_000_000_000, bytes_accessed=30_000_000, transcendentals=0),
     )(*args)
 
 
-def column_kernel(cost_ref, out_ref):
+def column_kernel(cost_ref, out_ref, sum_ref):
     length, width, _ = cost_ref.shape
     lane = lax.broadcasted_iota(jnp.int32, (width, DISP), 1)
 
-    def step(state, cost):
+    def step(state, index):
+        cost = cost_ref[index].astype(jnp.float32)
         low = jnp.min(state, axis=1, keepdims=True)
         above = jnp.where(lane == DISP - 1, BIG, pltpu.roll(state, DISP - 1, 1))
         below = jnp.where(lane == 0, BIG, pltpu.roll(state, 1, 1))
@@ -300,17 +315,17 @@
         return cost + jnp.minimum(jnp.minimum(state, near), low + P_LARGE) - low
 
     def first(index, states):
-        down = step(states[0], cost_ref[index])
-        up = step(states[1], cost_ref[length - 1 - index])
-        out_ref[index] = down
-        out_ref[length - 1 - index] = up
+        down = step(states[0], index)
+        up = step(states[1], length - 1 - index)
+        sum_ref[index] = down
+        sum_ref[length - 1 - index] = up
         return down, up
 
     def second(index, states):
-        down = step(states[0], cost_ref[index])
-        up = step(states[1], cost_ref[length - 1 - index])
-        out_ref[index] += down
-        out_ref[length - 1 - index] += up
+        down = step(states[0], index)
+        up = step(states[1], length - 1 - index)
+        out_ref[index] = (sum_ref[index] + down).astype(jnp.bfloat16)
+        out_ref[length - 1 - index] = (sum_ref[length - 1 - index] + up).astype(jnp.bfloat16)
         return down, up
 
     zero = jnp.zeros((width, DISP), jnp.float32)
@@ -322,58 +337,96 @@
     vmem = pl.BlockSpec(memory_space=pltpu.VMEM)
     return pl.pallas_call(
         column_kernel,
-        out_shape=jax.ShapeDtypeStruct(columns.shape, jnp.float32),
+        out_shape=jax.ShapeDtypeStruct(columns.shape, jnp.bfloat16),
         in_specs=[vmem],
         out_specs=vmem,
-        compiler_params=pltpu.CompilerParams(vmem_limit_bytes=24 << 20),
+        scratch_shapes=[pltpu.VMEM(columns.shape, jnp.float32)],
+        compiler_params=pltpu.CompilerParams(vmem_limit_bytes=12 << 20),
         cost_estimate=pl.CostEstimate(flops=200_000_000, bytes_accessed=2_000_000, transcendentals=0),
     )(columns)
 
 
+def add_kernel(across_ref, down_ref, out_ref):
+    cols = across_ref.shape[1]
+    out_ref[0] = across_ref[0] + down_ref[...].reshape(cols, DISP).astype(jnp.float32)
+
+
+def add_vertical(horizontal, vertical):
+    rows, cols, _ = horizontal.shape
+    groups, _, per_group, _ = vertical.shape
+    if not packs(per_group):
+        return horizontal + jnp.swapaxes(vertical, 0, 1).reshape(rows, cols, DISP).astype(jnp.float32)
+    whole = pl.BlockSpec((1, cols, DISP), lambda row: (row, 0, 0))
+    return pl.pallas_call(
+        add_kernel,
+        out_shape=jax.ShapeDtypeStruct(horizontal.shape, jnp.float32),
+        grid=(rows,),
+        in_specs=[whole, pl.BlockSpec((groups, None, per_group, DISP), lambda row: (0, row, 0, 0))],
+        out_specs=whole,
+        cost_estimate=pl.CostEstimate(flops=300_000, bytes_accessed=2_600_000, transcendentals=0),
+    )(horizontal, vertical)
+
+
 def normalize(image_pixels):
     return (image_pixels.astype(jnp.float32) / 1024.0 - 2.0).astype(jnp.bfloat16)
 
 
-def layer_weights(conv_weights, rows_in, rows_out):
-    base = jnp.transpose(conv_weights, (0, 4, 3, 2, 1))
-    taps = base.shape[2]
-    columns = [
-        jnp.pad(base, ((0, 0), (0, 0), (row, rows_in - taps - row), (0, 0), (0, 0)))
-        for row in range(rows_out)
-    ]
-    joined = jnp.concatenate(columns, axis=-1)
-    return joined.reshape(base.shape[0], base.shape[1], rows_in * base.shape[3], rows_out * base.shape[4])
+def weights_kernel(rows, base_ref, first_ref, wt_ref, w1_ref):
+    wt_ref[...] = jnp.zeros_like(wt_ref)
+    layers, taps = base_ref.shape[0], base_ref.shape[1]
+    for layer in range(layers):
+        for dy in range(taps):
+            for dx in range(taps):
+                block = base_ref[layer, dy, dx].astype(jnp.float32).T.astype(jnp.bfloat16)
+                for out in range(wt_ref.shape[3] // CH):
+                    top = (out + dy) * CH
+                    wt_ref[layer, dx, top : top + CH, out * CH : (out + 1) * CH] = block
+    shape = w1_ref.shape
+    row = lax.broadcasted_iota(jnp.int32, shape, 0)
+    tall = rows + 8
+    dx_at, dy_at = row // tall, row % tall - lax.broadcasted_iota(jnp.int32, shape, 1) // CH
+    value = jnp.zeros(shape, jnp.float32)
+    for dy in range(taps):
+        for dx in range(taps):
+            line = first_ref[dy * taps + dx : dy * taps + dx + 1, :]
+            value = jnp.where((dx_at == dx) & (dy_at == dy), line, value)
+    w1_ref[...] = value.astype(jnp.bfloat16)
+
+
+def banded_weights(first_weight, conv_weights, rows):
+    base = jnp.transpose(conv_weights, (0, 3, 4, 1, 2))
+    lines = jnp.transpose(first_weight, (1, 2, 3, 0)).reshape(9, CH).astype(jnp.float32)
+    lines = jnp.tile(lines, (1, rows + 6))
+    vmem = pl.BlockSpec(memory_space=pltpu.VMEM)
+    return pl.pallas_call(
+        functools.partial(weights_kernel, rows),
+        out_shape=(
+            jax.ShapeDtypeStruct((base.shape[0], 3, 6 * CH, 4 * CH), jnp.bfloat16),
+            jax.ShapeDtypeStruct((LANES, (rows + 6) * CH), jnp.bfloat16),
+        ),
+        in_specs=[vmem, vmem],
+        out_specs=(vmem, vmem),
+        compiler_params=pltpu.CompilerParams(vmem_limit_bytes=12 << 20),
+        cost_estimate=pl.CostEstimate(flops=10_000_000, bytes_accessed=2_500_000, transcendentals=0),
+    )(base, lines)
 
 
 def neighbours(pair, row_axis, strip_axis):
     groups, strips = lax.axis_size(row_axis), lax.axis_size(strip_axis)
-    axes = (row_axis, strip_axis)
-    strip = lax.axis_index(strip_axis)
-
-    def moved(up, across):
-        route = []
-        for r in range(groups):
-            for s in range(strips):
-                source = (r + up, s ^ across)
-                if 0 <= source[0] < groups:
-                    route.append((source[0] * strips + source[1], r * strips + s))
-        return lax.ppermute(pair, axes, route)
-
-    bands = []
-    for up in (-1, 0, 1):
-        own = pair if up == 0 else moved(up, 0)
-        other = moved(up, 1)
-        joined = jnp.where(strip == 0, jnp.concatenate([own, other], 2), jnp.concatenate([other, own], 2))
-        bands.append(joined)
-    return jnp.concatenate(bands, axis=1)
+    above = lax.ppermute(pair, row_axis, [(i, i + 1) for i in range(groups - 1)])
+    below = lax.ppermute(pair, row_axis, [(i + 1, i) for i in range(groups - 1)])
+    own = jnp.concatenate([above, pair, below], axis=1)
+    other = lax.ppermute(own, strip_axis, [(i, i ^ 1) for i in range(strips)])
+    first = lax.axis_index(strip_axis) == 0
+    return jnp.concatenate([jnp.where(first, own, other), jnp.where(first, other, own)], axis=2)
 
 
 def stacked(image, start, length, flipped):
-    parts = []
-    for dx in range(3):
-        part = lax.dynamic_slice_in_dim(image, start + dx - 1, length, 1)
-        parts.append(part[:, ::-1] if flipped else part)
-    joined = jnp.concatenate(parts, axis=0)
+    part = lax.dynamic_slice_in_dim(image, start - 1, length + 2, 1)
+    if flipped:
+        part = part[:, ::-1]
+    shifts = [part[:, dx : dx + length] for dx in ((2, 1, 0) if flipped else (0, 1, 2))]
+    joined = jnp.concatenate(shifts, axis=0)
     joined = jnp.pad(joined, ((0, LANES - joined.shape[0]), (0, 0)))
     return joined.T
 
@@ -384,10 +437,7 @@
     group, strip = lax.axis_index("rows"), lax.axis_index("strips")
     total_rows, total_cols = rows * groups, cols * strips
 
-    wt = layer_weights(conv_weights, 6, 4)
-    w1 = layer_weights(first_weight[None], rows + 8, rows + 6)[0].reshape(3 * (rows + 8), (rows + 6) * CH)
-    w1 = jnp.pad(w1, ((0, LANES - w1.shape[0]), (0, 0)))
-
+    wt, w1 = banded_weights(first_weight, conv_weights, rows)
     pair = jnp.stack([normalize(left_pixels), normalize(right_pixels)])
     band = neighbours(pair, "rows", "strips")[:, rows - 4 : 2 * rows + 4]
     left_length, right_length = plan(cols)[0], plan(cols + DISP)[0]
@@ -401,10 +451,14 @@
     mask = jnp.repeat((valid_mask.astype(jnp.float32) * scale).astype(jnp.bfloat16).T, CH, axis=1)
     place = jnp.stack([group * rows, first_col, strip]).astype(jnp.int32)
 
-    cost = cost_volume(left_stack, right_stack, mask, w1, wt, place, rows, cols, total_rows, total_cols)
-
     per_group = cols // groups
-    grouped = jnp.swapaxes(cost.reshape(rows, groups, per_group, DISP), 0, 1)
+    cost, *packed = cost_volume(
+        left_stack, right_stack, mask, w1, wt, place, rows, cols, total_rows, total_cols, per_group
+    )
+    if packed:
+        grouped = packed[0].reshape(groups, rows, per_group, DISP)
+    else:
+        grouped = jnp.swapaxes(cost.astype(jnp.bfloat16).reshape(rows, groups, per_group, DISP), 0, 1)
     columns = lax.all_to_all(grouped, "rows", split_axis=0, concat_axis=0, tiled=True)
     columns = columns.reshape(total_rows, per_group, DISP)
 
@@ -417,8 +471,7 @@
         column_sum.reshape(groups, rows, per_group, DISP), "rows", split_axis=0, concat_axis=0, tiled=True
     )
     horizontal, _ = row_scan(place, cost, received, leading, True)
-    vertical = jnp.swapaxes(vertical, 0, 1).reshape(rows, cols, DISP)
-    return horizontal + vertical
+    return add_vertical(horizontal, vertical)
 
 
 def solution(mesh):

time: 109 us -> 84.6 us (0.78)
  waiting for transfers between devices: 14.8 us -> 4.26 us
  starting transfers between devices: 27.4 us -> 20.7 us
  local copies, waits for them, and re-layouts: 11.9 us -> 5.53 us
  other arithmetic: 6.78 us -> 2.38 us
  Pallas kernels: 47 us -> 51 us
    all_to_all x1, waiting for transfers between devices: 8.38 us -> 0.17 us  [per_device(): lax.all_to_all(grouped, 'rows', split_axis=0, concat_axis=0, tiled=True)]
    all_to_all x1, waiting for transfers between devices: 5.14 us -> 0.01 us  [per_device(): lax.all_to_all(column_sum.reshape(groups, rows, per_group, DISP), 'rows',...]
    ppermute x5 -> x3, starting transfers between devices: 11 us -> 6.21 us  [the longest x1 4.84 us: neighbours(): lax.ppermute(pair, row_axis, [(i, i + 1) for i in range(groups - 1)])]
    concatenate x4, other arithmetic: 4.83 us -> 0.15 us  [the longest x1 0.09 us: neighbours(): jnp.concatenate([jnp.where(first, own, other), jnp.where(first, other, ow...]
    pallas_call x0 -> x2, Pallas kernels: none -> 4.36 us  [the longest x1 3.45 us: add_vertical(): pl.pallas_call(add_kernel, out_shape=jax.ShapeDtypeStruct(horizontal.shap...]
    concatenate x5 -> x2, local copies, waits for them, and re-layouts: 4.04 us -> 0.32 us  [stacked(): joined = jnp.concatenate(shifts, axis=0)]
    ppermute x5 -> x3, waiting for transfers between devices: 0.01 us -> 2.85 us  [the longest x1 2.85 us: neighbours(): lax.ppermute(pair, row_axis, [(i + 1, i) for i in range(groups - 1)])]
    all_to_all x1, starting transfers between devices: 9.41 us -> 7.65 us  [per_device(): lax.all_to_all(grouped, 'rows', split_axis=0, concat_axis=0, tiled=True)]
  transfers between devices with their start and end apart: 8 -> 6, of which waited for: 3 -> 3; matrix products, arithmetic and copies ran while one was open for 9% -> 2% of each run, Pallas kernels for 29% -> 38%
where the time goes in v3:
time: 84.6 us; the launch traced here: 84.1 us
  Pallas kernels  51 us (60%)
  starting transfers between devices  20.7 us (24%)
  local copies, waits for them, and re-layouts  5.53 us (7%)
  waiting for transfers between devices  4.26 us (5%)
  other arithmetic  2.38 us (3%)
    pallas_call x2, Pallas kernels, row_scan(): pl.pallas_call(functools.partial(row_scan_kernel, (rows, cols, flip, batc...  31.3 us
    pallas_call x1, Pallas kernels, column_scan(): pl.pallas_call(column_kernel, out_shape=jax.ShapeDtypeStruct(columns.shap...  7.73 us
    all_to_all x1, starting transfers between devices, per_device(): lax.all_to_all(grouped, 'rows', split_axis=0, concat_axis=0, tiled=True)  7.65 us
    pallas_call x1, Pallas kernels, cost_volume(): pl.pallas_call(functools.partial(cost_kernel, (rows, cols, total_rows, to...  7.63 us
    all_to_all x1, starting transfers between devices, per_device(): lax.all_to_all(column_sum.reshape(groups, rows, per_group, DISP), 'rows',...  6.75 us
    ppermute x1, starting transfers between devices, neighbours(): lax.ppermute(pair, row_axis, [(i, i + 1) for i in range(groups - 1)])  4.84 us
    unnamed x12, local copies, waits for them, and re-layouts  4.52 us
    pallas_call x1, Pallas kernels, add_vertical(): pl.pallas_call(add_kernel, out_shape=jax.ShapeDtypeStruct(horizontal.shap...  3.45 us
  transfers between devices with their start and end apart: 6, of which 3 were waited for; matrix products, arithmetic and copies ran while one was open for 2% of the time, Pallas kernels for 38%

profile of v3, /device:TPU:0, one launch (start us, length us, event | category | flops | bytes accessed | tf_op | source)
XLA Modules:
  0.0 84.1 jit_solution(13445454941378902073)
XLA Ops:
  0.0 0.7 fusion.4
  0.7 4.8 %collective-permute-start = (bf16[2,4,512]{2,1,0:T(4,128)(2,1)S(1)}, bf16[2,4,512]{2,1,0:T(4,128)(2,1)S(1)}, u32[]{:S(2)}, u32[]{:S(2)}) collective-permute-start(bf16[2,4,512]{2,1,0:T(4,128)(2,1)S(1)} %pad_maximum_fusion.3), channel_id=1, source_target_pairs={{0,2},{2,4},{4,6},{6,8},{8,10},{10,12},{12,14},{14,16},{16,18},{18... | collective-permute-start | bytes 24584 | tf_op jit(solution)/shard_map/ppermute | solution.py:416
  5.6 1.3 %collective-permute-start.1 = (bf16[2,4,512]{2,1,0:T(4,128)(2,1)S(1)}, bf16[2,4,512]{2,1,0:T(4,128)(2,1)S(1)}, u32[]{:S(2)}, u32[]{:S(2)}) collective-permute-start(bf16[2,4,512]{2,1,0:T(4,128)(2,1)S(1)} %pad_maximum_fusion.3), channel_id=1, source_target_pairs={{2,0},{4,2},{6,4},{8,6},{10,8},{12,10},{14,12},{16,14},{18,16},{20... | collective-permute-start | bytes 24584 | tf_op jit(solution)/shard_map/ppermute | solution.py:417
  6.9 0.7 fusion.6
  7.6 0.7 convert_bitcast_fusion
  8.3 0.0 collective-permute-done
  8.3 2.8 %collective-permute-done.1 = bf16[2,4,512]{2,1,0:T(4,128)(2,1)S(1)} collective-permute-done((bf16[2,4,512]{2,1,0:T(4,128)(2,1)S(1)}, bf16[2,4,512]{2,1,0:T(4,128)(2,1)S(1)}, u32[]{:S(2)}, u32[]{:S(2)}) %collective-permute-start.1) | collective-permute-done | bytes 8224 | tf_op jit(solution)/shard_map/ppermute | solution.py:417
  11.2 0.1 collective-permute-start.2
  11.2 0.1 pad_add_fusion.where_ref.place_ref
  11.3 0.1 tile.10.first_ref
  11.4 0.1 copy.14.mask_ref
  11.6 0.0 copy-start.1
  11.6 1.0 %copy-done.1 = bf16[3,64,64,3,3]{2,1,4,3,0:T(8,128)(2,1)S(1)} copy-done((bf16[3,64,64,3,3]{2,1,4,3,0:T(8,128)(2,1)S(1)}, bf16[3,64,64,3,3]{2,1,4,3,0:T(8,128)(2,1)}, u32[]{:S(2)}) %copy-start.1) | copy-done | bytes 221208
  12.6 0.9 %shard_map.55 = (bf16[3,3,384,256]{3,2,1,0:T(8,128)(2,1)S(1)}, bf16[128,640]{1,0:T(8,128)(2,1)S(1)}) custom-call(bf16[3,3,3,64,64]{4,3,2,1,0:T(8,128)(2,1)S(1)} %bitcast.28, f32[9,640]{1,0:T(8,128)S(1)} %tile.10.first_ref), custom_call_target="tpu_custom_call" | custom-call | flops 10000000 | bytes 2500000 | tf_op jit(solution)/shard_map/pallas_call | solution.py:401
  13.5 0.0 collective-permute-done.2
  13.6 0.1 fusion.3
  13.7 0.1 dynamic-slice_bitcast_fusion
  13.8 0.1 fusion.8
  13.9 0.5 reverse.3
  14.4 0.1 slice.52
  14.4 0.5 reverse.4
  14.9 0.1 slice.53
  15.0 0.5 reverse.5
  15.5 0.1 slice.54
  15.6 0.2 copy.13
  15.8 0.1 dynamic-slice_bitcast_fusion.1
  15.9 0.1 fusion.9
  16.0 0.1 copy.12
  16.2 7.6 %shard_map.56 = (f32[4,512,128]{2,1,0:T(8,128)S(1)}, bf16[16,128,128]{2,1,0:T(8,128)(2,1)}) custom-call(s32[3]{0:T(128)S(1)} %pad_add_fusion.where_ref.place_ref, bf16[560,128]{1,0:T(8,128)(2,1)S(1)} %pad_bitcast_fusion.1.left_ref, bf16[688,128]{1,0:T(8,128)(2,1)S(1)} %pad_bitcast_fusion.right_ref, bf16[512,256]{1,0:T(8,128)(2,1)S(1)} %copy.14.mask_ref, ...), custom_call_target="tpu_custom_call" | custom-call | flops 8000000000 | bytes 6000000 | tf_op jit(solution)/shard_map/pallas_call | solution.py:140
  23.9 7.6 %all-to-all-start = ((bf16[16,4,32,128]{3,2,1,0:T(8,128)(2,1)}), bf16[16,4,32,128]{3,2,1,0:T(8,128)(2,1)S(1)}, u32[]{:S(2)}, u32[]{:S(2)}) async-start(bf16[16,4,32,128]{3,2,1,0:T(8,128)(2,1)} %bitcast.13), calls=%async_computation | async-start | bytes 1048576 | tf_op jit(solution)/shard_map/all_to_all | solution.py:462
  31.5 15.3 %shard_map.57 = (f32[4,512,128]{2,1,0:T(8,128)S(1)}, f32[16,8,128]{2,1,0:T(8,128)S(1)}) custom-call(s32[3]{0:T(128)S(1)} %pad_add_fusion.where_ref.place_ref, f32[4,512,128]{2,1,0:T(8,128)S(1)} %get-tuple-element.16.cost_ref, f32[16,8,128]{2,1,0:T(8,128)S(1)} %broadcast_in_dim.7.state_ref), custom_call_target="tpu_custom_call" | custom-call | flops 2000000000 | bytes 30000000 | tf_op jit(solution)/shard_map/pallas_call | solution.py:281
  46.8 0.2 all-to-all-done
  47.0 7.7 %shard_map.59 = bf16[64,32,128]{2,1,0:T(8,128)(2,1)} custom-call(bf16[64,32,128]{2,1,0:T(8,128)(2,1)S(1)} %bitcast.27), custom_call_target="tpu_custom_call" | custom-call | flops 200000000 | bytes 2000000 | tf_op jit(solution)/shard_map/pallas_call | solution.py:338
  54.7 6.8 %all-to-all-start.1 = ((bf16[16,4,32,128]{3,2,1,0:T(8,128)(2,1)}), bf16[16,4,32,128]{3,2,1,0:T(8,128)(2,1)S(1)}, u32[]{:S(2)}, u32[]{:S(2)}) async-start(bf16[16,4,32,128]{3,2,1,0:T(8,128)(2,1)} %bitcast.15), calls=%async_computation.1 | async-start | bytes 1048576 | tf_op jit(solution)/shard_map/all_to_all | solution.py:470
  61.5 0.1 collective-permute-start.3
  61.5 1.2 %collective-permute-done.3.state_ref = f32[16,8,128]{2,1,0:T(8,128)S(1)} collective-permute-done((f32[16,8,128]{2,1,0:T(8,128)S(1)}, f32[16,8,128]{2,1,0:T(8,128)S(1)}, u32[]{:S(2)}, u32[]{:S(2)}) %collective-permute-start.3) | collective-permute-done | bytes 65568 | tf_op jit(solution)/shard_map/ppermute | solution.py:469
  62.8 16.0 %shard_map.58 = (f32[4,512,128]{2,1,0:T(8,128)S(1)}, f32[16,8,128]{2,1,0:T(8,128)}) custom-call(s32[3]{0:T(128)S(1)} %pad_add_fusion.where_ref.place_ref, f32[4,512,128]{2,1,0:T(8,128)S(1)} %get-tuple-element.16.cost_ref, f32[16,8,128]{2,1,0:T(8,128)S(1)} %collective-permute-done.3.state_ref, f32[4,512,128]{2,1,0:T(8,128)S(1)} %get-tuple-element.20.rest_0_), custom_call_target="tpu_custom_call" | custom-call | flops 2000000000 | bytes 30000000 | tf_op jit(solution)/shard_map/pallas_call | solution.py:281
  78.8 0.0 copy-start
  78.8 1.0 %copy-done = f32[4,512,128]{2,1,0:T(8,128)} copy-done((f32[4,512,128]{2,1,0:T(8,128)}, f32[4,512,128]{2,1,0:T(8,128)S(1)}, u32[]{:S(2)}) %copy-start) | copy-done | bytes 1048600
  79.8 0.0 all-to-all-done.1.down_ref
  79.8 0.0 copy-start.2
  79.8 0.8 copy-done.2
  80.6 3.4 %shard_map.60 = f32[4,512,128]{2,1,0:T(8,128)} custom-call(f32[4,512,128]{2,1,0:T(8,128)} %copy-done, bf16[16,4,32,128]{3,2,1,0:T(8,128)(2,1)} %copy-done.2), custom_call_target="tpu_custom_call" | custom-call | flops 300000 | bytes 2600000 | tf_op jit(solution)/shard_map/pallas_call | solution.py:360
  (12 shorter events, 0.2 us)
Async XLA Ops:
  0.7 7.5 %collective-permute-start = (bf16[2,4,512]{2,1,0:T(4,128)(2,1)S(1)}, bf16[2,4,512]{2,1,0:T(4,128)(2,1)S(1)}, u32[]{:S(2)}, u32[]{:S(2)}) collective-permute-start(bf16[2,4,512]{2,1,0:T(4,128)(2,1)S(1)} %pad_maximum_fusion.3), channel_id=1, source_target_pairs={{0,2},{2,4},{4,6},{6,8},{8,10},{10,12},{12,14},{14,16},{16,18},{18... | collective-permute-start | bytes 24584 | tf_op jit(solution)/shard_map/ppermute | solution.py:416
  5.6 5.5 %collective-permute-start.1 = (bf16[2,4,512]{2,1,0:T(4,128)(2,1)S(1)}, bf16[2,4,512]{2,1,0:T(4,128)(2,1)S(1)}, u32[]{:S(2)}, u32[]{:S(2)}) collective-permute-start(bf16[2,4,512]{2,1,0:T(4,128)(2,1)S(1)} %pad_maximum_fusion.3), channel_id=1, source_target_pairs={{2,0},{4,2},{6,4},{8,6},{10,8},{12,10},{14,12},{16,14},{18,16},{20... | collective-permute-start | bytes 24584 | tf_op jit(solution)/shard_map/ppermute | solution.py:417
  11.2 2.4 %collective-permute-start.2 = (bf16[2,12,512]{2,1,0:T(8,128)(2,1)S(1)}, bf16[2,12,512]{2,1,0:T(8,128)(2,1)S(1)}, u32[]{:S(2)}, u32[]{:S(2)}) collective-permute-start(bf16[2,12,512]{2,1,0:T(8,128)(2,1)S(1)} %pad_maximum_fusion.2), channel_id=1, source_target_pairs={{0,1},{1,0},{2,3},{3,2},{4,5},{5,4},{6,7},{7,6},{8,9},{9,8},{10,11... | collective-permute-start | bytes 73736 | tf_op jit(solution)/shard_map/ppermute | solution.py:419
  11.6 1.0 %copy-start.1 = (bf16[3,64,64,3,3]{2,1,4,3,0:T(8,128)(2,1)S(1)}, bf16[3,64,64,3,3]{2,1,4,3,0:T(8,128)(2,1)}, u32[]{:S(2)}) copy-start(bf16[3,64,64,3,3]{2,1,4,3,0:T(8,128)(2,1)} %param.9) | copy-start | bytes 663556
  23.9 23.1 %all-to-all-start = ((bf16[16,4,32,128]{3,2,1,0:T(8,128)(2,1)}), bf16[16,4,32,128]{3,2,1,0:T(8,128)(2,1)S(1)}, u32[]{:S(2)}, u32[]{:S(2)}) async-start(bf16[16,4,32,128]{3,2,1,0:T(8,128)(2,1)} %bitcast.13), calls=%async_computation | async-start | bytes 1048576 | tf_op jit(solution)/shard_map/all_to_all | solution.py:462
  54.7 25.1 %all-to-all-start.1 = ((bf16[16,4,32,128]{3,2,1,0:T(8,128)(2,1)}), bf16[16,4,32,128]{3,2,1,0:T(8,128)(2,1)S(1)}, u32[]{:S(2)}, u32[]{:S(2)}) async-start(bf16[16,4,32,128]{3,2,1,0:T(8,128)(2,1)} %bitcast.15), calls=%async_computation.1 | async-start | bytes 1048576 | tf_op jit(solution)/shard_map/all_to_all | solution.py:470
  61.5 1.3 %collective-permute-start.3 = (f32[16,8,128]{2,1,0:T(8,128)S(1)}, f32[16,8,128]{2,1,0:T(8,128)S(1)}, u32[]{:S(2)}, u32[]{:S(2)}) collective-permute-start(f32[16,8,128]{2,1,0:T(8,128)S(1)} %get-tuple-element.19), channel_id=1, source_target_pairs={{0,1},{1,0},{2,3},{3,2},{4,5},{5,4},{6,7},{7,6},{8,9},{9,8},{10,11... | collective-permute-start | bytes 196616 | tf_op jit(solution)/shard_map/ppermute | solution.py:469
  78.8 1.0 %copy-start = (f32[4,512,128]{2,1,0:T(8,128)}, f32[4,512,128]{2,1,0:T(8,128)S(1)}, u32[]{:S(2)}) copy-start(f32[4,512,128]{2,1,0:T(8,128)S(1)} %get-tuple-element.21.across_ref) | copy-start | bytes 3145732
  79.8 0.8 copy-start.2

commit v4 on v3

--- a/solution.py
+++ b/solution.py
@@ -116,6 +116,7 @@
             skewed = skewed[:, :LANES]
             cost_ref[row, pl.ds(start, LANES), :] = skewed
             if payload_ref is not None:
+                skewed = skewed - jnp.mean(skewed, axis=1, keepdims=True)
                 for k in range(LANES // per_group):
                     piece = skewed[k * per_group : (k + 1) * per_group].astype(jnp.bfloat16)
                     group = index * (LANES // per_group) + k
@@ -169,15 +170,6 @@
 
     lax.fori_loop(0, width // 2, build_pick, 0)
 
-    def lowest(state):
-        level = list(state)
-        while len(level) > 1:
-            level = [jnp.minimum(level[i], level[i + 1]) for i in range(0, len(level), 2)]
-        low = level[0]
-        for shift in (4, 2, 1):
-            low = jnp.minimum(low, pltpu.roll(low, shift, 0))
-        return low
-
     def chunk_start(index):
         chunk = jnp.where(forward, index, count - 1 - index)
         return pl.multiple_of(chunk * width, width)
@@ -210,7 +202,8 @@
         for row in range(rows):
             piece = done[row * width : (row + 1) * width]
             if has_sum:
-                piece = piece + lead_ref[row, pl.ds(start, width), :]
+                offset = jnp.mean(cost_ref[row, pl.ds(start, width), :], axis=1, keepdims=True)
+                piece = piece + (lead_ref[row, pl.ds(start, width), :] + 2.0 * offset)
             out_ref[row, pl.ds(start, width), :] = piece
 
     def advance(state, low, slot, step, current):
@@ -333,36 +326,140 @@
     lax.fori_loop(length // 2, length, second, states)
 
 
+def lowest(state):
+    level = list(state)
+    while len(level) > 1:
+        level = [jnp.minimum(level[i], level[i + 1]) for i in range(0, len(level), 2)]
+    low = level[0]
+    for shift in (4, 2, 1):
+        low = jnp.minimum(low, pltpu.roll(low, shift, 0))
+    return low
+
+
+def column_tiles_kernel(cost_ref, out_ref, tile_ref, split_ref, spread_ref, path_ref, turn_ref, sum_ref):
+    length, width, _ = cost_ref.shape
+    both = 2 * width
+    per = LANES // both
+    tiles = length // per
+    sublane = lax.broadcasted_iota(jnp.int32, (8, LANES), 0)
+    lane_step = lax.broadcasted_iota(jnp.int32, (8, LANES), 1) // both
+    k = lax.broadcasted_iota(jnp.int32, (LANES, per * LANES), 0)
+    n = lax.broadcasted_iota(jnp.int32, (LANES, per * LANES), 1)
+    pick = jnp.where(k == n // LANES * both + n % both, 1.0, 0.0).astype(jnp.bfloat16)
+
+    def places(tile):
+        rows = []
+        for step in range(per):
+            rows += [tile * per + step, length - 1 - (tile * per + step)]
+        return rows
+
+    def prepare(index, carry):
+        for slot in range(8):
+            tile = index * 8 + slot
+            block = jnp.concatenate([cost_ref[row] for row in places(tile)], axis=0)
+            tile_ref[slot] = block.astype(jnp.float32).T
+            for v in range(0, 16, 2):
+                plane = jnp.concatenate(
+                    [tile_ref[slot, pl.ds(v, 8, stride=16), :], tile_ref[slot, pl.ds(v + 1, 8, stride=16), :]], axis=0
+                )
+                split_ref[slot * LANES + v * 8 : slot * LANES + v * 8 + 16, :] = plane.astype(jnp.bfloat16)
+        spread = jnp.dot(split_ref[...], pick, preferred_element_type=jnp.float32)
+        for slot in range(8):
+            for step in range(per):
+                spread_ref[index * 8 + slot, step] = spread[
+                    slot * LANES : slot * LANES + LANES, step * LANES : step * LANES + LANES
+                ]
+        return carry
+
+    lax.fori_loop(0, tiles // 8, prepare, 0)
+
+    def emit(tile, last):
+        tile = jnp.maximum(tile, 0)
+        for v in range(16):
+            turn_ref[pl.ds(v, 8, stride=16), :] = path_ref[v]
+        done = turn_ref[...].T
+        for i, row in enumerate(places(tile)):
+            piece = done[i * width : (i + 1) * width]
+            if last:
+                out_ref[row] = (sum_ref[row] + piece).astype(jnp.bfloat16)
+            else:
+                sum_ref[row] = piece
+
+    def run(tile, state, last):
+        emit(tile - 1, last)
+        state = list(state)
+        for step in range(per):
+            low = lowest(state)
+            bound = low + P_LARGE
+            above = jnp.where(sublane == 7, BIG, pltpu.roll(state[0], 7, 0))
+            below = jnp.where(sublane == 0, BIG, pltpu.roll(state[15], 1, 0))
+            padded = [below] + state + [above]
+            fresh = []
+            for v in range(16):
+                near = jnp.minimum(padded[v], padded[v + 2]) + P_SMALL
+                best = jnp.minimum(jnp.minimum(state[v], near), bound)
+                value = spread_ref[tile, step, v * 8 : v * 8 + 8, :] + (best - low)
+                if step:
+                    pltpu.store(path_ref.at[v], value, mask=lane_step == step)
+                else:
+                    path_ref[v] = value
+                fresh.append(value)
+            state = fresh
+        return tuple(state)
+
+    def loop(begin, end, state, last):
+        return lax.fori_loop(begin, end, lambda tile, carry: run(tile, carry, last), state, unroll=8)
+
+    state = (jnp.zeros((8, LANES), jnp.float32),) * 16
+    state = loop(0, tiles // 2, state, False)
+    emit(tiles // 2 - 1, False)
+    state = loop(tiles // 2, tiles, state, True)
+    emit(tiles - 1, True)
+
+
 def column_scan(columns):
+    length, width, _ = columns.shape
     vmem = pl.BlockSpec(memory_space=pltpu.VMEM)
+    scratch = [pltpu.VMEM(columns.shape, jnp.float32)]
+    kernel = column_kernel
+    per = LANES // (2 * width)
+    if width % 16 == 0 and LANES % (2 * width) == 0 and length % (16 * per) == 0:
+        kernel = column_tiles_kernel
+        scratch = [
+            pltpu.VMEM((8, LANES, LANES), jnp.float32),
+            pltpu.VMEM((8 * LANES, LANES), jnp.bfloat16),
+            pltpu.VMEM((length // per, per, LANES, LANES), jnp.float32),
+            pltpu.VMEM((16, 8, LANES), jnp.float32),
+            pltpu.VMEM((LANES, LANES), jnp.float32),
+        ] + scratch
     return pl.pallas_call(
-        column_kernel,
+        kernel,
         out_shape=jax.ShapeDtypeStruct(columns.shape, jnp.bfloat16),
         in_specs=[vmem],
         out_specs=vmem,
-        scratch_shapes=[pltpu.VMEM(columns.shape, jnp.float32)],
-        compiler_params=pltpu.CompilerParams(vmem_limit_bytes=12 << 20),
+        scratch_shapes=scratch,
+        compiler_params=pltpu.CompilerParams(vmem_limit_bytes=20 << 20),
         cost_estimate=pl.CostEstimate(flops=200_000_000, bytes_accessed=2_000_000, transcendentals=0),
     )(columns)
 
 
 def add_kernel(across_ref, down_ref, out_ref):
-    cols = across_ref.shape[1]
-    out_ref[0] = across_ref[0] + down_ref[...].reshape(cols, DISP).astype(jnp.float32)
+    rows, cols, _ = across_ref.shape
+    for row in range(rows):
+        out_ref[row] = across_ref[row] + down_ref[:, row].reshape(cols, DISP).astype(jnp.float32)
 
 
 def add_vertical(horizontal, vertical):
     rows, cols, _ = horizontal.shape
-    groups, _, per_group, _ = vertical.shape
-    if not packs(per_group):
+    if not packs(vertical.shape[2]):
         return horizontal + jnp.swapaxes(vertical, 0, 1).reshape(rows, cols, DISP).astype(jnp.float32)
-    whole = pl.BlockSpec((1, cols, DISP), lambda row: (row, 0, 0))
+    vmem = pl.BlockSpec(memory_space=pltpu.VMEM)
     return pl.pallas_call(
         add_kernel,
         out_shape=jax.ShapeDtypeStruct(horizontal.shape, jnp.float32),
-        grid=(rows,),
-        in_specs=[whole, pl.BlockSpec((groups, None, per_group, DISP), lambda row: (0, row, 0, 0))],
-        out_specs=whole,
+        in_specs=[vmem, vmem],
+        out_specs=vmem,
+        compiler_params=pltpu.CompilerParams(vmem_limit_bytes=8 << 20),
         cost_estimate=pl.CostEstimate(flops=300_000, bytes_accessed=2_600_000, transcendentals=0),
     )(horizontal, vertical)
 
@@ -411,20 +508,21 @@
     )(base, lines)
 
 
-def neighbours(pair, row_axis, strip_axis):
+def neighbours(pair, weights, row_axis, strip_axis):
     groups, strips = lax.axis_size(row_axis), lax.axis_size(strip_axis)
     above = lax.ppermute(pair, row_axis, [(i, i + 1) for i in range(groups - 1)])
     below = lax.ppermute(pair, row_axis, [(i + 1, i) for i in range(groups - 1)])
+    above, below, weights = lax.optimization_barrier((above, below, weights))
     own = jnp.concatenate([above, pair, below], axis=1)
     other = lax.ppermute(own, strip_axis, [(i, i ^ 1) for i in range(strips)])
     first = lax.axis_index(strip_axis) == 0
-    return jnp.concatenate([jnp.where(first, own, other), jnp.where(first, other, own)], axis=2)
+    return jnp.concatenate([jnp.where(first, own, other), jnp.where(first, other, own)], axis=2), weights
 
 
 def stacked(image, start, length, flipped):
     part = lax.dynamic_slice_in_dim(image, start - 1, length + 2, 1)
     if flipped:
-        part = part[:, ::-1]
+        part = lax.optimization_barrier(part[:, ::-1])
     shifts = [part[:, dx : dx + length] for dx in ((2, 1, 0) if flipped else (0, 1, 2))]
     joined = jnp.concatenate(shifts, axis=0)
     joined = jnp.pad(joined, ((0, LANES - joined.shape[0]), (0, 0)))
@@ -439,7 +537,8 @@
 
     wt, w1 = banded_weights(first_weight, conv_weights, rows)
     pair = jnp.stack([normalize(left_pixels), normalize(right_pixels)])
-    band = neighbours(pair, "rows", "strips")[:, rows - 4 : 2 * rows + 4]
+    band, (wt, w1) = neighbours(pair, (wt, w1), "rows", "strips")
+    band = band[:, rows - 4 : 2 * rows + 4]
     left_length, right_length = plan(cols)[0], plan(cols + DISP)[0]
     margin = right_length + 8
     band = jnp.pad(band, ((0, 0), (0, 0), (margin, margin)))
@@ -458,7 +557,8 @@
     if packed:
         grouped = packed[0].reshape(groups, rows, per_group, DISP)
     else:
-        grouped = jnp.swapaxes(cost.astype(jnp.bfloat16).reshape(rows, groups, per_group, DISP), 0, 1)
+        centred = (cost - jnp.mean(cost, axis=2, keepdims=True)).astype(jnp.bfloat16)
+        grouped = jnp.swapaxes(centred.reshape(rows, groups, per_group, DISP), 0, 1)
     columns = lax.all_to_all(grouped, "rows", split_axis=0, concat_axis=0, tiled=True)
     columns = columns.reshape(total_rows, per_group, DISP)
 

time: 84.6 us -> 82 us (0.969)
  Pallas kernels: 51 us -> 47.9 us
  local copies, waits for them, and re-layouts: 5.53 us -> 7.01 us
  waiting for transfers between devices: 4.26 us -> 3.01 us
    pallas_call x1, Pallas kernels: 7.73 us -> 4.99 us  [column_scan(): pl.pallas_call(kernel, out_shape=jax.ShapeDtypeStruct(columns.shape, jnp....]
    pallas_call x1, Pallas kernels: 3.45 us -> 1.06 us  [add_vertical(): pl.pallas_call(add_kernel, out_shape=jax.ShapeDtypeStruct(horizontal.shap...]
    pallas_call x1, Pallas kernels: 7.63 us -> 9.91 us  [cost_volume(): pl.pallas_call(functools.partial(cost_kernel, (rows, cols, total_rows, to...]
    ppermute x1, waiting for transfers between devices: 2.85 us -> 0.81 us  [neighbours(): lax.ppermute(pair, row_axis, [(i + 1, i) for i in range(groups - 1)])]
    unnamed x12 -> x14, local copies, waits for them, and re-layouts: 4.52 us -> 6 us
    ppermute x1, waiting for transfers between devices: 0.01 us -> 0.95 us  [neighbours(): other = lax.ppermute(own, strip_axis, [(i, i ^ 1) for i in range(strips)])]
  transfers between devices with their start and end apart: 6 -> 6, of which waited for: 3 -> 3; matrix products, arithmetic and copies ran while one was open for 2% -> 2% of each run, Pallas kernels for 38% -> 39%
where the time goes in v4:
time: 82 us; the launch traced here: 81.4 us
  Pallas kernels  47.9 us (58%)
  starting transfers between devices  20.8 us (25%)
  local copies, waits for them, and re-layouts  7.01 us (9%)
  waiting for transfers between devices  3.01 us (4%)
  other arithmetic  2.38 us (3%)
    pallas_call x2, Pallas kernels, row_scan(): pl.pallas_call(functools.partial(row_scan_kernel, (rows, cols, flip, batc...  31.1 us
    pallas_call x1, Pallas kernels, cost_volume(): pl.pallas_call(functools.partial(cost_kernel, (rows, cols, total_rows, to...  9.91 us
    all_to_all x1, starting transfers between devices, per_device(): lax.all_to_all(grouped, 'rows', split_axis=0, concat_axis=0, tiled=True)  7.66 us
    all_to_all x1, starting transfers between devices, per_device(): lax.all_to_all(column_sum.reshape(groups, rows, per_group, DISP), 'rows',...  6.9 us
    unnamed x14, local copies, waits for them, and re-layouts  6 us
    pallas_call x1, Pallas kernels, column_scan(): pl.pallas_call(kernel, out_shape=jax.ShapeDtypeStruct(columns.shape, jnp....  4.99 us
    ppermute x1, starting transfers between devices, neighbours(): lax.ppermute(pair, row_axis, [(i, i + 1) for i in range(groups - 1)])  4.84 us
  transfers between devices with their start and end apart: 6, of which 3 were waited for; matrix products, arithmetic and copies ran while one was open for 2% of the time, Pallas kernels for 39%

profile of v4, /device:TPU:0, one launch (start us, length us, event | category | flops | bytes accessed | tf_op | source)
XLA Modules:
  0.0 81.4 jit_solution(13106088892063579821)
XLA Ops:
  0.0 0.7 fusion.4
  0.7 4.8 %collective-permute-start = (bf16[2,4,512]{2,1,0:T(4,128)(2,1)S(1)}, bf16[2,4,512]{2,1,0:T(4,128)(2,1)S(1)}, u32[]{:S(2)}, u32[]{:S(2)}) collective-permute-start(bf16[2,4,512]{2,1,0:T(4,128)(2,1)S(1)} %pad_maximum_fusion.3), channel_id=1, source_target_pairs={{0,2},{2,4},{4,6},{6,8},{8,10},{10,12},{12,14},{14,16},{16,18},{18... | collective-permute-start | bytes 24584 | tf_op jit(solution)/shard_map/ppermute | solution.py:513
  5.6 1.3 %collective-permute-start.1 = (bf16[2,4,512]{2,1,0:T(4,128)(2,1)S(1)}, bf16[2,4,512]{2,1,0:T(4,128)(2,1)S(1)}, u32[]{:S(2)}, u32[]{:S(2)}) collective-permute-start(bf16[2,4,512]{2,1,0:T(4,128)(2,1)S(1)} %pad_maximum_fusion.3), channel_id=1, source_target_pairs={{2,0},{4,2},{6,4},{8,6},{10,8},{12,10},{14,12},{16,14},{18,16},{20... | collective-permute-start | bytes 24584 | tf_op jit(solution)/shard_map/ppermute | solution.py:514
  6.9 0.7 fusion.6
  7.6 0.7 convert_bitcast_fusion
  8.3 0.1 tile.10.first_ref
  8.4 0.0 copy-start
  8.4 1.0 %copy-done = bf16[3,64,64,3,3]{2,1,4,3,0:T(8,128)(2,1)S(1)} copy-done((bf16[3,64,64,3,3]{2,1,4,3,0:T(8,128)(2,1)S(1)}, bf16[3,64,64,3,3]{2,1,4,3,0:T(8,128)(2,1)}, u32[]{:S(2)}) %copy-start) | copy-done | bytes 221208
  9.4 0.9 %shard_map.55 = (bf16[3,3,384,256]{3,2,1,0:T(8,128)(2,1)S(1)}, bf16[128,640]{1,0:T(8,128)(2,1)S(1)}) custom-call(bf16[3,3,3,64,64]{4,3,2,1,0:T(8,128)(2,1)S(1)} %bitcast.26, f32[9,640]{1,0:T(8,128)S(1)} %tile.10.first_ref), custom_call_target="tpu_custom_call" | custom-call | flops 10000000 | bytes 2500000 | tf_op jit(solution)/shard_map/pallas_call | solution.py:498
  10.3 0.0 collective-permute-done
  10.3 0.8 collective-permute-done.1
  11.2 0.1 collective-permute-start.2
  11.2 0.1 pad_add_fusion.where_ref.place_ref
  11.3 0.1 copy.14.mask_ref
  11.5 0.9 %collective-permute-done.2 = bf16[2,12,512]{2,1,0:T(8,128)(2,1)S(1)} collective-permute-done((bf16[2,12,512]{2,1,0:T(8,128)(2,1)S(1)}, bf16[2,12,512]{2,1,0:T(8,128)(2,1)S(1)}, u32[]{:S(2)}, u32[]{:S(2)}) %collective-permute-start.2) | collective-permute-done | bytes 24608 | tf_op jit(solution)/shard_map/ppermute | solution.py:517
  12.5 0.1 fusion.3
  12.6 0.1 dynamic-slice_bitcast_fusion
  12.7 0.5 reverse
  13.2 0.1 slice.40
  13.2 0.1 fusion.8
  13.4 0.2 copy.13
  13.6 0.1 dynamic-slice_bitcast_fusion.1
  13.7 0.1 fusion.9
  13.8 0.1 copy.12
  14.0 9.9 %shard_map.56 = (f32[4,512,128]{2,1,0:T(8,128)S(1)}, bf16[16,128,128]{2,1,0:T(8,128)(2,1)}) custom-call(s32[3]{0:T(128)S(1)} %pad_add_fusion.where_ref.place_ref, bf16[560,128]{1,0:T(8,128)(2,1)S(1)} %pad_bitcast_fusion.1.left_ref, bf16[688,128]{1,0:T(8,128)(2,1)S(1)} %pad_bitcast_fusion.right_ref, bf16[512,256]{1,0:T(8,128)(2,1)S(1)} %copy.14.mask_ref, ...), custom_call_target="tpu_custom_call" | custom-call | flops 8000000000 | bytes 6000000 | tf_op jit(solution)/shard_map/pallas_call | solution.py:141
  23.9 0.0 copy-start.1
  23.9 1.0 %copy-done.1 = f32[4,512,128]{2,1,0:T(8,128)} copy-done((f32[4,512,128]{2,1,0:T(8,128)}, f32[4,512,128]{2,1,0:T(8,128)S(1)}, u32[]{:S(2)}) %copy-start.1) | copy-done | bytes 1048600
  24.8 7.7 %all-to-all-start = ((bf16[16,4,32,128]{3,2,1,0:T(8,128)(2,1)}), bf16[16,4,32,128]{3,2,1,0:T(8,128)(2,1)S(1)}, u32[]{:S(2)}, u32[]{:S(2)}) async-start(bf16[16,4,32,128]{3,2,1,0:T(8,128)(2,1)} %bitcast.13), calls=%async_computation | async-start | bytes 1048576 | tf_op jit(solution)/shard_map/all_to_all | solution.py:562
  32.5 0.0 copy-start.2
  32.5 1.2 %copy-done.2 = f32[4,512,128]{2,1,0:T(8,128)S(1)} copy-done((f32[4,512,128]{2,1,0:T(8,128)S(1)}, f32[4,512,128]{2,1,0:T(8,128)}, u32[]{:S(2)}) %copy-start.2) | copy-done | bytes 1048600
  33.8 15.2 %shard_map.57 = (f32[4,512,128]{2,1,0:T(8,128)S(1)}, f32[16,8,128]{2,1,0:T(8,128)S(1)}) custom-call(s32[3]{0:T(128)S(1)} %pad_add_fusion.where_ref.place_ref, f32[4,512,128]{2,1,0:T(8,128)S(1)} %copy-done.2, f32[16,8,128]{2,1,0:T(8,128)S(1)} %broadcast_in_dim.7.state_ref), custom_call_target="tpu_custom_call" | custom-call | flops 2000000000 | bytes 30000000 | tf_op jit(solution)/shard_map/pallas_call | solution.py:274
  49.0 0.0 copy-start.4
  49.0 1.0 %copy-done.4 = f32[4,512,128]{2,1,0:T(8,128)} copy-done((f32[4,512,128]{2,1,0:T(8,128)}, f32[4,512,128]{2,1,0:T(8,128)S(1)}, u32[]{:S(2)}) %copy-start.4) | copy-done | bytes 1048600
  50.0 0.0 copy-start.3
  50.0 0.0 all-to-all-done
  50.0 5.0 %shard_map.59 = bf16[64,32,128]{2,1,0:T(8,128)(2,1)} custom-call(bf16[64,32,128]{2,1,0:T(8,128)(2,1)S(1)} %bitcast.25), custom_call_target="tpu_custom_call" | custom-call | flops 200000000 | bytes 2000000 | tf_op jit(solution)/shard_map/pallas_call | solution.py:435
  55.0 6.9 %all-to-all-start.1 = ((bf16[16,4,32,128]{3,2,1,0:T(8,128)(2,1)}), bf16[16,4,32,128]{3,2,1,0:T(8,128)(2,1)S(1)}, u32[]{:S(2)}, u32[]{:S(2)}) async-start(bf16[16,4,32,128]{3,2,1,0:T(8,128)(2,1)} %bitcast.15), calls=%async_computation.1 | async-start | bytes 1048576 | tf_op jit(solution)/shard_map/all_to_all | solution.py:570
  61.9 0.1 collective-permute-start.3
  62.0 1.2 %collective-permute-done.3.state_ref = f32[16,8,128]{2,1,0:T(8,128)S(1)} collective-permute-done((f32[16,8,128]{2,1,0:T(8,128)S(1)}, f32[16,8,128]{2,1,0:T(8,128)S(1)}, u32[]{:S(2)}, u32[]{:S(2)}) %collective-permute-start.3) | collective-permute-done | bytes 65568 | tf_op jit(solution)/shard_map/ppermute | solution.py:569
  63.2 0.0 copy-done.3
  63.2 0.0 copy-start.5
  63.2 1.2 %copy-done.5 = f32[4,512,128]{2,1,0:T(8,128)S(1)} copy-done((f32[4,512,128]{2,1,0:T(8,128)S(1)}, f32[4,512,128]{2,1,0:T(8,128)}, u32[]{:S(2)}) %copy-start.5) | copy-done | bytes 1048600
  64.4 15.9 %shard_map.58 = (f32[4,512,128]{2,1,0:T(8,128)S(1)}, f32[16,8,128]{2,1,0:T(8,128)}) custom-call(s32[3]{0:T(128)S(1)} %pad_add_fusion.where_ref.place_ref, f32[4,512,128]{2,1,0:T(8,128)S(1)} %copy-done.3, f32[16,8,128]{2,1,0:T(8,128)S(1)} %collective-permute-done.3.state_ref, f32[4,512,128]{2,1,0:T(8,128)S(1)} %copy-done.5), custom_call_target="tpu_custom_call" | custom-call | flops 2000000000 | bytes 30000000 | tf_op jit(solution)/shard_map/pallas_call | solution.py:274
  80.3 0.0 all-to-all-done.1.down_ref
  80.3 1.1 %shard_map.60 = f32[4,512,128]{2,1,0:T(8,128)} custom-call(f32[4,512,128]{2,1,0:T(8,128)S(1)} %get-tuple-element.29.across_ref, bf16[16,4,32,128]{3,2,1,0:T(8,128)(2,1)S(1)} %all-to-all-done.1.down_ref), custom_call_target="tpu_custom_call" | custom-call | flops 300000 | bytes 2600000 | tf_op jit(solution)/shard_map/pallas_call | solution.py:457
  (12 shorter events, 0.2 us)
Async XLA Ops:
  0.7 9.6 %collective-permute-start = (bf16[2,4,512]{2,1,0:T(4,128)(2,1)S(1)}, bf16[2,4,512]{2,1,0:T(4,128)(2,1)S(1)}, u32[]{:S(2)}, u32[]{:S(2)}) collective-permute-start(bf16[2,4,512]{2,1,0:T(4,128)(2,1)S(1)} %pad_maximum_fusion.3), channel_id=1, source_target_pairs={{0,2},{2,4},{4,6},{6,8},{8,10},{10,12},{12,14},{14,16},{16,18},{18... | collective-permute-start | bytes 24584 | tf_op jit(solution)/shard_map/ppermute | solution.py:513
  5.6 5.5 %collective-permute-start.1 = (bf16[2,4,512]{2,1,0:T(4,128)(2,1)S(1)}, bf16[2,4,512]{2,1,0:T(4,128)(2,1)S(1)}, u32[]{:S(2)}, u32[]{:S(2)}) collective-permute-start(bf16[2,4,512]{2,1,0:T(4,128)(2,1)S(1)} %pad_maximum_fusion.3), channel_id=1, source_target_pairs={{2,0},{4,2},{6,4},{8,6},{10,8},{12,10},{14,12},{16,14},{18,16},{20... | collective-permute-start | bytes 24584 | tf_op jit(solution)/shard_map/ppermute | solution.py:514
  8.4 1.0 %copy-start = (bf16[3,64,64,3,3]{2,1,4,3,0:T(8,128)(2,1)S(1)}, bf16[3,64,64,3,3]{2,1,4,3,0:T(8,128)(2,1)}, u32[]{:S(2)}) copy-start(bf16[3,64,64,3,3]{2,1,4,3,0:T(8,128)(2,1)} %param.9) | copy-start | bytes 663556
  11.2 1.3 %collective-permute-start.2 = (bf16[2,12,512]{2,1,0:T(8,128)(2,1)S(1)}, bf16[2,12,512]{2,1,0:T(8,128)(2,1)S(1)}, u32[]{:S(2)}, u32[]{:S(2)}) collective-permute-start(bf16[2,12,512]{2,1,0:T(8,128)(2,1)S(1)} %pad_maximum_fusion.2), channel_id=1, source_target_pairs={{0,1},{1,0},{2,3},{3,2},{4,5},{5,4},{6,7},{7,6},{8,9},{9,8},{10,11... | collective-permute-start | bytes 73736 | tf_op jit(solution)/shard_map/ppermute | solution.py:517
  23.9 1.0 %copy-start.1 = (f32[4,512,128]{2,1,0:T(8,128)}, f32[4,512,128]{2,1,0:T(8,128)S(1)}, u32[]{:S(2)}) copy-start(f32[4,512,128]{2,1,0:T(8,128)S(1)} %get-tuple-element.24.cost_ref) | copy-start | bytes 3145732
  24.8 25.1 %all-to-all-start = ((bf16[16,4,32,128]{3,2,1,0:T(8,128)(2,1)}), bf16[16,4,32,128]{3,2,1,0:T(8,128)(2,1)S(1)}, u32[]{:S(2)}, u32[]{:S(2)}) async-start(bf16[16,4,32,128]{3,2,1,0:T(8,128)(2,1)} %bitcast.13), calls=%async_computation | async-start | bytes 1048576 | tf_op jit(solution)/shard_map/all_to_all | solution.py:562
  32.5 1.2 %copy-start.2 = (f32[4,512,128]{2,1,0:T(8,128)S(1)}, f32[4,512,128]{2,1,0:T(8,128)}, u32[]{:S(2)}) copy-start(f32[4,512,128]{2,1,0:T(8,128)} %copy-done.1) | copy-start | bytes 3145732
  49.0 1.0 %copy-start.4 = (f32[4,512,128]{2,1,0:T(8,128)}, f32[4,512,128]{2,1,0:T(8,128)S(1)}, u32[]{:S(2)}) copy-start(f32[4,512,128]{2,1,0:T(8,128)S(1)} %get-tuple-element.28.rest_0_) | copy-start | bytes 3145732
  50.0 13.2 %copy-start.3 = (f32[4,512,128]{2,1,0:T(8,128)S(1)}, f32[4,512,128]{2,1,0:T(8,128)}, u32[]{:S(2)}) copy-start(f32[4,512,128]{2,1,0:T(8,128)} %copy-done.1) | copy-start | bytes 3145732
  55.0 25.3 %all-to-all-start.1 = ((bf16[16,4,32,128]{3,2,1,0:T(8,128)(2,1)}), bf16[16,4,32,128]{3,2,1,0:T(8,128)(2,1)S(1)}, u32[]{:S(2)}, u32[]{:S(2)}) async-start(bf16[16,4,32,128]{3,2,1,0:T(8,128)(2,1)} %bitcast.15), calls=%async_computation.1 | async-start | bytes 1048576 | tf_op jit(solution)/shard_map/all_to_all | solution.py:570
  61.9 1.3 %collective-permute-start.3 = (f32[16,8,128]{2,1,0:T(8,128)S(1)}, f32[16,8,128]{2,1,0:T(8,128)S(1)}, u32[]{:S(2)}, u32[]{:S(2)}) collective-permute-start(f32[16,8,128]{2,1,0:T(8,128)S(1)} %get-tuple-element.27), channel_id=1, source_target_pairs={{0,1},{1,0},{2,3},{3,2},{4,5},{5,4},{6,7},{7,6},{8,9},{9,8},{10,11... | collective-permute-start | bytes 196616 | tf_op jit(solution)/shard_map/ppermute | solution.py:569
  63.2 1.2 %copy-start.5 = (f32[4,512,128]{2,1,0:T(8,128)S(1)}, f32[4,512,128]{2,1,0:T(8,128)}, u32[]{:S(2)}) copy-start(f32[4,512,128]{2,1,0:T(8,128)} %copy-done.4) | copy-start | bytes 3145732

commit v5 on v4

--- a/solution.py
+++ b/solution.py
@@ -76,13 +76,19 @@
         lax.fori_loop(0, PARTS, convolve, 0)
 
 
+def offsets(costs):
+    even = jnp.full((DISP, DISP), 1.0 / DISP, jnp.bfloat16)
+    return jnp.dot(costs.astype(jnp.bfloat16), even, preferred_element_type=jnp.float32)
+
+
 def packs(per_group):
     return per_group % 16 == 0 and LANES % per_group == 0
 
 
-def cost_kernel(dims, where_ref, left_ref, right_ref, mask_ref, w1_ref, wt_ref, cost_ref, *rest):
+def cost_kernel(dims, where_ref, left_ref, right_ref, mask_ref, w1_ref, wt_ref, out_ref, *rest):
     rows, cols, total_rows, total_cols, per_group = dims
-    payload_ref, bufs = (rest[0], rest[1:]) if len(rest) % 2 else (None, rest)
+    payload_ref, rest = (rest[0], rest[1:]) if packs(per_group) else (None, rest)
+    cost_ref, sems, *bufs = rest
     first_row, first_col = where_ref[0], where_ref[1]
     row_low, row_high = -first_row, total_rows - first_row
     left_bufs, right_bufs = bufs[:4], bufs[4:]
@@ -116,7 +122,7 @@
             skewed = skewed[:, :LANES]
             cost_ref[row, pl.ds(start, LANES), :] = skewed
             if payload_ref is not None:
-                skewed = skewed - jnp.mean(skewed, axis=1, keepdims=True)
+                skewed = skewed - offsets(skewed)
                 for k in range(LANES // per_group):
                     piece = skewed[k * per_group : (k + 1) * per_group].astype(jnp.bfloat16)
                     group = index * (LANES // per_group) + k
@@ -124,10 +130,13 @@
             return carry
 
         lax.fori_loop(0, cols // LANES, block, 0, unroll=BLOCKS)
+        pltpu.make_async_copy(cost_ref.at[row], out_ref.at[row], sems.at[row]).start()
+    for row in range(rows):
+        pltpu.make_async_copy(cost_ref.at[row], out_ref.at[row], sems.at[row]).wait()
 
 
 def cost_volume(left_stack, right_stack, mask, w1, wt, place, rows, cols, total_rows, total_cols, per_group):
-    bufs = []
+    bufs = [pltpu.VMEM((rows, cols, DISP), jnp.float32), pltpu.SemaphoreType.DMA((rows,))]
     for width in (cols, cols + DISP):
         sizes = plan(width)
         for layer in range(4):
@@ -142,18 +151,20 @@
         functools.partial(cost_kernel, (rows, cols, total_rows, total_cols, per_group)),
         out_shape=tuple(shapes),
         in_specs=[pl.BlockSpec(memory_space=pltpu.SMEM)] + [vmem] * 5,
-        out_specs=(vmem,) * len(shapes),
+        out_specs=(pl.BlockSpec(memory_space=pltpu.HBM), vmem)[: len(shapes)],
         scratch_shapes=bufs,
         compiler_params=pltpu.CompilerParams(vmem_limit_bytes=40 << 20),
         cost_estimate=pl.CostEstimate(flops=8_000_000_000, bytes_accessed=6_000_000, transcendentals=0),
     )(place, left_stack, right_stack, mask, w1, wt)
 
 
-def row_scan_kernel(dims, has_sum, place_ref, cost_ref, state_ref, *rest):
+def row_scan_kernel(dims, has_sum, place_ref, cost_hbm, state_ref, *rest):
     rows, cols, flip, batch = dims
     if has_sum:
-        lead_ref, rest = rest[0], rest[1:]
-    out_ref, end_ref, tile_ref, turn_ref, pick_ref, split_a, split_b, even_ref, odd_ref, path_ref, low_ref = rest
+        lead_hbm, out_ref, end_ref, lead_ref, lead_sem, *rest = rest
+    else:
+        out_hbm, end_ref, out_ref, out_sems, *rest = rest
+    cost_ref, cost_sems, tile_ref, turn_ref, pick_ref, split_a, split_b, even_ref, odd_ref, path_ref, low_ref = rest
     width = LANES // rows
     count = cols // width
     forward = place_ref[2] == (1 if flip else 0)
@@ -161,6 +172,29 @@
     sublane = lax.broadcasted_iota(jnp.int32, (8, LANES), 0)
     lane_col = lane % width
 
+    def copy_in(index):
+        part = pl.ds(chunk_start(index), width)
+        return pltpu.make_async_copy(cost_hbm.at[:, part], cost_ref.at[:, part], cost_sems.at[index])
+
+    rounds = count // batch // 2
+    early = max(rounds // 2 * 2 * batch - 1, 0)
+
+    def copy_out(part):
+        length = (early, count - early)[part] * width
+        begin = jnp.where(forward, (0, early * width)[part], ((count - early) * width, 0)[part])
+        cut = pl.ds(pl.multiple_of(begin, width), length)
+        return pltpu.make_async_copy(out_ref.at[:, cut], out_hbm.at[:, cut], out_sems.at[part])
+
+    def chunk_start(index):
+        chunk = jnp.where(forward, index, count - 1 - index)
+        return pl.multiple_of(chunk * width, width)
+
+    for index in range(count):
+        copy_in(index).start()
+    if has_sum:
+        copy_lead = pltpu.make_async_copy(lead_hbm, lead_ref, lead_sem)
+        copy_lead.start()
+
     def build_pick(pair, carry):
         k = lax.broadcasted_iota(jnp.int32, (2 * LANES, 2 * LANES), 0) % LANES
         n = lax.broadcasted_iota(jnp.int32, (2 * LANES, 2 * LANES), 1)
@@ -169,10 +203,6 @@
         return carry
 
     lax.fori_loop(0, width // 2, build_pick, 0)
-
-    def chunk_start(index):
-        chunk = jnp.where(forward, index, count - 1 - index)
-        return pl.multiple_of(chunk * width, width)
 
     def split(index, target):
         start = chunk_start(jnp.minimum(index, count - 1))
@@ -199,11 +229,13 @@
         for v in range(16):
             turn_ref[pl.ds(v, 8, stride=16), :] = path_ref[v] - low
         done = turn_ref[...].T
+        if has_sum:
+            tile = jnp.concatenate([cost_ref[row, pl.ds(start, width), :] for row in range(rows)], axis=0)
+            done = done + 2.0 * offsets(tile)
         for row in range(rows):
             piece = done[row * width : (row + 1) * width]
             if has_sum:
-                offset = jnp.mean(cost_ref[row, pl.ds(start, width), :], axis=1, keepdims=True)
-                piece = piece + (lead_ref[row, pl.ds(start, width), :] + 2.0 * offset)
+                piece = piece + lead_ref[row, pl.ds(start, width), :]
             out_ref[row, pl.ds(start, width), :] = piece
 
     def advance(state, low, slot, step, current):
@@ -243,6 +275,8 @@
 
         return lax.fori_loop(0, batch, one_chunk, state)
 
+    for index in range(2 * batch):
+        copy_in(index).wait()
     for slot in range(batch):
         split(slot, split_a.at[pl.ds(slot * LANES, LANES)])
         split(batch + slot, split_b.at[pl.ds(slot * LANES, LANES)])
@@ -254,32 +288,57 @@
 
     lax.fori_loop(0, width // 8, first, 0)
 
+    for index in range(2 * batch, count):
+        copy_in(index).wait()
+    if has_sum:
+        copy_lead.wait()
+
     def two_batches(index, state):
         state = one_batch(2 * index, state, even_ref, odd_ref, split_b, split_a)
-        return one_batch(2 * index + 1, state, odd_ref, even_ref, split_a, split_b)
+        state = one_batch(2 * index + 1, state, odd_ref, even_ref, split_a, split_b)
+        if not has_sum and early:
+
+            @pl.when(index == rounds // 2 - 1)
+            def _():
+                copy_out(0).start()
+
+        return state
 
     state = tuple(state_ref[v] for v in range(16))
-    state = lax.fori_loop(0, count // batch // 2, two_batches, state)
+    state = lax.fori_loop(0, rounds, two_batches, state)
     emit(count - 1)
+    if not has_sum:
+        copy_out(1).start()
     for v in range(16):
         end_ref[v] = state[v]
+    if not has_sum:
+        for part in range(2 if early else 1):
+            copy_out(1 - part).wait()
 
 
 def row_scan(place, cost, state, lead, flip):
     rows, cols, _ = cost.shape
     width = LANES // rows
-    batch = math.gcd(cols // width // 2, BATCH)
+    count = cols // width
+    batch = math.gcd(count // 2, BATCH)
     vmem = pl.BlockSpec(memory_space=pltpu.VMEM)
-    args = [place, cost, state] + ([] if lead is None else [lead])
+    hbm = pl.BlockSpec(memory_space=pltpu.HBM)
+    has_sum = lead is not None
+    args = [place, cost, state] + ([lead] if has_sum else [])
+    whole = pltpu.VMEM(cost.shape, jnp.float32)
+    moved = [whole, pltpu.SemaphoreType.DMA(() if has_sum else (2,))]
     return pl.pallas_call(
-        functools.partial(row_scan_kernel, (rows, cols, flip, batch), lead is not None),
+        functools.partial(row_scan_kernel, (rows, cols, flip, batch), has_sum),
         out_shape=(
             jax.ShapeDtypeStruct(cost.shape, jnp.float32),
             jax.ShapeDtypeStruct((16, 8, LANES), jnp.float32),
         ),
-        in_specs=[pl.BlockSpec(memory_space=pltpu.SMEM)] + [vmem] * (len(args) - 1),
-        out_specs=(vmem, vmem),
-        scratch_shapes=[
+        in_specs=[pl.BlockSpec(memory_space=pltpu.SMEM), hbm, vmem] + ([hbm] if has_sum else []),
+        out_specs=(vmem if has_sum else hbm, vmem),
+        scratch_shapes=moved
+        + [
+            whole,
+            pltpu.SemaphoreType.DMA((count,)),
             pltpu.VMEM((LANES, LANES), jnp.float32),
             pltpu.VMEM((LANES, LANES), jnp.float32),
             pltpu.VMEM((width // 2, 2 * LANES, 2 * LANES), jnp.bfloat16),
@@ -290,7 +349,7 @@
             pltpu.VMEM((16, 8, LANES), jnp.float32),
             pltpu.VMEM((8, LANES), jnp.float32),
         ],
-        compiler_params=pltpu.CompilerParams(vmem_limit_bytes=20 << 20),
+        compiler_params=pltpu.CompilerParams(vmem_limit_bytes=24 << 20),
         cost_estimate=pl.CostEstimate(flops=2_000_000_000, bytes_accessed=30_000_000, transcendentals=0),
     )(*args)
 
@@ -557,7 +616,7 @@
     if packed:
         grouped = packed[0].reshape(groups, rows, per_group, DISP)
     else:
-        centred = (cost - jnp.mean(cost, axis=2, keepdims=True)).astype(jnp.bfloat16)
+        centred = (cost - offsets(cost.reshape(-1, DISP)).reshape(cost.shape)).astype(jnp.bfloat16)
         grouped = jnp.swapaxes(centred.reshape(rows, groups, per_group, DISP), 0, 1)
     columns = lax.all_to_all(grouped, "rows", split_axis=0, concat_axis=0, tiled=True)
     columns = columns.reshape(total_rows, per_group, DISP)

time: 82 us -> 80.7 us (0.984)
  Pallas kernels: 47.9 us -> 46.6 us
    pallas_call x2, Pallas kernels: 31.1 us -> 29.8 us  [row_scan(): pl.pallas_call(functools.partial(row_scan_kernel, (rows, cols, flip, batc...]
  transfers between devices with their start and end apart: 6 -> 6, of which waited for: 3 -> 3; matrix products, arithmetic and copies ran while one was open for 2% -> 2% of each run, Pallas kernels for 39% -> 38%
where the time goes in v5:
time: 80.7 us; the launch traced here: 80.1 us
  Pallas kernels  46.6 us (58%)
  starting transfers between devices  20.8 us (26%)
  local copies, waits for them, and re-layouts  7 us (9%)
  waiting for transfers between devices  3.01 us (4%)
  other arithmetic  2.38 us (3%)
    pallas_call x2, Pallas kernels, row_scan(): pl.pallas_call(functools.partial(row_scan_kernel, (rows, cols, flip, batc...  29.8 us
    pallas_call x1, Pallas kernels, cost_volume(): pl.pallas_call(functools.partial(cost_kernel, (rows, cols, total_rows, to...  9.83 us
    all_to_all x1, starting transfers between devices, per_device(): lax.all_to_all(grouped, 'rows', split_axis=0, concat_axis=0, tiled=True)  7.66 us
    all_to_all x1, starting transfers between devices, per_device(): lax.all_to_all(column_sum.reshape(groups, rows, per_group, DISP), 'rows',...  6.9 us
    unnamed x14, local copies, waits for them, and re-layouts  5.99 us
    pallas_call x1, Pallas kernels, column_scan(): pl.pallas_call(kernel, out_shape=jax.ShapeDtypeStruct(columns.shape, jnp....  4.99 us
    ppermute x1, starting transfers between devices, neighbours(): lax.ppermute(pair, row_axis, [(i, i + 1) for i in range(groups - 1)])  4.84 us
  transfers between devices with their start and end apart: 6, of which 3 were waited for; matrix products, arithmetic and copies ran while one was open for 2% of the time, Pallas kernels for 38%

profile of v5, /device:TPU:0, one launch (start us, length us, event | category | flops | bytes accessed | tf_op | source)
XLA Modules:
  0.0 80.1 jit_solution(13275579756424758384)
XLA Ops:
  0.0 0.7 fusion.4
  0.7 4.8 %collective-permute-start = (bf16[2,4,512]{2,1,0:T(4,128)(2,1)S(1)}, bf16[2,4,512]{2,1,0:T(4,128)(2,1)S(1)}, u32[]{:S(2)}, u32[]{:S(2)}) collective-permute-start(bf16[2,4,512]{2,1,0:T(4,128)(2,1)S(1)} %pad_maximum_fusion.3), channel_id=1, source_target_pairs={{0,2},{2,4},{4,6},{6,8},{8,10},{10,12},{12,14},{14,16},{16,18},{18... | collective-permute-start | bytes 24584 | tf_op jit(solution)/shard_map/ppermute | solution.py:572
  5.6 1.3 %collective-permute-start.1 = (bf16[2,4,512]{2,1,0:T(4,128)(2,1)S(1)}, bf16[2,4,512]{2,1,0:T(4,128)(2,1)S(1)}, u32[]{:S(2)}, u32[]{:S(2)}) collective-permute-start(bf16[2,4,512]{2,1,0:T(4,128)(2,1)S(1)} %pad_maximum_fusion.3), channel_id=1, source_target_pairs={{2,0},{4,2},{6,4},{8,6},{10,8},{12,10},{14,12},{16,14},{18,16},{20... | collective-permute-start | bytes 24584 | tf_op jit(solution)/shard_map/ppermute | solution.py:573
  6.9 0.7 fusion.6
  7.6 0.7 convert_bitcast_fusion
  8.3 0.1 tile.10.first_ref
  8.4 0.0 copy-start
  8.4 1.0 %copy-done = bf16[3,64,64,3,3]{2,1,4,3,0:T(8,128)(2,1)S(1)} copy-done((bf16[3,64,64,3,3]{2,1,4,3,0:T(8,128)(2,1)S(1)}, bf16[3,64,64,3,3]{2,1,4,3,0:T(8,128)(2,1)}, u32[]{:S(2)}) %copy-start) | copy-done | bytes 221208
  9.4 0.9 %shard_map.55 = (bf16[3,3,384,256]{3,2,1,0:T(8,128)(2,1)S(1)}, bf16[128,640]{1,0:T(8,128)(2,1)S(1)}) custom-call(bf16[3,3,3,64,64]{4,3,2,1,0:T(8,128)(2,1)S(1)} %bitcast.26, f32[9,640]{1,0:T(8,128)S(1)} %tile.10.first_ref), custom_call_target="tpu_custom_call" | custom-call | flops 10000000 | bytes 2500000 | tf_op jit(solution)/shard_map/pallas_call | solution.py:557
  10.3 0.0 collective-permute-done
  10.3 0.8 %collective-permute-done.1 = bf16[2,4,512]{2,1,0:T(4,128)(2,1)S(1)} collective-permute-done((bf16[2,4,512]{2,1,0:T(4,128)(2,1)S(1)}, bf16[2,4,512]{2,1,0:T(4,128)(2,1)S(1)}, u32[]{:S(2)}, u32[]{:S(2)}) %collective-permute-start.1) | collective-permute-done | bytes 8224 | tf_op jit(solution)/shard_map/ppermute | solution.py:573
  11.2 0.1 collective-permute-start.2
  11.2 0.1 pad_add_fusion.where_ref.place_ref
  11.3 0.1 copy.14.mask_ref
  11.5 0.9 %collective-permute-done.2 = bf16[2,12,512]{2,1,0:T(8,128)(2,1)S(1)} collective-permute-done((bf16[2,12,512]{2,1,0:T(8,128)(2,1)S(1)}, bf16[2,12,512]{2,1,0:T(8,128)(2,1)S(1)}, u32[]{:S(2)}, u32[]{:S(2)}) %collective-permute-start.2) | collective-permute-done | bytes 24608 | tf_op jit(solution)/shard_map/ppermute | solution.py:576
  12.5 0.1 fusion.3
  12.6 0.1 dynamic-slice_bitcast_fusion
  12.7 0.5 reverse
  13.2 0.1 slice.40
  13.2 0.1 fusion.8
  13.4 0.2 copy.13
  13.6 0.1 dynamic-slice_bitcast_fusion.1
  13.7 0.1 fusion.9
  13.8 0.1 copy.12
  14.0 9.8 %shard_map.56 = (f32[4,512,128]{2,1,0:T(8,128)S(1)}, bf16[16,128,128]{2,1,0:T(8,128)(2,1)}) custom-call(s32[3]{0:T(128)S(1)} %pad_add_fusion.where_ref.place_ref, bf16[560,128]{1,0:T(8,128)(2,1)S(1)} %pad_bitcast_fusion.1.left_ref, bf16[688,128]{1,0:T(8,128)(2,1)S(1)} %pad_bitcast_fusion.right_ref, bf16[512,256]{1,0:T(8,128)(2,1)S(1)} %copy.14.mask_ref, ...), custom_call_target="tpu_custom_call" | custom-call | flops 8000000000 | bytes 6000000 | tf_op jit(solution)/shard_map/pallas_call | solution.py:150
  23.8 0.0 copy-start.1
  23.8 1.0 %copy-done.1 = f32[4,512,128]{2,1,0:T(8,128)} copy-done((f32[4,512,128]{2,1,0:T(8,128)}, f32[4,512,128]{2,1,0:T(8,128)S(1)}, u32[]{:S(2)}) %copy-start.1) | copy-done | bytes 1048600
  24.8 7.7 %all-to-all-start = ((bf16[16,4,32,128]{3,2,1,0:T(8,128)(2,1)}), bf16[16,4,32,128]{3,2,1,0:T(8,128)(2,1)S(1)}, u32[]{:S(2)}, u32[]{:S(2)}) async-start(bf16[16,4,32,128]{3,2,1,0:T(8,128)(2,1)} %bitcast.13), calls=%async_computation | async-start | bytes 1048576 | tf_op jit(solution)/shard_map/all_to_all | solution.py:621
  32.5 0.0 copy-start.2
  32.5 1.2 %copy-done.2 = f32[4,512,128]{2,1,0:T(8,128)S(1)} copy-done((f32[4,512,128]{2,1,0:T(8,128)S(1)}, f32[4,512,128]{2,1,0:T(8,128)}, u32[]{:S(2)}) %copy-start.2) | copy-done | bytes 1048600
  33.7 16.0 %shard_map.57 = (f32[4,512,128]{2,1,0:T(8,128)S(1)}, f32[16,8,128]{2,1,0:T(8,128)S(1)}) custom-call(s32[3]{0:T(128)S(1)} %pad_add_fusion.where_ref.place_ref, f32[4,512,128]{2,1,0:T(8,128)S(1)} %copy-done.2, f32[16,8,128]{2,1,0:T(8,128)S(1)} %broadcast_in_dim.7.state_ref), custom_call_target="tpu_custom_call" | custom-call | flops 2000000000 | bytes 30000000 | tf_op jit(solution)/shard_map/pallas_call | solution.py:330
  49.7 0.0 copy-start.4
  49.7 1.0 %copy-done.4 = f32[4,512,128]{2,1,0:T(8,128)} copy-done((f32[4,512,128]{2,1,0:T(8,128)}, f32[4,512,128]{2,1,0:T(8,128)S(1)}, u32[]{:S(2)}) %copy-start.4) | copy-done | bytes 1048600
  50.7 0.0 copy-start.3
  50.7 0.0 all-to-all-done
  50.7 5.0 %shard_map.59 = bf16[64,32,128]{2,1,0:T(8,128)(2,1)} custom-call(bf16[64,32,128]{2,1,0:T(8,128)(2,1)S(1)} %bitcast.25), custom_call_target="tpu_custom_call" | custom-call | flops 200000000 | bytes 2000000 | tf_op jit(solution)/shard_map/pallas_call | solution.py:494
  55.7 6.9 %all-to-all-start.1 = ((bf16[16,4,32,128]{3,2,1,0:T(8,128)(2,1)}), bf16[16,4,32,128]{3,2,1,0:T(8,128)(2,1)S(1)}, u32[]{:S(2)}, u32[]{:S(2)}) async-start(bf16[16,4,32,128]{3,2,1,0:T(8,128)(2,1)} %bitcast.15), calls=%async_computation.1 | async-start | bytes 1048576 | tf_op jit(solution)/shard_map/all_to_all | solution.py:629
  62.6 0.1 collective-permute-start.3
  62.6 1.2 %collective-permute-done.3.state_ref = f32[16,8,128]{2,1,0:T(8,128)S(1)} collective-permute-done((f32[16,8,128]{2,1,0:T(8,128)S(1)}, f32[16,8,128]{2,1,0:T(8,128)S(1)}, u32[]{:S(2)}, u32[]{:S(2)}) %collective-permute-start.3) | collective-permute-done | bytes 65568 | tf_op jit(solution)/shard_map/ppermute | solution.py:628
  63.9 0.0 copy-done.3
  63.9 0.0 copy-start.5
  63.9 1.2 %copy-done.5 = f32[4,512,128]{2,1,0:T(8,128)S(1)} copy-done((f32[4,512,128]{2,1,0:T(8,128)S(1)}, f32[4,512,128]{2,1,0:T(8,128)}, u32[]{:S(2)}) %copy-start.5) | copy-done | bytes 1048600
  65.1 13.9 %shard_map.58 = (f32[4,512,128]{2,1,0:T(8,128)S(1)}, f32[16,8,128]{2,1,0:T(8,128)}) custom-call(s32[3]{0:T(128)S(1)} %pad_add_fusion.where_ref.place_ref, f32[4,512,128]{2,1,0:T(8,128)S(1)} %copy-done.3, f32[16,8,128]{2,1,0:T(8,128)S(1)} %collective-permute-done.3.state_ref, f32[4,512,128]{2,1,0:T(8,128)S(1)} %copy-done.5), custom_call_target="tpu_custom_call" | custom-call | flops 2000000000 | bytes 30000000 | tf_op jit(solution)/shard_map/pallas_call | solution.py:330
  79.0 0.0 all-to-all-done.1.down_ref
  79.0 1.1 %shard_map.60 = f32[4,512,128]{2,1,0:T(8,128)} custom-call(f32[4,512,128]{2,1,0:T(8,128)S(1)} %get-tuple-element.29.across_ref, bf16[16,4,32,128]{3,2,1,0:T(8,128)(2,1)S(1)} %all-to-all-done.1.down_ref), custom_call_target="tpu_custom_call" | custom-call | flops 300000 | bytes 2600000 | tf_op jit(solution)/shard_map/pallas_call | solution.py:516
  (12 shorter events, 0.2 us)
Async XLA Ops:
  0.7 9.6 %collective-permute-start = (bf16[2,4,512]{2,1,0:T(4,128)(2,1)S(1)}, bf16[2,4,512]{2,1,0:T(4,128)(2,1)S(1)}, u32[]{:S(2)}, u32[]{:S(2)}) collective-permute-start(bf16[2,4,512]{2,1,0:T(4,128)(2,1)S(1)} %pad_maximum_fusion.3), channel_id=1, source_target_pairs={{0,2},{2,4},{4,6},{6,8},{8,10},{10,12},{12,14},{14,16},{16,18},{18... | collective-permute-start | bytes 24584 | tf_op jit(solution)/shard_map/ppermute | solution.py:572
  5.6 5.5 %collective-permute-start.1 = (bf16[2,4,512]{2,1,0:T(4,128)(2,1)S(1)}, bf16[2,4,512]{2,1,0:T(4,128)(2,1)S(1)}, u32[]{:S(2)}, u32[]{:S(2)}) collective-permute-start(bf16[2,4,512]{2,1,0:T(4,128)(2,1)S(1)} %pad_maximum_fusion.3), channel_id=1, source_target_pairs={{2,0},{4,2},{6,4},{8,6},{10,8},{12,10},{14,12},{16,14},{18,16},{20... | collective-permute-start | bytes 24584 | tf_op jit(solution)/shard_map/ppermute | solution.py:573
  8.4 1.0 %copy-start = (bf16[3,64,64,3,3]{2,1,4,3,0:T(8,128)(2,1)S(1)}, bf16[3,64,64,3,3]{2,1,4,3,0:T(8,128)(2,1)}, u32[]{:S(2)}) copy-start(bf16[3,64,64,3,3]{2,1,4,3,0:T(8,128)(2,1)} %param.9) | copy-start | bytes 663556
  11.2 1.3 %collective-permute-start.2 = (bf16[2,12,512]{2,1,0:T(8,128)(2,1)S(1)}, bf16[2,12,512]{2,1,0:T(8,128)(2,1)S(1)}, u32[]{:S(2)}, u32[]{:S(2)}) collective-permute-start(bf16[2,12,512]{2,1,0:T(8,128)(2,1)S(1)} %pad_maximum_fusion.2), channel_id=1, source_target_pairs={{0,1},{1,0},{2,3},{3,2},{4,5},{5,4},{6,7},{7,6},{8,9},{9,8},{10,11... | collective-permute-start | bytes 73736 | tf_op jit(solution)/shard_map/ppermute | solution.py:576
  23.8 1.0 %copy-start.1 = (f32[4,512,128]{2,1,0:T(8,128)}, f32[4,512,128]{2,1,0:T(8,128)S(1)}, u32[]{:S(2)}) copy-start(f32[4,512,128]{2,1,0:T(8,128)S(1)} %get-tuple-element.24.cost_hbm) | copy-start | bytes 3145732
  24.8 25.9 %all-to-all-start = ((bf16[16,4,32,128]{3,2,1,0:T(8,128)(2,1)}), bf16[16,4,32,128]{3,2,1,0:T(8,128)(2,1)S(1)}, u32[]{:S(2)}, u32[]{:S(2)}) async-start(bf16[16,4,32,128]{3,2,1,0:T(8,128)(2,1)} %bitcast.13), calls=%async_computation | async-start | bytes 1048576 | tf_op jit(solution)/shard_map/all_to_all | solution.py:621
  32.5 1.2 %copy-start.2 = (f32[4,512,128]{2,1,0:T(8,128)S(1)}, f32[4,512,128]{2,1,0:T(8,128)}, u32[]{:S(2)}) copy-start(f32[4,512,128]{2,1,0:T(8,128)} %copy-done.1) | copy-start | bytes 3145732
  49.7 1.0 %copy-start.4 = (f32[4,512,128]{2,1,0:T(8,128)}, f32[4,512,128]{2,1,0:T(8,128)S(1)}, u32[]{:S(2)}) copy-start(f32[4,512,128]{2,1,0:T(8,128)S(1)} %get-tuple-element.28.rest_0_) | copy-start | bytes 3145732
  50.7 13.2 %copy-start.3 = (f32[4,512,128]{2,1,0:T(8,128)S(1)}, f32[4,512,128]{2,1,0:T(8,128)}, u32[]{:S(2)}) copy-start(f32[4,512,128]{2,1,0:T(8,128)} %copy-done.1) | copy-start | bytes 3145732
  55.7 23.4 %all-to-all-start.1 = ((bf16[16,4,32,128]{3,2,1,0:T(8,128)(2,1)}), bf16[16,4,32,128]{3,2,1,0:T(8,128)(2,1)S(1)}, u32[]{:S(2)}, u32[]{:S(2)}) async-start(bf16[16,4,32,128]{3,2,1,0:T(8,128)(2,1)} %bitcast.15), calls=%async_computation.1 | async-start | bytes 1048576 | tf_op jit(solution)/shard_map/all_to_all | solution.py:629
  62.6 1.3 %collective-permute-start.3 = (f32[16,8,128]{2,1,0:T(8,128)S(1)}, f32[16,8,128]{2,1,0:T(8,128)S(1)}, u32[]{:S(2)}, u32[]{:S(2)}) collective-permute-start(f32[16,8,128]{2,1,0:T(8,128)S(1)} %get-tuple-element.27), channel_id=1, source_target_pairs={{0,1},{1,0},{2,3},{3,2},{4,5},{5,4},{6,7},{7,6},{8,9},{9,8},{10,11... | collective-permute-start | bytes 196616 | tf_op jit(solution)/shard_map/ppermute | solution.py:628
  63.9 1.2 %copy-start.5 = (f32[4,512,128]{2,1,0:T(8,128)S(1)}, f32[4,512,128]{2,1,0:T(8,128)}, u32[]{:S(2)}) copy-start(f32[4,512,128]{2,1,0:T(8,128)} %copy-done.4) | copy-start | bytes 3145732

commit v6 on v5

--- a/solution.py
+++ b/solution.py
@@ -17,7 +17,9 @@
 LANES = 128
 BATCH = 2
 PARTS = 1
-BLOCKS = 4
+COST_ROOM = 60_000_000
+SCAN_ROOM = 62_600_000
+ADD_ROOM = 62_450_000
 
 
 def plan(width):
@@ -28,7 +30,7 @@
     return totals[::-1]
 
 
-def feature_stacks(stacks, w1_ref, wt_ref, row_low, row_high):
+def feature_stacks(stacks, w1_ref, wt_ref, weights_of, row_low, row_high):
     def inside(test, base, count, lanes, halo, lane0):
         position = lax.broadcasted_iota(jnp.int32, (count, lanes), 0) + base
         row = (lax.broadcasted_iota(jnp.int32, (count, lanes), 1) + lane0) // CH - halo
@@ -37,13 +39,14 @@
     def first(index, carry):
         for pix_ref, bufs, test, flipped in stacks:
             chunk = bufs[0].shape[0] // PARTS
-            start = pl.multiple_of(index * chunk, 16)
+            start = index * chunk
             value = jnp.dot(pix_ref[pl.ds(start, chunk), :], w1_ref[...], preferred_element_type=jnp.float32)
             keep = inside(test, start - 3 * EDGE, chunk, bufs[0].shape[1], 3, 0)
             bufs[0][pl.ds(start, chunk), :] = jnp.where(keep, jnp.maximum(value, 0.0), 0.0).astype(jnp.bfloat16)
         return carry
 
-    lax.fori_loop(0, PARTS, first, 0)
+    for index in range(PARTS):
+        first(index, 0)
 
     for layer in range(1, 4):
 
@@ -54,7 +57,7 @@
                 out_rows = target.shape[1] // CH
                 chunk = target.shape[0] // PARTS
                 reach = chunk + 2 * EDGE
-                start = pl.multiple_of(index * chunk, 16)
+                start = index * chunk
                 for group in range(0, out_rows, 4):
                     count = min(4, out_rows - group)
                     wide, deep = count * CH, (count + 2) * CH
@@ -73,7 +76,9 @@
                     target[pl.ds(start, chunk), group * CH : group * CH + wide] = value
             return carry
 
-        lax.fori_loop(0, PARTS, convolve, 0)
+        weights_of(layer - 1).wait()
+        for index in range(PARTS):
+            convolve(index, 0)
 
 
 def offsets(costs):
@@ -85,10 +90,16 @@
     return per_group % 16 == 0 and LANES % per_group == 0
 
 
-def cost_kernel(dims, where_ref, left_ref, right_ref, mask_ref, w1_ref, wt_ref, out_ref, *rest):
+def cost_kernel(dims, where_ref, left_ref, right_ref, mask_ref, w1_ref, wt_hbm, out_ref, *rest):
     rows, cols, total_rows, total_cols, per_group = dims
     payload_ref, rest = (rest[0], rest[1:]) if packs(per_group) else (None, rest)
-    cost_ref, sems, *bufs = rest
+    cost_ref, sems, wt_ref, wt_sems, *bufs = rest
+
+    def weights_of(layer):
+        return pltpu.make_async_copy(wt_hbm.at[layer], wt_ref.at[layer], wt_sems.at[layer])
+
+    for layer in range(3):
+        weights_of(layer).start()
     first_row, first_col = where_ref[0], where_ref[1]
     row_low, row_high = -first_row, total_rows - first_row
     left_bufs, right_bufs = bufs[:4], bufs[4:]
@@ -103,7 +114,7 @@
 
     feature_stacks(
         [(left_ref, left_bufs, left_col, False), (right_ref, right_bufs, right_col, True)],
-        w1_ref, wt_ref, row_low, row_high,
+        w1_ref, wt_ref, weights_of, row_low, row_high,
     )
     left, right = left_bufs[3], right_bufs[3]
     for row in range(rows):
@@ -111,25 +122,21 @@
         lane = lax.broadcasted_iota(jnp.int32, (LANES, LANES), 1)
         own = (lane // CH) == row % 2
 
-        def block(index, carry, pair=pair, own=own, row=row):
-            start = pl.multiple_of(index * LANES, LANES)
-            window = pl.multiple_of(cols - LANES - start, LANES)
-            scale = mask_ref[pl.ds(start, LANES), pair : pair + LANES]
-            a = jnp.where(own, left[pl.ds(start, LANES), pair : pair + LANES] * scale, jnp.zeros((), jnp.bfloat16))
-            b = right[pl.ds(window, 2 * LANES), pair : pair + LANES]
+        for index in range(cols // LANES):
+            start = index * LANES
+            window = cols - LANES - start
+            scale = mask_ref[start : start + LANES, pair : pair + LANES]
+            a = jnp.where(own, left[start : start + LANES, pair : pair + LANES] * scale, jnp.zeros((), jnp.bfloat16))
+            b = right[window : window + 2 * LANES, pair : pair + LANES]
             product = lax.dot_general(a, b, (((1,), (1,)), ((), ())), preferred_element_type=jnp.float32)
-            skewed = pltpu.roll(product, LANES + 1, 1, stride=1, stride_axis=0)
-            skewed = skewed[:, :LANES]
-            cost_ref[row, pl.ds(start, LANES), :] = skewed
+            skewed = pltpu.roll(product, LANES + 1, 1, stride=1, stride_axis=0)[:, :LANES]
+            cost_ref[row, start : start + LANES, :] = skewed
             if payload_ref is not None:
                 skewed = skewed - offsets(skewed)
                 for k in range(LANES // per_group):
                     piece = skewed[k * per_group : (k + 1) * per_group].astype(jnp.bfloat16)
                     group = index * (LANES // per_group) + k
                     payload_ref[group, row * per_group : (row + 1) * per_group, :] = piece
-            return carry
-
-        lax.fori_loop(0, cols // LANES, block, 0, unroll=BLOCKS)
         pltpu.make_async_copy(cost_ref.at[row], out_ref.at[row], sems.at[row]).start()
     for row in range(rows):
         pltpu.make_async_copy(cost_ref.at[row], out_ref.at[row], sems.at[row]).wait()
@@ -137,6 +144,7 @@
 
 def cost_volume(left_stack, right_stack, mask, w1, wt, place, rows, cols, total_rows, total_cols, per_group):
     bufs = [pltpu.VMEM((rows, cols, DISP), jnp.float32), pltpu.SemaphoreType.DMA((rows,))]
+    bufs += [pltpu.VMEM(wt.shape, wt.dtype), pltpu.SemaphoreType.DMA((3,))]
     for width in (cols, cols + DISP):
         sizes = plan(width)
         for layer in range(4):
@@ -150,10 +158,10 @@
     return pl.pallas_call(
         functools.partial(cost_kernel, (rows, cols, total_rows, total_cols, per_group)),
         out_shape=tuple(shapes),
-        in_specs=[pl.BlockSpec(memory_space=pltpu.SMEM)] + [vmem] * 5,
+        in_specs=[pl.BlockSpec(memory_space=pltpu.SMEM)] + [vmem] * 4 + [pl.BlockSpec(memory_space=pltpu.HBM)],
         out_specs=(pl.BlockSpec(memory_space=pltpu.HBM), vmem)[: len(shapes)],
         scratch_shapes=bufs,
-        compiler_params=pltpu.CompilerParams(vmem_limit_bytes=40 << 20),
+        compiler_params=pltpu.CompilerParams(vmem_limit_bytes=COST_ROOM),
         cost_estimate=pl.CostEstimate(flops=8_000_000_000, bytes_accessed=6_000_000, transcendentals=0),
     )(place, left_stack, right_stack, mask, w1, wt)
 
@@ -161,10 +169,10 @@
 def row_scan_kernel(dims, has_sum, place_ref, cost_hbm, state_ref, *rest):
     rows, cols, flip, batch = dims
     if has_sum:
-        lead_hbm, out_ref, end_ref, lead_ref, lead_sem, *rest = rest
+        lead_hbm, out_hbm, end_ref, lead_ref, lead_sem, *rest = rest
     else:
-        out_hbm, end_ref, out_ref, out_sems, *rest = rest
-    cost_ref, cost_sems, tile_ref, turn_ref, pick_ref, split_a, split_b, even_ref, odd_ref, path_ref, low_ref = rest
+        out_hbm, end_ref, *rest = rest
+    out_ref, out_sems, cost_ref, cost_sems, tile_ref, turn_ref, pick_ref, split_a, split_b, even_ref, odd_ref, path_ref, low_ref = rest
     width = LANES // rows
     count = cols // width
     forward = place_ref[2] == (1 if flip else 0)
@@ -296,7 +304,7 @@
     def two_batches(index, state):
         state = one_batch(2 * index, state, even_ref, odd_ref, split_b, split_a)
         state = one_batch(2 * index + 1, state, odd_ref, even_ref, split_a, split_b)
-        if not has_sum and early:
+        if early:
 
             @pl.when(index == rounds // 2 - 1)
             def _():
@@ -307,13 +315,11 @@
     state = tuple(state_ref[v] for v in range(16))
     state = lax.fori_loop(0, rounds, two_batches, state)
     emit(count - 1)
-    if not has_sum:
-        copy_out(1).start()
+    copy_out(1).start()
     for v in range(16):
         end_ref[v] = state[v]
-    if not has_sum:
-        for part in range(2 if early else 1):
-            copy_out(1 - part).wait()
+    for part in range(2 if early else 1):
+        copy_out(1 - part).wait()
 
 
 def row_scan(place, cost, state, lead, flip):
@@ -326,7 +332,7 @@
     has_sum = lead is not None
     args = [place, cost, state] + ([lead] if has_sum else [])
     whole = pltpu.VMEM(cost.shape, jnp.float32)
-    moved = [whole, pltpu.SemaphoreType.DMA(() if has_sum else (2,))]
+    moved = [whole, pltpu.SemaphoreType.DMA(())] if has_sum else []
     return pl.pallas_call(
         functools.partial(row_scan_kernel, (rows, cols, flip, batch), has_sum),
         out_shape=(
@@ -334,9 +340,11 @@
             jax.ShapeDtypeStruct((16, 8, LANES), jnp.float32),
         ),
         in_specs=[pl.BlockSpec(memory_space=pltpu.SMEM), hbm, vmem] + ([hbm] if has_sum else []),
-        out_specs=(vmem if has_sum else hbm, vmem),
+        out_specs=(hbm, vmem),
         scratch_shapes=moved
         + [
+            whole,
+            pltpu.SemaphoreType.DMA((2,)),
             whole,
             pltpu.SemaphoreType.DMA((count,)),
             pltpu.VMEM((LANES, LANES), jnp.float32),
@@ -349,7 +357,7 @@
             pltpu.VMEM((16, 8, LANES), jnp.float32),
             pltpu.VMEM((8, LANES), jnp.float32),
         ],
-        compiler_params=pltpu.CompilerParams(vmem_limit_bytes=24 << 20),
+        compiler_params=pltpu.CompilerParams(vmem_limit_bytes=SCAN_ROOM),
         cost_estimate=pl.CostEstimate(flops=2_000_000_000, bytes_accessed=30_000_000, transcendentals=0),
     )(*args)
 
@@ -502,23 +510,45 @@
     )(columns)
 
 
-def add_kernel(across_ref, down_ref, out_ref):
+def add_kernel(across_hbm, down_hbm, out_hbm, across_ref, down_ref, sems):
     rows, cols, _ = across_ref.shape
+
+    def moves(row):
+        return (
+            pltpu.make_async_copy(across_hbm.at[row], across_ref.at[row], sems.at[0, row]),
+            pltpu.make_async_copy(down_hbm.at[:, row], down_ref.at[row], sems.at[1, row]),
+            pltpu.make_async_copy(across_ref.at[row], out_hbm.at[row], sems.at[2, row]),
+        )
+
     for row in range(rows):
-        out_ref[row] = across_ref[row] + down_ref[:, row].reshape(cols, DISP).astype(jnp.float32)
+        moves(row)[0].start()
+        moves(row)[1].start()
+    for row in range(rows):
+        moves(row)[0].wait()
+        moves(row)[1].wait()
+        across_ref[row] += down_ref[row].reshape(cols, DISP).astype(jnp.float32)
+        moves(row)[2].start()
+    for row in range(rows):
+        moves(row)[2].wait()
 
 
 def add_vertical(horizontal, vertical):
     rows, cols, _ = horizontal.shape
-    if not packs(vertical.shape[2]):
+    groups, _, per_group, _ = vertical.shape
+    if not packs(per_group):
         return horizontal + jnp.swapaxes(vertical, 0, 1).reshape(rows, cols, DISP).astype(jnp.float32)
-    vmem = pl.BlockSpec(memory_space=pltpu.VMEM)
+    hbm = pl.BlockSpec(memory_space=pltpu.HBM)
     return pl.pallas_call(
         add_kernel,
         out_shape=jax.ShapeDtypeStruct(horizontal.shape, jnp.float32),
-        in_specs=[vmem, vmem],
-        out_specs=vmem,
-        compiler_params=pltpu.CompilerParams(vmem_limit_bytes=8 << 20),
+        in_specs=[hbm, hbm],
+        out_specs=hbm,
+        scratch_shapes=[
+            pltpu.VMEM(horizontal.shape, jnp.float32),
+            pltpu.VMEM((rows, groups, per_group, DISP), jnp.bfloat16),
+            pltpu.SemaphoreType.DMA((3, rows)),
+        ],
+        compiler_params=pltpu.CompilerParams(vmem_limit_bytes=ADD_ROOM),
         cost_estimate=pl.CostEstimate(flops=300_000, bytes_accessed=2_600_000, transcendentals=0),
     )(horizontal, vertical)
 

time: 80.7 us -> 87.4 us (1.083)
  Pallas kernels: 46.6 us -> 52.3 us
  waiting for transfers between devices: 3.01 us -> 1.25 us
  local copies, waits for them, and re-layouts: 7 us -> 8.58 us
    pallas_call x2, Pallas kernels: 29.8 us -> 33 us  [row_scan(): pl.pallas_call(functools.partial(row_scan_kernel, (rows, cols, flip, batc...]
    pallas_call x1, Pallas kernels: 9.83 us -> 11.3 us  [cost_volume(): pl.pallas_call(functools.partial(cost_kernel, (rows, cols, total_rows, to...]
    transpose x2, local copies, waits for them, and re-layouts: 0.07 us -> 1.39 us  [stacked(): return joined.T]
    pallas_call x1, Pallas kernels: 1.06 us -> 2.19 us  [add_vertical(): pl.pallas_call(add_kernel, out_shape=jax.ShapeDtypeStruct(horizontal.shap...]
    unnamed x14, local copies, waits for them, and re-layouts: 5.99 us -> 4.91 us
    ppermute x1, waiting for transfers between devices: 0.95 us -> 0.01 us  [neighbours(): other = lax.ppermute(own, strip_axis, [(i, i ^ 1) for i in range(strips)])]
  transfers between devices with their start and end apart: 6 -> 6, of which waited for: 3 -> 1; matrix products, arithmetic and copies ran while one was open for 2% -> 4% of each run, Pallas kernels for 38% -> 39%
where the time goes in v6:
time: 87.4 us; the launch traced here: 86.7 us
  Pallas kernels  52.3 us (60%)
  starting transfers between devices  21.2 us (24%)
  local copies, waits for them, and re-layouts  8.58 us (10%)
  other arithmetic  2.97 us (3%)
  waiting for transfers between devices  1.25 us (1%)
    pallas_call x2, Pallas kernels, row_scan(): pl.pallas_call(functools.partial(row_scan_kernel, (rows, cols, flip, batc...  33 us
    pallas_call x1, Pallas kernels, cost_volume(): pl.pallas_call(functools.partial(cost_kernel, (rows, cols, total_rows, to...  11.3 us
    all_to_all x1, starting transfers between devices, per_device(): lax.all_to_all(grouped, 'rows', split_axis=0, concat_axis=0, tiled=True)  8.04 us
    all_to_all x1, starting transfers between devices, per_device(): lax.all_to_all(column_sum.reshape(groups, rows, per_group, DISP), 'rows',...  6.91 us
    pallas_call x1, Pallas kernels, column_scan(): pl.pallas_call(kernel, out_shape=jax.ShapeDtypeStruct(columns.shape, jnp....  4.98 us
    unnamed x14, local copies, waits for them, and re-layouts  4.91 us
    ppermute x1, starting transfers between devices, neighbours(): lax.ppermute(pair, row_axis, [(i, i + 1) for i in range(groups - 1)])  4.84 us
    pallas_call x1, Pallas kernels, add_vertical(): pl.pallas_call(add_kernel, out_shape=jax.ShapeDtypeStruct(horizontal.shap...  2.19 us
  transfers between devices with their start and end apart: 6, of which 1 were waited for; matrix products, arithmetic and copies ran while one was open for 4% of the time, Pallas kernels for 39%

profile of v6, /device:TPU:0, one launch (start us, length us, event | category | flops | bytes accessed | tf_op | source)
XLA Modules:
  0.0 86.7 jit_solution(13778591232119930114)
XLA Ops:
  0.0 0.7 fusion.4
  0.7 4.8 %collective-permute-start = (bf16[2,4,512]{2,1,0:T(4,128)(2,1)S(1)}, bf16[2,4,512]{2,1,0:T(4,128)(2,1)S(1)}, u32[]{:S(2)}, u32[]{:S(2)}) collective-permute-start(bf16[2,4,512]{2,1,0:T(4,128)(2,1)S(1)} %pad_maximum_fusion.3), channel_id=1, source_target_pairs={{0,2},{2,4},{4,6},{6,8},{8,10},{10,12},{12,14},{14,16},{16,18},{18... | collective-permute-start | bytes 24584 | tf_op jit(solution)/shard_map/ppermute | solution.py:602
  5.6 1.3 %collective-permute-start.1 = (bf16[2,4,512]{2,1,0:T(4,128)(2,1)S(1)}, bf16[2,4,512]{2,1,0:T(4,128)(2,1)S(1)}, u32[]{:S(2)}, u32[]{:S(2)}) collective-permute-start(bf16[2,4,512]{2,1,0:T(4,128)(2,1)S(1)} %pad_maximum_fusion.3), channel_id=1, source_target_pairs={{2,0},{4,2},{6,4},{8,6},{10,8},{12,10},{14,12},{16,14},{18,16},{20... | collective-permute-start | bytes 24584 | tf_op jit(solution)/shard_map/ppermute | solution.py:603
  6.9 0.7 fusion.6
  7.6 0.7 convert_bitcast_fusion
  8.3 0.1 tile.10.first_ref
  8.4 0.0 copy-start
  8.4 1.0 %copy-done = bf16[3,64,64,3,3]{2,1,4,3,0:T(8,128)(2,1)S(1)} copy-done((bf16[3,64,64,3,3]{2,1,4,3,0:T(8,128)(2,1)S(1)}, bf16[3,64,64,3,3]{2,1,4,3,0:T(8,128)(2,1)}, u32[]{:S(2)}) %copy-start) | copy-done | bytes 221208
  9.4 0.9 %shard_map.55 = (bf16[3,3,384,256]{3,2,1,0:T(8,128)(2,1)S(1)}, bf16[128,640]{1,0:T(8,128)(2,1)S(1)}) custom-call(bf16[3,3,3,64,64]{4,3,2,1,0:T(8,128)(2,1)S(1)} %bitcast.26, f32[9,640]{1,0:T(8,128)S(1)} %tile.10.first_ref), custom_call_target="tpu_custom_call" | custom-call | flops 10000000 | bytes 2500000 | tf_op jit(solution)/shard_map/pallas_call | solution.py:587
  10.3 0.0 copy-start.1
  10.3 1.2 %copy-done.1 = bf16[3,3,384,256]{3,2,1,0:T(8,128)(2,1)} copy-done((bf16[3,3,384,256]{3,2,1,0:T(8,128)(2,1)}, bf16[3,3,384,256]{3,2,1,0:T(8,128)(2,1)S(1)}, u32[]{:S(2)}) %copy-start.1) | copy-done | bytes 1769496
  11.6 0.0 copy-start.2
  11.6 0.7 copy-done.2
  12.2 0.0 collective-permute-done
  12.2 0.0 collective-permute-done.1
  12.2 0.1 collective-permute-start.2
  12.3 0.7 pad_add_fusion.where_ref.place_ref
  13.0 0.8 copy.14.mask_ref
  13.9 0.0 collective-permute-done.2
  13.9 0.1 fusion.3
  14.0 0.1 dynamic-slice_bitcast_fusion
  14.1 0.5 reverse
  14.6 0.1 slice.40
  14.7 0.1 fusion.8
  14.8 0.2 copy.13
  15.0 0.7 pad_bitcast_fusion.right_ref
  15.7 0.1 dynamic-slice_bitcast_fusion.1
  15.8 0.1 fusion.9
  15.9 0.1 copy.12
  16.0 0.7 pad_bitcast_fusion.1.left_ref
  16.7 11.3 %shard_map.56 = (f32[4,512,128]{2,1,0:T(8,128)}, bf16[16,128,128]{2,1,0:T(8,128)(2,1)}) custom-call(s32[3]{0:T(128)} %pad_add_fusion.where_ref.place_ref, bf16[560,128]{1,0:T(8,128)(2,1)} %pad_bitcast_fusion.1.left_ref, bf16[688,128]{1,0:T(8,128)(2,1)} %pad_bitcast_fusion.right_ref, bf16[512,256]{1,0:T(8,128)(2,1)} %copy.14.mask_ref, ...), custom_call_target="tpu_custom_call" | custom-call | flops 8000000000 | bytes 6000000 | tf_op jit(solution)/shard_map/pallas_call | solution.py:158
  28.0 8.0 %all-to-all-start = ((bf16[16,4,32,128]{3,2,1,0:T(8,128)(2,1)}), bf16[16,4,32,128]{3,2,1,0:T(8,128)(2,1)S(1)}, u32[]{:S(2)}, u32[]{:S(2)}) async-start(bf16[16,4,32,128]{3,2,1,0:T(8,128)(2,1)} %bitcast.28), calls=%async_computation | async-start | bytes 1048576 | tf_op jit(solution)/shard_map/all_to_all | solution.py:651
  36.0 0.6 broadcast_in_dim.7.state_ref
  36.7 17.6 %shard_map.57 = (f32[4,512,128]{2,1,0:T(8,128)}, f32[16,8,128]{2,1,0:T(8,128)}) custom-call(s32[3]{0:T(128)} %pad_add_fusion.where_ref.place_ref, f32[4,512,128]{2,1,0:T(8,128)} %get-tuple-element.24.cost_hbm, f32[16,8,128]{2,1,0:T(8,128)} %broadcast_in_dim.7.state_ref), custom_call_target="tpu_custom_call" | custom-call | flops 2000000000 | bytes 30000000 | tf_op jit(solution)/shard_map/pallas_call | solution.py:336
  54.2 0.0 copy-start.4
  54.3 0.0 all-to-all-done
  54.3 5.0 %shard_map.59 = bf16[64,32,128]{2,1,0:T(8,128)(2,1)} custom-call(bf16[64,32,128]{2,1,0:T(8,128)(2,1)S(1)} %bitcast.25), custom_call_target="tpu_custom_call" | custom-call | flops 200000000 | bytes 2000000 | tf_op jit(solution)/shard_map/pallas_call | solution.py:502
  59.2 6.9 %all-to-all-start.1 = ((bf16[16,4,32,128]{3,2,1,0:T(8,128)(2,1)}), bf16[16,4,32,128]{3,2,1,0:T(8,128)(2,1)S(1)}, u32[]{:S(2)}, u32[]{:S(2)}) async-start(bf16[16,4,32,128]{3,2,1,0:T(8,128)(2,1)} %bitcast.15), calls=%async_computation.1 | async-start | bytes 1048576 | tf_op jit(solution)/shard_map/all_to_all | solution.py:659
  66.2 0.0 copy-done.4
  66.2 0.1 collective-permute-start.3
  66.3 1.2 %collective-permute-done.3.state_ref = f32[16,8,128]{2,1,0:T(8,128)S(1)} collective-permute-done((f32[16,8,128]{2,1,0:T(8,128)S(1)}, f32[16,8,128]{2,1,0:T(8,128)S(1)}, u32[]{:S(2)}, u32[]{:S(2)}) %collective-permute-start.3) | collective-permute-done | bytes 65568 | tf_op jit(solution)/shard_map/ppermute | solution.py:658
  67.5 0.0 copy-start.5
  67.5 0.6 copy-done.5
  68.1 15.4 %shard_map.58 = (f32[4,512,128]{2,1,0:T(8,128)}, f32[16,8,128]{2,1,0:T(8,128)}) custom-call(s32[3]{0:T(128)} %pad_add_fusion.where_ref.place_ref, f32[4,512,128]{2,1,0:T(8,128)} %get-tuple-element.24.cost_hbm, f32[16,8,128]{2,1,0:T(8,128)} %copy-done.5, f32[4,512,128]{2,1,0:T(8,128)} %get-tuple-element.28.rest_0_), custom_call_target="tpu_custom_call" | custom-call | flops 2000000000 | bytes 30000000 | tf_op jit(solution)/shard_map/pallas_call | solution.py:336
  83.5 0.0 all-to-all-done.1.down_hbm
  83.5 0.0 copy-start.3
  83.5 0.8 copy-done.3
  84.3 2.2 %shard_map.60 = f32[4,512,128]{2,1,0:T(8,128)} custom-call(f32[4,512,128]{2,1,0:T(8,128)} %get-tuple-element.29.across_hbm, bf16[16,4,32,128]{3,2,1,0:T(8,128)(2,1)} %copy-done.3), custom_call_target="tpu_custom_call" | custom-call | flops 300000 | bytes 2600000 | tf_op jit(solution)/shard_map/pallas_call | solution.py:541
  (9 shorter events, 0.2 us)
Async XLA Ops:
  0.7 11.5 %collective-permute-start = (bf16[2,4,512]{2,1,0:T(4,128)(2,1)S(1)}, bf16[2,4,512]{2,1,0:T(4,128)(2,1)S(1)}, u32[]{:S(2)}, u32[]{:S(2)}) collective-permute-start(bf16[2,4,512]{2,1,0:T(4,128)(2,1)S(1)} %pad_maximum_fusion.3), channel_id=1, source_target_pairs={{0,2},{2,4},{4,6},{6,8},{8,10},{10,12},{12,14},{14,16},{16,18},{18... | collective-permute-start | bytes 24584 | tf_op jit(solution)/shard_map/ppermute | solution.py:602
  5.6 6.6 %collective-permute-start.1 = (bf16[2,4,512]{2,1,0:T(4,128)(2,1)S(1)}, bf16[2,4,512]{2,1,0:T(4,128)(2,1)S(1)}, u32[]{:S(2)}, u32[]{:S(2)}) collective-permute-start(bf16[2,4,512]{2,1,0:T(4,128)(2,1)S(1)} %pad_maximum_fusion.3), channel_id=1, source_target_pairs={{2,0},{4,2},{6,4},{8,6},{10,8},{12,10},{14,12},{16,14},{18,16},{20... | collective-permute-start | bytes 24584 | tf_op jit(solution)/shard_map/ppermute | solution.py:603
  8.4 1.0 %copy-start = (bf16[3,64,64,3,3]{2,1,4,3,0:T(8,128)(2,1)S(1)}, bf16[3,64,64,3,3]{2,1,4,3,0:T(8,128)(2,1)}, u32[]{:S(2)}) copy-start(bf16[3,64,64,3,3]{2,1,4,3,0:T(8,128)(2,1)} %param.9) | copy-start | bytes 663556
  10.3 1.2 %copy-start.1 = (bf16[3,3,384,256]{3,2,1,0:T(8,128)(2,1)}, bf16[3,3,384,256]{3,2,1,0:T(8,128)(2,1)S(1)}, u32[]{:S(2)}) copy-start(bf16[3,3,384,256]{3,2,1,0:T(8,128)(2,1)S(1)} %get-tuple-element.23.wt_hbm) | copy-start | bytes 5308420
  11.6 0.7 copy-start.2
  12.2 1.6 %collective-permute-start.2 = (bf16[2,12,512]{2,1,0:T(8,128)(2,1)S(1)}, bf16[2,12,512]{2,1,0:T(8,128)(2,1)S(1)}, u32[]{:S(2)}, u32[]{:S(2)}) collective-permute-start(bf16[2,12,512]{2,1,0:T(8,128)(2,1)S(1)} %pad_maximum_fusion.2), channel_id=1, source_target_pairs={{0,1},{1,0},{2,3},{3,2},{4,5},{5,4},{6,7},{7,6},{8,9},{9,8},{10,11... | collective-permute-start | bytes 73736 | tf_op jit(solution)/shard_map/ppermute | solution.py:606
  28.0 26.3 %all-to-all-start = ((bf16[16,4,32,128]{3,2,1,0:T(8,128)(2,1)}), bf16[16,4,32,128]{3,2,1,0:T(8,128)(2,1)S(1)}, u32[]{:S(2)}, u32[]{:S(2)}) async-start(bf16[16,4,32,128]{3,2,1,0:T(8,128)(2,1)} %bitcast.28), calls=%async_computation | async-start | bytes 1048576 | tf_op jit(solution)/shard_map/all_to_all | solution.py:651
  54.2 11.9 %copy-start.4 = (f32[16,8,128]{2,1,0:T(8,128)S(1)}, f32[16,8,128]{2,1,0:T(8,128)}, u32[]{:S(2)}) copy-start(f32[16,8,128]{2,1,0:T(8,128)} %get-tuple-element.27) | copy-start | bytes 196612
  59.2 24.3 %all-to-all-start.1 = ((bf16[16,4,32,128]{3,2,1,0:T(8,128)(2,1)}), bf16[16,4,32,128]{3,2,1,0:T(8,128)(2,1)S(1)}, u32[]{:S(2)}, u32[]{:S(2)}) async-start(bf16[16,4,32,128]{3,2,1,0:T(8,128)(2,1)} %bitcast.15), calls=%async_computation.1 | async-start | bytes 1048576 | tf_op jit(solution)/shard_map/all_to_all | solution.py:659
  66.2 1.3 %collective-permute-start.3 = (f32[16,8,128]{2,1,0:T(8,128)S(1)}, f32[16,8,128]{2,1,0:T(8,128)S(1)}, u32[]{:S(2)}, u32[]{:S(2)}) collective-permute-start(f32[16,8,128]{2,1,0:T(8,128)S(1)} %copy-done.4), channel_id=1, source_target_pairs={{0,1},{1,0},{2,3},{3,2},{4,5},{5,4},{6,7},{7,6},{8,9},{9,8},{10,11... | collective-permute-start | bytes 196616 | tf_op jit(solution)/shard_map/ppermute | solution.py:658
  67.5 0.6 copy-start.5
  83.5 0.8 copy-start.3

commit v7 on v5

--- a/solution.py
+++ b/solution.py
@@ -17,7 +17,8 @@
 LANES = 128
 BATCH = 2
 PARTS = 1
-BLOCKS = 4
+SCAN_ROOM = 62_600_000
+SUM_ROOM = 24 << 20
 
 
 def plan(width):
@@ -37,13 +38,14 @@
     def first(index, carry):
         for pix_ref, bufs, test, flipped in stacks:
             chunk = bufs[0].shape[0] // PARTS
-            start = pl.multiple_of(index * chunk, 16)
+            start = index * chunk
             value = jnp.dot(pix_ref[pl.ds(start, chunk), :], w1_ref[...], preferred_element_type=jnp.float32)
             keep = inside(test, start - 3 * EDGE, chunk, bufs[0].shape[1], 3, 0)
             bufs[0][pl.ds(start, chunk), :] = jnp.where(keep, jnp.maximum(value, 0.0), 0.0).astype(jnp.bfloat16)
         return carry
 
-    lax.fori_loop(0, PARTS, first, 0)
+    for index in range(PARTS):
+        first(index, 0)
 
     for layer in range(1, 4):
 
@@ -54,7 +56,7 @@
                 out_rows = target.shape[1] // CH
                 chunk = target.shape[0] // PARTS
                 reach = chunk + 2 * EDGE
-                start = pl.multiple_of(index * chunk, 16)
+                start = index * chunk
                 for group in range(0, out_rows, 4):
                     count = min(4, out_rows - group)
                     wide, deep = count * CH, (count + 2) * CH
@@ -73,22 +75,18 @@
                     target[pl.ds(start, chunk), group * CH : group * CH + wide] = value
             return carry
 
-        lax.fori_loop(0, PARTS, convolve, 0)
-
-
-def offsets(costs):
-    even = jnp.full((DISP, DISP), 1.0 / DISP, jnp.bfloat16)
-    return jnp.dot(costs.astype(jnp.bfloat16), even, preferred_element_type=jnp.float32)
+        for index in range(PARTS):
+            convolve(index, 0)
 
 
 def packs(per_group):
     return per_group % 16 == 0 and LANES % per_group == 0
 
 
-def cost_kernel(dims, where_ref, left_ref, right_ref, mask_ref, w1_ref, wt_ref, out_ref, *rest):
+def cost_kernel(dims, where_ref, left_ref, right_ref, mask_ref, w1_ref, wt_ref, cost_ref, off_ref, *rest):
     rows, cols, total_rows, total_cols, per_group = dims
     payload_ref, rest = (rest[0], rest[1:]) if packs(per_group) else (None, rest)
-    cost_ref, sems, *bufs = rest
+    bufs = rest
     first_row, first_col = where_ref[0], where_ref[1]
     row_low, row_high = -first_row, total_rows - first_row
     left_bufs, right_bufs = bufs[:4], bufs[4:]
@@ -111,32 +109,32 @@
         lane = lax.broadcasted_iota(jnp.int32, (LANES, LANES), 1)
         own = (lane // CH) == row % 2
 
-        def block(index, carry, pair=pair, own=own, row=row):
-            start = pl.multiple_of(index * LANES, LANES)
-            window = pl.multiple_of(cols - LANES - start, LANES)
-            scale = mask_ref[pl.ds(start, LANES), pair : pair + LANES]
-            a = jnp.where(own, left[pl.ds(start, LANES), pair : pair + LANES] * scale, jnp.zeros((), jnp.bfloat16))
-            b = right[pl.ds(window, 2 * LANES), pair : pair + LANES]
-            product = lax.dot_general(a, b, (((1,), (1,)), ((), ())), preferred_element_type=jnp.float32)
-            skewed = pltpu.roll(product, LANES + 1, 1, stride=1, stride_axis=0)
-            skewed = skewed[:, :LANES]
-            cost_ref[row, pl.ds(start, LANES), :] = skewed
+        for index in range(cols // LANES):
+            start = index * LANES
+            window = cols - LANES - start
+            scale = mask_ref[start : start + LANES, pair : pair + LANES]
+            a = jnp.where(own, left[start : start + LANES, pair : pair + LANES] * scale, jnp.zeros((), jnp.bfloat16))
+            b = right[window : window + 2 * LANES, pair : pair + LANES]
+            mean = jnp.mean(b.astype(jnp.float32), axis=0, keepdims=True).astype(jnp.bfloat16)
+            mean = jnp.broadcast_to(mean, (LANES, LANES))
+            product = lax.dot_general(
+                a, jnp.concatenate([b, mean], axis=0), (((1,), (1,)), ((), ())), preferred_element_type=jnp.float32
+            )
+            off_ref[row, index] = lax.dot_general(
+                mean[:16], a, (((1,), (1,)), ((), ())), preferred_element_type=jnp.float32
+            )[:8]
+            skewed = pltpu.roll(product[:, : 2 * LANES], LANES + 1, 1, stride=1, stride_axis=0)[:, :LANES]
+            cost_ref[row, start : start + LANES, :] = skewed
             if payload_ref is not None:
-                skewed = skewed - offsets(skewed)
+                skewed = skewed - product[:, 2 * LANES :]
                 for k in range(LANES // per_group):
                     piece = skewed[k * per_group : (k + 1) * per_group].astype(jnp.bfloat16)
                     group = index * (LANES // per_group) + k
                     payload_ref[group, row * per_group : (row + 1) * per_group, :] = piece
-            return carry
-
-        lax.fori_loop(0, cols // LANES, block, 0, unroll=BLOCKS)
-        pltpu.make_async_copy(cost_ref.at[row], out_ref.at[row], sems.at[row]).start()
-    for row in range(rows):
-        pltpu.make_async_copy(cost_ref.at[row], out_ref.at[row], sems.at[row]).wait()
 
 
 def cost_volume(left_stack, right_stack, mask, w1, wt, place, rows, cols, total_rows, total_cols, per_group):
-    bufs = [pltpu.VMEM((rows, cols, DISP), jnp.float32), pltpu.SemaphoreType.DMA((rows,))]
+    bufs = []
     for width in (cols, cols + DISP):
         sizes = plan(width)
         for layer in range(4):
@@ -145,13 +143,14 @@
             bufs.append(pltpu.VMEM((length, out_rows * CH), jnp.bfloat16))
     vmem = pl.BlockSpec(memory_space=pltpu.VMEM)
     shapes = [jax.ShapeDtypeStruct((rows, cols, DISP), jnp.float32)]
+    shapes.append(jax.ShapeDtypeStruct((rows, cols // LANES, 8, LANES), jnp.float32))
     if packs(per_group):
         shapes.append(jax.ShapeDtypeStruct((cols // per_group, rows * per_group, DISP), jnp.bfloat16))
     return pl.pallas_call(
         functools.partial(cost_kernel, (rows, cols, total_rows, total_cols, per_group)),
         out_shape=tuple(shapes),
         in_specs=[pl.BlockSpec(memory_space=pltpu.SMEM)] + [vmem] * 5,
-        out_specs=(pl.BlockSpec(memory_space=pltpu.HBM), vmem)[: len(shapes)],
+        out_specs=(vmem,) * len(shapes),
         scratch_shapes=bufs,
         compiler_params=pltpu.CompilerParams(vmem_limit_bytes=40 << 20),
         cost_estimate=pl.CostEstimate(flops=8_000_000_000, bytes_accessed=6_000_000, transcendentals=0),
@@ -161,7 +160,7 @@
 def row_scan_kernel(dims, has_sum, place_ref, cost_hbm, state_ref, *rest):
     rows, cols, flip, batch = dims
     if has_sum:
-        lead_hbm, out_ref, end_ref, lead_ref, lead_sem, *rest = rest
+        lead_hbm, off_ref, out_ref, end_ref, lead_ref, lead_sem, shift_ref, *rest = rest
     else:
         out_hbm, end_ref, out_ref, out_sems, *rest = rest
     cost_ref, cost_sems, tile_ref, turn_ref, pick_ref, split_a, split_b, even_ref, odd_ref, path_ref, low_ref = rest
@@ -185,15 +184,24 @@
         cut = pl.ds(pl.multiple_of(begin, width), length)
         return pltpu.make_async_copy(out_ref.at[:, cut], out_hbm.at[:, cut], out_sems.at[part])
 
+    def chunk_of(index):
+        return jnp.where(forward, index, count - 1 - index)
+
     def chunk_start(index):
-        chunk = jnp.where(forward, index, count - 1 - index)
-        return pl.multiple_of(chunk * width, width)
+        return pl.multiple_of(chunk_of(index) * width, width)
 
     for index in range(count):
         copy_in(index).start()
     if has_sum:
         copy_lead = pltpu.make_async_copy(lead_hbm, lead_ref, lead_sem)
         copy_lead.start()
+        for chunk in range(count):
+            block, within = divmod(chunk * width, LANES)
+            twice = jnp.zeros((8, LANES), jnp.float32)
+            for row in range(rows):
+                value = pltpu.roll(off_ref[row, block], (row * width - within) % LANES, 1)
+                twice = jnp.where(lane // width == row, 2.0 * value, twice)
+            shift_ref[chunk] = twice
 
     def build_pick(pair, carry):
         k = lax.broadcasted_iota(jnp.int32, (2 * LANES, 2 * LANES), 0) % LANES
@@ -226,12 +234,11 @@
     def emit(index):
         start = chunk_start(jnp.maximum(index, 0))
         low = low_ref[...]
+        if has_sum:
+            low = low - shift_ref[chunk_of(jnp.maximum(index, 0))]
         for v in range(16):
             turn_ref[pl.ds(v, 8, stride=16), :] = path_ref[v] - low
         done = turn_ref[...].T
-        if has_sum:
-            tile = jnp.concatenate([cost_ref[row, pl.ds(start, width), :] for row in range(rows)], axis=0)
-            done = done + 2.0 * offsets(tile)
         for row in range(rows):
             piece = done[row * width : (row + 1) * width]
             if has_sum:
@@ -316,7 +323,7 @@
             copy_out(1 - part).wait()
 
 
-def row_scan(place, cost, state, lead, flip):
+def row_scan(place, cost, state, lead, off, flip):
     rows, cols, _ = cost.shape
     width = LANES // rows
     count = cols // width
@@ -324,16 +331,18 @@
     vmem = pl.BlockSpec(memory_space=pltpu.VMEM)
     hbm = pl.BlockSpec(memory_space=pltpu.HBM)
     has_sum = lead is not None
-    args = [place, cost, state] + ([lead] if has_sum else [])
+    args = [place, cost, state] + ([lead, off] if has_sum else [])
     whole = pltpu.VMEM(cost.shape, jnp.float32)
     moved = [whole, pltpu.SemaphoreType.DMA(() if has_sum else (2,))]
+    if has_sum:
+        moved.append(pltpu.VMEM((count, 8, LANES), jnp.float32))
     return pl.pallas_call(
         functools.partial(row_scan_kernel, (rows, cols, flip, batch), has_sum),
         out_shape=(
             jax.ShapeDtypeStruct(cost.shape, jnp.float32),
             jax.ShapeDtypeStruct((16, 8, LANES), jnp.float32),
         ),
-        in_specs=[pl.BlockSpec(memory_space=pltpu.SMEM), hbm, vmem] + ([hbm] if has_sum else []),
+        in_specs=[pl.BlockSpec(memory_space=pltpu.SMEM), hbm, vmem] + ([hbm, vmem] if has_sum else []),
         out_specs=(vmem if has_sum else hbm, vmem),
         scratch_shapes=moved
         + [
@@ -349,7 +358,7 @@
             pltpu.VMEM((16, 8, LANES), jnp.float32),
             pltpu.VMEM((8, LANES), jnp.float32),
         ],
-        compiler_params=pltpu.CompilerParams(vmem_limit_bytes=24 << 20),
+        compiler_params=pltpu.CompilerParams(vmem_limit_bytes=SUM_ROOM if has_sum else SCAN_ROOM),
         cost_estimate=pl.CostEstimate(flops=2_000_000_000, bytes_accessed=30_000_000, transcendentals=0),
     )(*args)
 
@@ -610,26 +619,26 @@
     place = jnp.stack([group * rows, first_col, strip]).astype(jnp.int32)
 
     per_group = cols // groups
-    cost, *packed = cost_volume(
+    cost, off, *packed = cost_volume(
         left_stack, right_stack, mask, w1, wt, place, rows, cols, total_rows, total_cols, per_group
     )
     if packed:
         grouped = packed[0].reshape(groups, rows, per_group, DISP)
     else:
-        centred = (cost - offsets(cost.reshape(-1, DISP)).reshape(cost.shape)).astype(jnp.bfloat16)
+        centred = (cost - off[:, :, 0].reshape(rows, cols, 1)).astype(jnp.bfloat16)
         grouped = jnp.swapaxes(centred.reshape(rows, groups, per_group, DISP), 0, 1)
     columns = lax.all_to_all(grouped, "rows", split_axis=0, concat_axis=0, tiled=True)
     columns = columns.reshape(total_rows, per_group, DISP)
 
     zero = jnp.zeros((16, 8, LANES), jnp.float32)
-    leading, end = row_scan(place, cost, zero, None, False)
-    columns, end = lax.optimization_barrier((columns, end))
-    column_sum = column_scan(columns)
+    leading, end = row_scan(place, cost, zero, None, None, False)
     received = lax.ppermute(end, "strips", [(i, i ^ 1) for i in range(strips)])
+    columns, _ = lax.optimization_barrier((columns, end))
+    column_sum, received = lax.optimization_barrier((column_scan(columns), received))
     vertical = lax.all_to_all(
         column_sum.reshape(groups, rows, per_group, DISP), "rows", split_axis=0, concat_axis=0, tiled=True
     )
-    horizontal, _ = row_scan(place, cost, received, leading, True)
+    horizontal, _ = row_scan(place, cost, received, leading, off, True)
     return add_vertical(horizontal, vertical)
 
 

time: 80.7 us -> 80.7 us (level)
  Pallas kernels: 46.6 us -> 49.4 us
  local copies, waits for them, and re-layouts: 7 us -> 5.43 us
  waiting for transfers between devices: 3.01 us -> 1.77 us
    pallas_call x2, Pallas kernels: 29.8 us -> 34.4 us  [row_scan(): pl.pallas_call(functools.partial(row_scan_kernel, (rows, cols, flip, batc...]
    unnamed x14, local copies, waits for them, and re-layouts: 5.99 us -> 3.79 us
    pallas_call x1, Pallas kernels: 9.83 us -> 8.07 us  [cost_volume(): pl.pallas_call(functools.partial(cost_kernel, (rows, cols, total_rows, to...]
    ppermute x1, waiting for transfers between devices: 1.24 us -> 0.01 us  [per_device(): received = lax.ppermute(end, 'strips', [(i, i ^ 1) for i in range(strips)])]
  transfers between devices with their start and end apart: 6 -> 6, of which waited for: 3 -> 2; matrix products, arithmetic and copies ran while one was open for 2% -> 3% of each run, Pallas kernels for 38% -> 50%
where the time goes in v7:
time: 80.7 us; the launch traced here: 80 us
  Pallas kernels  49.4 us (61%)
  starting transfers between devices  20.8 us (26%)
  local copies, waits for them, and re-layouts  5.43 us (7%)
  other arithmetic  2.38 us (3%)
  waiting for transfers between devices  1.77 us (2%)
    pallas_call x2, Pallas kernels, row_scan(): pl.pallas_call(functools.partial(row_scan_kernel, (rows, cols, flip, batc...  34.4 us
    pallas_call x1, Pallas kernels, cost_volume(): pl.pallas_call(functools.partial(cost_kernel, (rows, cols, total_rows, to...  8.07 us
    all_to_all x1, starting transfers between devices, per_device(): lax.all_to_all(grouped, 'rows', split_axis=0, concat_axis=0, tiled=True)  7.65 us
    all_to_all x1, starting transfers between devices, per_device(): lax.all_to_all(column_sum.reshape(groups, rows, per_group, DISP), 'rows',...  6.9 us
    pallas_call x1, Pallas kernels, column_scan(): pl.pallas_call(kernel, out_shape=jax.ShapeDtypeStruct(columns.shape, jnp....  4.99 us
    ppermute x1, starting transfers between devices, neighbours(): lax.ppermute(pair, row_axis, [(i, i + 1) for i in range(groups - 1)])  4.84 us
    unnamed x14, local copies, waits for them, and re-layouts  3.79 us
  transfers between devices with their start and end apart: 6, of which 2 were waited for; matrix products, arithmetic and copies ran while one was open for 3% of the time, Pallas kernels for 50%

profile of v7, /device:TPU:0, one launch (start us, length us, event | category | flops | bytes accessed | tf_op | source)
XLA Modules:
  0.0 80.0 jit_solution(7795078163794957818)
XLA Ops:
  0.0 0.7 fusion.4
  0.7 4.8 %collective-permute-start = (bf16[2,4,512]{2,1,0:T(4,128)(2,1)S(1)}, bf16[2,4,512]{2,1,0:T(4,128)(2,1)S(1)}, u32[]{:S(2)}, u32[]{:S(2)}) collective-permute-start(bf16[2,4,512]{2,1,0:T(4,128)(2,1)S(1)} %pad_maximum_fusion.3), channel_id=1, source_target_pairs={{0,2},{2,4},{4,6},{6,8},{8,10},{10,12},{12,14},{14,16},{16,18},{18... | collective-permute-start | bytes 24584 | tf_op jit(solution)/shard_map/ppermute | solution.py:581
  5.6 1.3 %collective-permute-start.1 = (bf16[2,4,512]{2,1,0:T(4,128)(2,1)S(1)}, bf16[2,4,512]{2,1,0:T(4,128)(2,1)S(1)}, u32[]{:S(2)}, u32[]{:S(2)}) collective-permute-start(bf16[2,4,512]{2,1,0:T(4,128)(2,1)S(1)} %pad_maximum_fusion.3), channel_id=1, source_target_pairs={{2,0},{4,2},{6,4},{8,6},{10,8},{12,10},{14,12},{16,14},{18,16},{20... | collective-permute-start | bytes 24584 | tf_op jit(solution)/shard_map/ppermute | solution.py:582
  6.9 0.7 fusion.6
  7.6 0.7 convert_bitcast_fusion
  8.3 0.1 tile.10.first_ref
  8.4 0.0 copy-start
  8.4 1.0 %copy-done = bf16[3,64,64,3,3]{2,1,4,3,0:T(8,128)(2,1)S(1)} copy-done((bf16[3,64,64,3,3]{2,1,4,3,0:T(8,128)(2,1)S(1)}, bf16[3,64,64,3,3]{2,1,4,3,0:T(8,128)(2,1)}, u32[]{:S(2)}) %copy-start) | copy-done | bytes 221208
  9.4 0.9 %shard_map.55 = (bf16[3,3,384,256]{3,2,1,0:T(8,128)(2,1)S(1)}, bf16[128,640]{1,0:T(8,128)(2,1)S(1)}) custom-call(bf16[3,3,3,64,64]{4,3,2,1,0:T(8,128)(2,1)S(1)} %bitcast.26, f32[9,640]{1,0:T(8,128)S(1)} %tile.10.first_ref), custom_call_target="tpu_custom_call" | custom-call | flops 10000000 | bytes 2500000 | tf_op jit(solution)/shard_map/pallas_call | solution.py:566
  10.3 0.0 collective-permute-done
  10.3 0.8 %collective-permute-done.1 = bf16[2,4,512]{2,1,0:T(4,128)(2,1)S(1)} collective-permute-done((bf16[2,4,512]{2,1,0:T(4,128)(2,1)S(1)}, bf16[2,4,512]{2,1,0:T(4,128)(2,1)S(1)}, u32[]{:S(2)}, u32[]{:S(2)}) %collective-permute-start.1) | collective-permute-done | bytes 8224 | tf_op jit(solution)/shard_map/ppermute | solution.py:582
  11.2 0.1 collective-permute-start.2
  11.2 0.1 pad_add_fusion.where_ref.place_ref
  11.3 0.0 copy-start.1
  11.3 0.1 copy.14.mask_ref
  11.5 0.9 %collective-permute-done.2 = bf16[2,12,512]{2,1,0:T(8,128)(2,1)S(1)} collective-permute-done((bf16[2,12,512]{2,1,0:T(8,128)(2,1)S(1)}, bf16[2,12,512]{2,1,0:T(8,128)(2,1)S(1)}, u32[]{:S(2)}, u32[]{:S(2)}) %collective-permute-start.2) | collective-permute-done | bytes 24608 | tf_op jit(solution)/shard_map/ppermute | solution.py:585
  12.5 0.1 fusion.3
  12.6 0.1 dynamic-slice_bitcast_fusion
  12.7 0.5 reverse
  13.2 0.1 slice.40
  13.2 0.1 fusion.8
  13.4 0.2 copy.13
  13.6 0.1 dynamic-slice_bitcast_fusion.1
  13.7 0.1 fusion.9
  13.8 0.1 copy.12
  14.0 8.1 %shard_map.56 = (f32[4,512,128]{2,1,0:T(8,128)S(1)}, f32[4,4,8,128]{3,2,1,0:T(8,128)S(1)}, bf16[16,128,128]{2,1,0:T(8,128)(2,1)}) custom-call(s32[3]{0:T(128)S(1)} %pad_add_fusion.where_ref.place_ref, bf16[560,128]{1,0:T(8,128)(2,1)S(1)} %pad_bitcast_fusion.1.left_ref, bf16[688,128]{1,0:T(8,128)(2,1)S(1)} %pad_bitcast_fusion.right_ref, ...), custom_call_target="tpu_custom_call" | custom-call | flops 8000000000 | bytes 6000000 | tf_op jit(solution)/shard_map/pallas_call | solution.py:149
  22.0 0.0 copy-done.1
  22.0 0.0 copy-start.3
  22.0 1.0 %copy-done.3 = f32[4,512,128]{2,1,0:T(8,128)} copy-done((f32[4,512,128]{2,1,0:T(8,128)}, f32[4,512,128]{2,1,0:T(8,128)S(1)}, u32[]{:S(2)}) %copy-start.3) | copy-done | bytes 1048600
  23.0 7.7 %all-to-all-start = ((bf16[16,4,32,128]{3,2,1,0:T(8,128)(2,1)}), bf16[16,4,32,128]{3,2,1,0:T(8,128)(2,1)S(1)}, u32[]{:S(2)}, u32[]{:S(2)}) async-start(bf16[16,4,32,128]{3,2,1,0:T(8,128)(2,1)} %bitcast.13), calls=%async_computation | async-start | bytes 1048576 | tf_op jit(solution)/shard_map/all_to_all | solution.py:630
  30.7 0.6 broadcast_in_dim.7.state_ref
  31.3 17.6 %shard_map.57 = (f32[4,512,128]{2,1,0:T(8,128)}, f32[16,8,128]{2,1,0:T(8,128)}) custom-call(s32[3]{0:T(128)} %copy-done.1, f32[4,512,128]{2,1,0:T(8,128)} %copy-done.3, f32[16,8,128]{2,1,0:T(8,128)} %broadcast_in_dim.7.state_ref), custom_call_target="tpu_custom_call" | custom-call | flops 2000000000 | bytes 30000000 | tf_op jit(solution)/shard_map/pallas_call | solution.py:339
  48.9 0.0 copy-start.2
  48.9 0.0 copy-start.4
  48.9 0.1 collective-permute-start.3
  49.0 0.0 all-to-all-done
  49.0 5.0 %shard_map.58 = bf16[64,32,128]{2,1,0:T(8,128)(2,1)} custom-call(bf16[64,32,128]{2,1,0:T(8,128)(2,1)S(1)} %bitcast.25), custom_call_target="tpu_custom_call" | custom-call | flops 200000000 | bytes 2000000 | tf_op jit(solution)/shard_map/pallas_call | solution.py:503
  54.0 0.0 collective-permute-done.3.state_ref
  54.0 6.9 %all-to-all-start.1 = ((bf16[16,4,32,128]{3,2,1,0:T(8,128)(2,1)}), bf16[16,4,32,128]{3,2,1,0:T(8,128)(2,1)S(1)}, u32[]{:S(2)}, u32[]{:S(2)}) async-start(bf16[16,4,32,128]{3,2,1,0:T(8,128)(2,1)} %bitcast.15), calls=%async_computation.1 | async-start | bytes 1048576 | tf_op jit(solution)/shard_map/all_to_all | solution.py:638
  60.9 0.0 copy-done.2
  60.9 0.0 copy-done.4
  60.9 0.0 copy-start.5
  60.9 1.2 %copy-done.5 = f32[4,512,128]{2,1,0:T(8,128)S(1)} copy-done((f32[4,512,128]{2,1,0:T(8,128)S(1)}, f32[4,512,128]{2,1,0:T(8,128)}, u32[]{:S(2)}) %copy-start.5) | copy-done | bytes 1048600
  62.2 16.8 %shard_map.59 = (f32[4,512,128]{2,1,0:T(8,128)S(1)}, f32[16,8,128]{2,1,0:T(8,128)}) custom-call(s32[3]{0:T(128)S(1)} %copy-done.2, f32[4,512,128]{2,1,0:T(8,128)S(1)} %copy-done.4, f32[16,8,128]{2,1,0:T(8,128)S(1)} %collective-permute-done.3.state_ref, f32[4,512,128]{2,1,0:T(8,128)S(1)} %copy-done.5, f32[4,4,8,128]{3,2,1,0:T(8,128)S(1)} %get-tuple-element.32.rest_1_), custom_call_target="tpu_custom_call" | custom-call | flops 2000000000 | bytes 30000000 | tf_op jit(solution)/shard_map/pallas_call | solution.py:339
  79.0 0.0 all-to-all-done.1.down_ref
  79.0 1.1 %shard_map.60 = f32[4,512,128]{2,1,0:T(8,128)} custom-call(f32[4,512,128]{2,1,0:T(8,128)S(1)} %get-tuple-element.33.across_ref, bf16[16,4,32,128]{3,2,1,0:T(8,128)(2,1)S(1)} %all-to-all-done.1.down_ref), custom_call_target="tpu_custom_call" | custom-call | flops 300000 | bytes 2600000 | tf_op jit(solution)/shard_map/pallas_call | solution.py:525
  (11 shorter events, 0.2 us)
Async XLA Ops:
  0.7 9.6 %collective-permute-start = (bf16[2,4,512]{2,1,0:T(4,128)(2,1)S(1)}, bf16[2,4,512]{2,1,0:T(4,128)(2,1)S(1)}, u32[]{:S(2)}, u32[]{:S(2)}) collective-permute-start(bf16[2,4,512]{2,1,0:T(4,128)(2,1)S(1)} %pad_maximum_fusion.3), channel_id=1, source_target_pairs={{0,2},{2,4},{4,6},{6,8},{8,10},{10,12},{12,14},{14,16},{16,18},{18... | collective-permute-start | bytes 24584 | tf_op jit(solution)/shard_map/ppermute | solution.py:581
  5.6 5.5 %collective-permute-start.1 = (bf16[2,4,512]{2,1,0:T(4,128)(2,1)S(1)}, bf16[2,4,512]{2,1,0:T(4,128)(2,1)S(1)}, u32[]{:S(2)}, u32[]{:S(2)}) collective-permute-start(bf16[2,4,512]{2,1,0:T(4,128)(2,1)S(1)} %pad_maximum_fusion.3), channel_id=1, source_target_pairs={{2,0},{4,2},{6,4},{8,6},{10,8},{12,10},{14,12},{16,14},{18,16},{20... | collective-permute-start | bytes 24584 | tf_op jit(solution)/shard_map/ppermute | solution.py:582
  8.4 1.0 %copy-start = (bf16[3,64,64,3,3]{2,1,4,3,0:T(8,128)(2,1)S(1)}, bf16[3,64,64,3,3]{2,1,4,3,0:T(8,128)(2,1)}, u32[]{:S(2)}) copy-start(bf16[3,64,64,3,3]{2,1,4,3,0:T(8,128)(2,1)} %param.9) | copy-start | bytes 663556
  11.2 1.3 %collective-permute-start.2 = (bf16[2,12,512]{2,1,0:T(8,128)(2,1)S(1)}, bf16[2,12,512]{2,1,0:T(8,128)(2,1)S(1)}, u32[]{:S(2)}, u32[]{:S(2)}) collective-permute-start(bf16[2,12,512]{2,1,0:T(8,128)(2,1)S(1)} %pad_maximum_fusion.2), channel_id=1, source_target_pairs={{0,1},{1,0},{2,3},{3,2},{4,5},{5,4},{6,7},{7,6},{8,9},{9,8},{10,11... | collective-permute-start | bytes 73736 | tf_op jit(solution)/shard_map/ppermute | solution.py:585
  11.3 10.7 %copy-start.1 = (s32[3]{0:T(128)}, s32[3]{0:T(128)S(1)}, u32[]{:S(2)}) copy-start(s32[3]{0:T(128)S(1)} %pad_add_fusion.where_ref.place_ref) | copy-start | bytes 40
  22.0 1.0 %copy-start.3 = (f32[4,512,128]{2,1,0:T(8,128)}, f32[4,512,128]{2,1,0:T(8,128)S(1)}, u32[]{:S(2)}) copy-start(f32[4,512,128]{2,1,0:T(8,128)S(1)} %get-tuple-element.26.cost_hbm) | copy-start | bytes 3145732
  23.0 26.0 %all-to-all-start = ((bf16[16,4,32,128]{3,2,1,0:T(8,128)(2,1)}), bf16[16,4,32,128]{3,2,1,0:T(8,128)(2,1)S(1)}, u32[]{:S(2)}, u32[]{:S(2)}) async-start(bf16[16,4,32,128]{3,2,1,0:T(8,128)(2,1)} %bitcast.13), calls=%async_computation | async-start | bytes 1048576 | tf_op jit(solution)/shard_map/all_to_all | solution.py:630
  48.9 12.0 %copy-start.2 = (s32[3]{0:T(128)S(1)}, s32[3]{0:T(128)}, u32[]{:S(2)}) copy-start(s32[3]{0:T(128)} %copy-done.1) | copy-start | bytes 40
  48.9 12.0 %copy-start.4 = (f32[4,512,128]{2,1,0:T(8,128)S(1)}, f32[4,512,128]{2,1,0:T(8,128)}, u32[]{:S(2)}) copy-start(f32[4,512,128]{2,1,0:T(8,128)} %copy-done.3) | copy-start | bytes 3145732
  48.9 5.1 %collective-permute-start.3 = (f32[16,8,128]{2,1,0:T(8,128)}, f32[16,8,128]{2,1,0:T(8,128)S(1)}, u32[]{:S(2)}, u32[]{:S(2)}) collective-permute-start(f32[16,8,128]{2,1,0:T(8,128)} %get-tuple-element.28), channel_id=1, source_target_pairs={{0,1},{1,0},{2,3},{3,2},{4,5},{5,4},{6,7},{7,6},{8,9},{9,8},{10,11... | collective-permute-start | bytes 196616 | tf_op jit(solution)/shard_map/ppermute | solution.py:635
  54.0 25.0 %all-to-all-start.1 = ((bf16[16,4,32,128]{3,2,1,0:T(8,128)(2,1)}), bf16[16,4,32,128]{3,2,1,0:T(8,128)(2,1)S(1)}, u32[]{:S(2)}, u32[]{:S(2)}) async-start(bf16[16,4,32,128]{3,2,1,0:T(8,128)(2,1)} %bitcast.15), calls=%async_computation.1 | async-start | bytes 1048576 | tf_op jit(solution)/shard_map/all_to_all | solution.py:638
  60.9 1.2 %copy-start.5 = (f32[4,512,128]{2,1,0:T(8,128)S(1)}, f32[4,512,128]{2,1,0:T(8,128)}, u32[]{:S(2)}) copy-start(f32[4,512,128]{2,1,0:T(8,128)} %get-tuple-element.31.rest_0_) | copy-start | bytes 3145732

commit v8 on v7

--- a/solution.py
+++ b/solution.py
@@ -21,6 +21,14 @@
 SUM_ROOM = 24 << 20
 
 
+def over(x, n):
+    return lax.shift_right_logical(x, n.bit_length() - 1) if n & (n - 1) == 0 else x // n
+
+
+def within(x, n):
+    return x & (n - 1) if n & (n - 1) == 0 else x % n
+
+
 def plan(width):
     unit = 16 * PARTS
     totals = [-(-width // unit) * unit]
@@ -32,7 +40,7 @@
 def feature_stacks(stacks, w1_ref, wt_ref, row_low, row_high):
     def inside(test, base, count, lanes, halo, lane0):
         position = lax.broadcasted_iota(jnp.int32, (count, lanes), 0) + base
-        row = (lax.broadcasted_iota(jnp.int32, (count, lanes), 1) + lane0) // CH - halo
+        row = over(lax.broadcasted_iota(jnp.int32, (count, lanes), 1) + lane0, CH) - halo
         return test(position) & (row >= row_low) & (row < row_high)
 
     def first(index, carry):
@@ -79,11 +87,16 @@
             convolve(index, 0)
 
 
+def offsets(costs):
+    even = jnp.full((DISP, DISP), 1.0 / DISP, jnp.bfloat16)
+    return jnp.dot(costs.astype(jnp.bfloat16), even, preferred_element_type=jnp.float32)
+
+
 def packs(per_group):
     return per_group % 16 == 0 and LANES % per_group == 0
 
 
-def cost_kernel(dims, where_ref, left_ref, right_ref, mask_ref, w1_ref, wt_ref, cost_ref, off_ref, *rest):
+def cost_kernel(dims, where_ref, left_ref, right_ref, mask_ref, w1_ref, wt_ref, cost_ref, *rest):
     rows, cols, total_rows, total_cols, per_group = dims
     payload_ref, rest = (rest[0], rest[1:]) if packs(per_group) else (None, rest)
     bufs = rest
@@ -107,7 +120,7 @@
     for row in range(rows):
         pair = row // 2 * LANES
         lane = lax.broadcasted_iota(jnp.int32, (LANES, LANES), 1)
-        own = (lane // CH) == row % 2
+        own = over(lane, CH) == row % 2
 
         for index in range(cols // LANES):
             start = index * LANES
@@ -115,18 +128,11 @@
             scale = mask_ref[start : start + LANES, pair : pair + LANES]
             a = jnp.where(own, left[start : start + LANES, pair : pair + LANES] * scale, jnp.zeros((), jnp.bfloat16))
             b = right[window : window + 2 * LANES, pair : pair + LANES]
-            mean = jnp.mean(b.astype(jnp.float32), axis=0, keepdims=True).astype(jnp.bfloat16)
-            mean = jnp.broadcast_to(mean, (LANES, LANES))
-            product = lax.dot_general(
-                a, jnp.concatenate([b, mean], axis=0), (((1,), (1,)), ((), ())), preferred_element_type=jnp.float32
-            )
-            off_ref[row, index] = lax.dot_general(
-                mean[:16], a, (((1,), (1,)), ((), ())), preferred_element_type=jnp.float32
-            )[:8]
-            skewed = pltpu.roll(product[:, : 2 * LANES], LANES + 1, 1, stride=1, stride_axis=0)[:, :LANES]
+            product = lax.dot_general(a, b, (((1,), (1,)), ((), ())), preferred_element_type=jnp.float32)
+            skewed = pltpu.roll(product, LANES + 1, 1, stride=1, stride_axis=0)[:, :LANES]
             cost_ref[row, start : start + LANES, :] = skewed
             if payload_ref is not None:
-                skewed = skewed - product[:, 2 * LANES :]
+                skewed = skewed - offsets(skewed)
                 for k in range(LANES // per_group):
                     piece = skewed[k * per_group : (k + 1) * per_group].astype(jnp.bfloat16)
                     group = index * (LANES // per_group) + k
@@ -143,7 +149,6 @@
             bufs.append(pltpu.VMEM((length, out_rows * CH), jnp.bfloat16))
     vmem = pl.BlockSpec(memory_space=pltpu.VMEM)
     shapes = [jax.ShapeDtypeStruct((rows, cols, DISP), jnp.float32)]
-    shapes.append(jax.ShapeDtypeStruct((rows, cols // LANES, 8, LANES), jnp.float32))
     if packs(per_group):
         shapes.append(jax.ShapeDtypeStruct((cols // per_group, rows * per_group, DISP), jnp.bfloat16))
     return pl.pallas_call(
@@ -157,10 +162,10 @@
     )(place, left_stack, right_stack, mask, w1, wt)
 
 
-def row_scan_kernel(dims, has_sum, place_ref, cost_hbm, state_ref, *rest):
+def row_scan_kernel(dims, has_sum, place_ref, cost_hbm, *rest):
     rows, cols, flip, batch = dims
     if has_sum:
-        lead_hbm, off_ref, out_ref, end_ref, lead_ref, lead_sem, shift_ref, *rest = rest
+        state_ref, lead_hbm, out_ref, end_ref, lead_ref, lead_sem, *rest = rest
     else:
         out_hbm, end_ref, out_ref, out_sems, *rest = rest
     cost_ref, cost_sems, tile_ref, turn_ref, pick_ref, split_a, split_b, even_ref, odd_ref, path_ref, low_ref = rest
@@ -169,7 +174,7 @@
     forward = place_ref[2] == (1 if flip else 0)
     lane = lax.broadcasted_iota(jnp.int32, (8, LANES), 1)
     sublane = lax.broadcasted_iota(jnp.int32, (8, LANES), 0)
-    lane_col = lane % width
+    lane_col = within(lane, width)
 
     def copy_in(index):
         part = pl.ds(chunk_start(index), width)
@@ -195,18 +200,11 @@
     if has_sum:
         copy_lead = pltpu.make_async_copy(lead_hbm, lead_ref, lead_sem)
         copy_lead.start()
-        for chunk in range(count):
-            block, within = divmod(chunk * width, LANES)
-            twice = jnp.zeros((8, LANES), jnp.float32)
-            for row in range(rows):
-                value = pltpu.roll(off_ref[row, block], (row * width - within) % LANES, 1)
-                twice = jnp.where(lane // width == row, 2.0 * value, twice)
-            shift_ref[chunk] = twice
 
     def build_pick(pair, carry):
-        k = lax.broadcasted_iota(jnp.int32, (2 * LANES, 2 * LANES), 0) % LANES
+        k = within(lax.broadcasted_iota(jnp.int32, (2 * LANES, 2 * LANES), 0), LANES)
         n = lax.broadcasted_iota(jnp.int32, (2 * LANES, 2 * LANES), 1)
-        wanted = n % LANES // width * width + 2 * pair + n // LANES
+        wanted = over(within(n, LANES), width) * width + 2 * pair + over(n, LANES)
         pick_ref[pair] = jnp.where(k == wanted, 1.0, 0.0).astype(jnp.bfloat16)
         return carry
 
@@ -234,11 +232,11 @@
     def emit(index):
         start = chunk_start(jnp.maximum(index, 0))
         low = low_ref[...]
-        if has_sum:
-            low = low - shift_ref[chunk_of(jnp.maximum(index, 0))]
         for v in range(16):
             turn_ref[pl.ds(v, 8, stride=16), :] = path_ref[v] - low
         done = turn_ref[...].T
+        tile = jnp.concatenate([cost_ref[row, pl.ds(start, width), :] for row in range(rows)], axis=0)
+        done = done + offsets(tile)
         for row in range(rows):
             piece = done[row * width : (row + 1) * width]
             if has_sum:
@@ -311,7 +309,10 @@
 
         return state
 
-    state = tuple(state_ref[v] for v in range(16))
+    if has_sum:
+        state = tuple(state_ref[v] for v in range(16))
+    else:
+        state = (jnp.zeros((8, LANES), jnp.float32),) * 16
     state = lax.fori_loop(0, rounds, two_batches, state)
     emit(count - 1)
     if not has_sum:
@@ -323,7 +324,7 @@
             copy_out(1 - part).wait()
 
 
-def row_scan(place, cost, state, lead, off, flip):
+def row_scan(place, cost, state, lead, flip):
     rows, cols, _ = cost.shape
     width = LANES // rows
     count = cols // width
@@ -331,18 +332,16 @@
     vmem = pl.BlockSpec(memory_space=pltpu.VMEM)
     hbm = pl.BlockSpec(memory_space=pltpu.HBM)
     has_sum = lead is not None
-    args = [place, cost, state] + ([lead, off] if has_sum else [])
+    args = [place, cost] + ([state, lead] if has_sum else [])
     whole = pltpu.VMEM(cost.shape, jnp.float32)
     moved = [whole, pltpu.SemaphoreType.DMA(() if has_sum else (2,))]
-    if has_sum:
-        moved.append(pltpu.VMEM((count, 8, LANES), jnp.float32))
     return pl.pallas_call(
         functools.partial(row_scan_kernel, (rows, cols, flip, batch), has_sum),
         out_shape=(
             jax.ShapeDtypeStruct(cost.shape, jnp.float32),
             jax.ShapeDtypeStruct((16, 8, LANES), jnp.float32),
         ),
-        in_specs=[pl.BlockSpec(memory_space=pltpu.SMEM), hbm, vmem] + ([hbm, vmem] if has_sum else []),
+        in_specs=[pl.BlockSpec(memory_space=pltpu.SMEM), hbm] + ([vmem, hbm] if has_sum else []),
         out_specs=(vmem if has_sum else hbm, vmem),
         scratch_shapes=moved
         + [
@@ -410,10 +409,10 @@
     per = LANES // both
     tiles = length // per
     sublane = lax.broadcasted_iota(jnp.int32, (8, LANES), 0)
-    lane_step = lax.broadcasted_iota(jnp.int32, (8, LANES), 1) // both
+    lane_step = over(lax.broadcasted_iota(jnp.int32, (8, LANES), 1), both)
     k = lax.broadcasted_iota(jnp.int32, (LANES, per * LANES), 0)
     n = lax.broadcasted_iota(jnp.int32, (LANES, per * LANES), 1)
-    pick = jnp.where(k == n // LANES * both + n % both, 1.0, 0.0).astype(jnp.bfloat16)
+    pick = jnp.where(k == over(n, LANES) * both + within(n, both), 1.0, 0.0).astype(jnp.bfloat16)
 
     def places(tile):
         rows = []
@@ -549,12 +548,12 @@
     shape = w1_ref.shape
     row = lax.broadcasted_iota(jnp.int32, shape, 0)
     tall = rows + 8
-    dx_at, dy_at = row // tall, row % tall - lax.broadcasted_iota(jnp.int32, shape, 1) // CH
+    column = over(lax.broadcasted_iota(jnp.int32, shape, 1), CH)
     value = jnp.zeros(shape, jnp.float32)
     for dy in range(taps):
         for dx in range(taps):
             line = first_ref[dy * taps + dx : dy * taps + dx + 1, :]
-            value = jnp.where((dx_at == dx) & (dy_at == dy), line, value)
+            value = jnp.where((row - dx * tall - column == dy) & (row >= dx * tall) & (row < (dx + 1) * tall), line, value)
     w1_ref[...] = value.astype(jnp.bfloat16)
 
 
@@ -619,26 +618,25 @@
     place = jnp.stack([group * rows, first_col, strip]).astype(jnp.int32)
 
     per_group = cols // groups
-    cost, off, *packed = cost_volume(
+    cost, *packed = cost_volume(
         left_stack, right_stack, mask, w1, wt, place, rows, cols, total_rows, total_cols, per_group
     )
     if packed:
         grouped = packed[0].reshape(groups, rows, per_group, DISP)
     else:
-        centred = (cost - off[:, :, 0].reshape(rows, cols, 1)).astype(jnp.bfloat16)
+        centred = (cost - offsets(cost.reshape(-1, DISP)).reshape(cost.shape)).astype(jnp.bfloat16)
         grouped = jnp.swapaxes(centred.reshape(rows, groups, per_group, DISP), 0, 1)
     columns = lax.all_to_all(grouped, "rows", split_axis=0, concat_axis=0, tiled=True)
     columns = columns.reshape(total_rows, per_group, DISP)
 
-    zero = jnp.zeros((16, 8, LANES), jnp.float32)
-    leading, end = row_scan(place, cost, zero, None, None, False)
+    leading, end = row_scan(place, cost, None, None, False)
     received = lax.ppermute(end, "strips", [(i, i ^ 1) for i in range(strips)])
     columns, _ = lax.optimization_barrier((columns, end))
     column_sum, received = lax.optimization_barrier((column_scan(columns), received))
     vertical = lax.all_to_all(
         column_sum.reshape(groups, rows, per_group, DISP), "rows", split_axis=0, concat_axis=0, tiled=True
     )
-    horizontal, _ = row_scan(place, cost, received, leading, off, True)
+    horizontal, _ = row_scan(place, cost, received, leading, True)
     return add_vertical(horizontal, vertical)
 
 

time: 80.7 us -> 75.8 us (0.939)
  Pallas kernels: 49.4 us -> 44.4 us
    pallas_call x2, Pallas kernels: 34.4 us -> 28.5 us  [row_scan(): pl.pallas_call(functools.partial(row_scan_kernel, (rows, cols, flip, batc...]
    pallas_call x1, Pallas kernels: 8.07 us -> 9.28 us  [cost_volume(): pl.pallas_call(functools.partial(cost_kernel, (rows, cols, total_rows, to...]
  transfers between devices with their start and end apart: 6 -> 6, of which waited for: 2 -> 3; matrix products, arithmetic and copies ran while one was open for 3% -> 2% of each run, Pallas kernels for 50% -> 45%
where the time goes in v8:
time: 75.8 us; the launch traced here: 75.2 us
  Pallas kernels  44.4 us (59%)
  starting transfers between devices  21.5 us (28%)
  local copies, waits for them, and re-layouts  4.78 us (6%)
  other arithmetic  2.39 us (3%)
  waiting for transfers between devices  1.93 us (3%)
    pallas_call x2, Pallas kernels, row_scan(): pl.pallas_call(functools.partial(row_scan_kernel, (rows, cols, flip, batc...  28.5 us
    pallas_call x1, Pallas kernels, cost_volume(): pl.pallas_call(functools.partial(cost_kernel, (rows, cols, total_rows, to...  9.28 us
    all_to_all x1, starting transfers between devices, per_device(): lax.all_to_all(grouped, 'rows', split_axis=0, concat_axis=0, tiled=True)  8.19 us
    all_to_all x1, starting transfers between devices, per_device(): lax.all_to_all(column_sum.reshape(groups, rows, per_group, DISP), 'rows',...  6.39 us
    ppermute x1, starting transfers between devices, neighbours(): lax.ppermute(pair, row_axis, [(i, i + 1) for i in range(groups - 1)])  5.47 us
    pallas_call x1, Pallas kernels, column_scan(): pl.pallas_call(kernel, out_shape=jax.ShapeDtypeStruct(columns.shape, jnp....  4.99 us
    unnamed x14, local copies, waits for them, and re-layouts  3.79 us
  transfers between devices with their start and end apart: 6, of which 3 were waited for; matrix products, arithmetic and copies ran while one was open for 2% of the time, Pallas kernels for 45%

profile of v8, /device:TPU:0, one launch (start us, length us, event | category | flops | bytes accessed | tf_op | source)
XLA Modules:
  0.0 75.2 jit_solution(7847495840773619280)
XLA Ops:
  0.0 0.7 fusion.4
  0.7 1.3 %collective-permute-start.1 = (bf16[2,4,512]{2,1,0:T(4,128)(2,1)S(1)}, bf16[2,4,512]{2,1,0:T(4,128)(2,1)S(1)}, u32[]{:S(2)}, u32[]{:S(2)}) collective-permute-start(bf16[2,4,512]{2,1,0:T(4,128)(2,1)S(1)} %pad_maximum_fusion.3), channel_id=1, source_target_pairs={{2,0},{4,2},{6,4},{8,6},{10,8},{12,10},{14,12},{16,14},{18,16},{20... | collective-permute-start | bytes 24584 | tf_op jit(solution)/shard_map/ppermute | solution.py:581
  2.0 5.5 %collective-permute-start = (bf16[2,4,512]{2,1,0:T(4,128)(2,1)S(1)}, bf16[2,4,512]{2,1,0:T(4,128)(2,1)S(1)}, u32[]{:S(2)}, u32[]{:S(2)}) collective-permute-start(bf16[2,4,512]{2,1,0:T(4,128)(2,1)S(1)} %pad_maximum_fusion.3), channel_id=1, source_target_pairs={{0,2},{2,4},{4,6},{6,8},{8,10},{10,12},{12,14},{14,16},{16,18},{18... | collective-permute-start | bytes 24584 | tf_op jit(solution)/shard_map/ppermute | solution.py:580
  7.5 0.7 fusion.6
  8.2 0.7 convert_bitcast_fusion
  8.9 0.1 tile.10.first_ref
  9.0 0.0 copy-start
  9.0 1.0 %copy-done = bf16[3,64,64,3,3]{2,1,4,3,0:T(8,128)(2,1)S(1)} copy-done((bf16[3,64,64,3,3]{2,1,4,3,0:T(8,128)(2,1)S(1)}, bf16[3,64,64,3,3]{2,1,4,3,0:T(8,128)(2,1)}, u32[]{:S(2)}) %copy-start) | copy-done | bytes 221208
  10.0 0.5 shard_map.55
  10.5 0.0 collective-permute-done.1
  10.6 0.0 collective-permute-done
  10.6 0.1 collective-permute-start.2
  10.7 0.1 pad_add_fusion.where_ref.place_ref
  10.8 0.0 copy-start.1
  10.8 0.1 copy.14.mask_ref
  10.9 0.9 %collective-permute-done.2 = bf16[2,12,512]{2,1,0:T(8,128)(2,1)S(1)} collective-permute-done((bf16[2,12,512]{2,1,0:T(8,128)(2,1)S(1)}, bf16[2,12,512]{2,1,0:T(8,128)(2,1)S(1)}, u32[]{:S(2)}, u32[]{:S(2)}) %collective-permute-start.2) | collective-permute-done | bytes 24608 | tf_op jit(solution)/shard_map/ppermute | solution.py:584
  11.9 0.1 fusion.3
  12.0 0.1 dynamic-slice_bitcast_fusion
  12.1 0.5 reverse
  12.6 0.1 slice.40
  12.7 0.1 dynamic-slice_bitcast_fusion.1
  12.8 0.1 fusion.9
  12.8 0.1 fusion.8
  13.0 0.1 copy.12
  13.2 0.2 copy.13
  13.4 9.3 %shard_map.56 = (f32[4,512,128]{2,1,0:T(8,128)S(1)}, bf16[16,128,128]{2,1,0:T(8,128)(2,1)}) custom-call(s32[3]{0:T(128)S(1)} %pad_add_fusion.where_ref.place_ref, bf16[560,128]{1,0:T(8,128)(2,1)S(1)} %pad_bitcast_fusion.1.left_ref, bf16[688,128]{1,0:T(8,128)(2,1)S(1)} %pad_bitcast_fusion.right_ref, bf16[512,256]{1,0:T(8,128)(2,1)S(1)} %copy.14.mask_ref, ...), custom_call_target="tpu_custom_call" | custom-call | flops 8000000000 | bytes 6000000 | tf_op jit(solution)/shard_map/pallas_call | solution.py:154
  22.7 0.0 copy-done.1
  22.7 0.0 copy-start.3
  22.7 1.0 %copy-done.3 = f32[4,512,128]{2,1,0:T(8,128)} copy-done((f32[4,512,128]{2,1,0:T(8,128)}, f32[4,512,128]{2,1,0:T(8,128)S(1)}, u32[]{:S(2)}) %copy-start.3) | copy-done | bytes 1048600
  23.7 8.2 %all-to-all-start = ((bf16[16,4,32,128]{3,2,1,0:T(8,128)(2,1)}), bf16[16,4,32,128]{3,2,1,0:T(8,128)(2,1)S(1)}, u32[]{:S(2)}, u32[]{:S(2)}) async-start(bf16[16,4,32,128]{3,2,1,0:T(8,128)(2,1)} %bitcast.13), calls=%async_computation | async-start | bytes 1048576 | tf_op jit(solution)/shard_map/all_to_all | solution.py:629
  31.9 14.8 %shard_map.57 = (f32[4,512,128]{2,1,0:T(8,128)}, f32[16,8,128]{2,1,0:T(8,128)}) custom-call(s32[3]{0:T(128)} %copy-done.1, f32[4,512,128]{2,1,0:T(8,128)} %copy-done.3), custom_call_target="tpu_custom_call" | custom-call | flops 2000000000 | bytes 30000000 | tf_op jit(solution)/shard_map/pallas_call | solution.py:338
  46.7 0.0 copy-start.2
  46.7 0.0 copy-start.4
  46.7 0.1 collective-permute-start.3
  46.8 0.5 all-to-all-done
  47.3 5.0 %shard_map.58 = bf16[64,32,128]{2,1,0:T(8,128)(2,1)} custom-call(bf16[64,32,128]{2,1,0:T(8,128)(2,1)S(1)} %bitcast.25), custom_call_target="tpu_custom_call" | custom-call | flops 200000000 | bytes 2000000 | tf_op jit(solution)/shard_map/pallas_call | solution.py:502
  52.3 0.0 collective-permute-done.3.rest_0_
  52.3 6.4 %all-to-all-start.1 = ((bf16[16,4,32,128]{3,2,1,0:T(8,128)(2,1)}), bf16[16,4,32,128]{3,2,1,0:T(8,128)(2,1)S(1)}, u32[]{:S(2)}, u32[]{:S(2)}) async-start(bf16[16,4,32,128]{3,2,1,0:T(8,128)(2,1)} %bitcast.15), calls=%async_computation.1 | async-start | bytes 1048576 | tf_op jit(solution)/shard_map/all_to_all | solution.py:636
  58.7 0.0 copy-done.2
  58.7 0.0 copy-done.4
  58.7 0.0 copy-start.5
  58.7 1.2 %copy-done.5 = f32[4,512,128]{2,1,0:T(8,128)S(1)} copy-done((f32[4,512,128]{2,1,0:T(8,128)S(1)}, f32[4,512,128]{2,1,0:T(8,128)}, u32[]{:S(2)}) %copy-start.5) | copy-done | bytes 1048600
  59.9 13.7 %shard_map.59 = (f32[4,512,128]{2,1,0:T(8,128)S(1)}, f32[16,8,128]{2,1,0:T(8,128)}) custom-call(s32[3]{0:T(128)S(1)} %copy-done.2, f32[4,512,128]{2,1,0:T(8,128)S(1)} %copy-done.4, f32[16,8,128]{2,1,0:T(8,128)S(1)} %collective-permute-done.3.rest_0_, f32[4,512,128]{2,1,0:T(8,128)S(1)} %copy-done.5), custom_call_target="tpu_custom_call" | custom-call | flops 2000000000 | bytes 30000000 | tf_op jit(solution)/shard_map/pallas_call | solution.py:338
  73.7 0.5 all-to-all-done.1.down_ref
  74.1 1.1 %shard_map.60 = f32[4,512,128]{2,1,0:T(8,128)} custom-call(f32[4,512,128]{2,1,0:T(8,128)S(1)} %get-tuple-element.31.across_ref, bf16[16,4,32,128]{3,2,1,0:T(8,128)(2,1)S(1)} %all-to-all-done.1.down_ref), custom_call_target="tpu_custom_call" | custom-call | flops 300000 | bytes 2600000 | tf_op jit(solution)/shard_map/pallas_call | solution.py:524
  (11 shorter events, 0.2 us)
Async XLA Ops:
  0.7 9.8 %collective-permute-start.1 = (bf16[2,4,512]{2,1,0:T(4,128)(2,1)S(1)}, bf16[2,4,512]{2,1,0:T(4,128)(2,1)S(1)}, u32[]{:S(2)}, u32[]{:S(2)}) collective-permute-start(bf16[2,4,512]{2,1,0:T(4,128)(2,1)S(1)} %pad_maximum_fusion.3), channel_id=1, source_target_pairs={{2,0},{4,2},{6,4},{8,6},{10,8},{12,10},{14,12},{16,14},{18,16},{20... | collective-permute-start | bytes 24584 | tf_op jit(solution)/shard_map/ppermute | solution.py:581
  2.0 8.5 %collective-permute-start = (bf16[2,4,512]{2,1,0:T(4,128)(2,1)S(1)}, bf16[2,4,512]{2,1,0:T(4,128)(2,1)S(1)}, u32[]{:S(2)}, u32[]{:S(2)}) collective-permute-start(bf16[2,4,512]{2,1,0:T(4,128)(2,1)S(1)} %pad_maximum_fusion.3), channel_id=1, source_target_pairs={{0,2},{2,4},{4,6},{6,8},{8,10},{10,12},{12,14},{14,16},{16,18},{18... | collective-permute-start | bytes 24584 | tf_op jit(solution)/shard_map/ppermute | solution.py:580
  9.0 1.0 %copy-start = (bf16[3,64,64,3,3]{2,1,4,3,0:T(8,128)(2,1)S(1)}, bf16[3,64,64,3,3]{2,1,4,3,0:T(8,128)(2,1)}, u32[]{:S(2)}) copy-start(bf16[3,64,64,3,3]{2,1,4,3,0:T(8,128)(2,1)} %param.9) | copy-start | bytes 663556
  10.6 1.3 %collective-permute-start.2 = (bf16[2,12,512]{2,1,0:T(8,128)(2,1)S(1)}, bf16[2,12,512]{2,1,0:T(8,128)(2,1)S(1)}, u32[]{:S(2)}, u32[]{:S(2)}) collective-permute-start(bf16[2,12,512]{2,1,0:T(8,128)(2,1)S(1)} %pad_maximum_fusion.2), channel_id=1, source_target_pairs={{0,1},{1,0},{2,3},{3,2},{4,5},{5,4},{6,7},{7,6},{8,9},{9,8},{10,11... | collective-permute-start | bytes 73736 | tf_op jit(solution)/shard_map/ppermute | solution.py:584
  10.8 11.9 %copy-start.1 = (s32[3]{0:T(128)}, s32[3]{0:T(128)S(1)}, u32[]{:S(2)}) copy-start(s32[3]{0:T(128)S(1)} %pad_add_fusion.where_ref.place_ref) | copy-start | bytes 40
  22.7 1.0 %copy-start.3 = (f32[4,512,128]{2,1,0:T(8,128)}, f32[4,512,128]{2,1,0:T(8,128)S(1)}, u32[]{:S(2)}) copy-start(f32[4,512,128]{2,1,0:T(8,128)S(1)} %get-tuple-element.25.cost_hbm) | copy-start | bytes 3145732
  23.7 23.6 %all-to-all-start = ((bf16[16,4,32,128]{3,2,1,0:T(8,128)(2,1)}), bf16[16,4,32,128]{3,2,1,0:T(8,128)(2,1)S(1)}, u32[]{:S(2)}, u32[]{:S(2)}) async-start(bf16[16,4,32,128]{3,2,1,0:T(8,128)(2,1)} %bitcast.13), calls=%async_computation | async-start | bytes 1048576 | tf_op jit(solution)/shard_map/all_to_all | solution.py:629
  46.7 12.0 %copy-start.2 = (s32[3]{0:T(128)S(1)}, s32[3]{0:T(128)}, u32[]{:S(2)}) copy-start(s32[3]{0:T(128)} %copy-done.1) | copy-start | bytes 40
  46.7 12.0 %copy-start.4 = (f32[4,512,128]{2,1,0:T(8,128)S(1)}, f32[4,512,128]{2,1,0:T(8,128)}, u32[]{:S(2)}) copy-start(f32[4,512,128]{2,1,0:T(8,128)} %copy-done.3) | copy-start | bytes 3145732
  46.7 5.6 %collective-permute-start.3 = (f32[16,8,128]{2,1,0:T(8,128)}, f32[16,8,128]{2,1,0:T(8,128)S(1)}, u32[]{:S(2)}, u32[]{:S(2)}) collective-permute-start(f32[16,8,128]{2,1,0:T(8,128)} %get-tuple-element.27), channel_id=1, source_target_pairs={{0,1},{1,0},{2,3},{3,2},{4,5},{5,4},{6,7},{7,6},{8,9},{9,8},{10,11... | collective-permute-start | bytes 196616 | tf_op jit(solution)/shard_map/ppermute | solution.py:633
  52.3 21.9 %all-to-all-start.1 = ((bf16[16,4,32,128]{3,2,1,0:T(8,128)(2,1)}), bf16[16,4,32,128]{3,2,1,0:T(8,128)(2,1)S(1)}, u32[]{:S(2)}, u32[]{:S(2)}) async-start(bf16[16,4,32,128]{3,2,1,0:T(8,128)(2,1)} %bitcast.15), calls=%async_computation.1 | async-start | bytes 1048576 | tf_op jit(solution)/shard_map/all_to_all | solution.py:636
  58.7 1.2 %copy-start.5 = (f32[4,512,128]{2,1,0:T(8,128)S(1)}, f32[4,512,128]{2,1,0:T(8,128)}, u32[]{:S(2)}) copy-start(f32[4,512,128]{2,1,0:T(8,128)} %get-tuple-element.30.rest_1_) | copy-start | bytes 3145732

commit v9 on v8

--- a/solution.py
+++ b/solution.py
@@ -421,8 +421,8 @@
         return rows
 
     def prepare(index, carry):
-        for slot in range(8):
-            tile = index * 8 + slot
+        for slot in range(16):
+            tile = index * 16 + slot
             block = jnp.concatenate([cost_ref[row] for row in places(tile)], axis=0)
             tile_ref[slot] = block.astype(jnp.float32).T
             for v in range(0, 16, 2):
@@ -431,14 +431,14 @@
                 )
                 split_ref[slot * LANES + v * 8 : slot * LANES + v * 8 + 16, :] = plane.astype(jnp.bfloat16)
         spread = jnp.dot(split_ref[...], pick, preferred_element_type=jnp.float32)
-        for slot in range(8):
+        for slot in range(16):
             for step in range(per):
-                spread_ref[index * 8 + slot, step] = spread[
+                spread_ref[index * 16 + slot, step] = spread[
                     slot * LANES : slot * LANES + LANES, step * LANES : step * LANES + LANES
                 ]
         return carry
 
-    lax.fori_loop(0, tiles // 8, prepare, 0)
+    lax.fori_loop(0, tiles // 16, prepare, 0)
 
     def emit(tile, last):
         tile = jnp.maximum(tile, 0)
@@ -475,7 +475,7 @@
         return tuple(state)
 
     def loop(begin, end, state, last):
-        return lax.fori_loop(begin, end, lambda tile, carry: run(tile, carry, last), state, unroll=8)
+        return lax.fori_loop(begin, end, lambda tile, carry: run(tile, carry, last), state, unroll=16)
 
     state = (jnp.zeros((8, LANES), jnp.float32),) * 16
     state = loop(0, tiles // 2, state, False)
@@ -490,11 +490,11 @@
     scratch = [pltpu.VMEM(columns.shape, jnp.float32)]
     kernel = column_kernel
     per = LANES // (2 * width)
-    if width % 16 == 0 and LANES % (2 * width) == 0 and length % (16 * per) == 0:
+    if width % 16 == 0 and LANES % (2 * width) == 0 and length % (32 * per) == 0:
         kernel = column_tiles_kernel
         scratch = [
-            pltpu.VMEM((8, LANES, LANES), jnp.float32),
-            pltpu.VMEM((8 * LANES, LANES), jnp.bfloat16),
+            pltpu.VMEM((16, LANES, LANES), jnp.float32),
+            pltpu.VMEM((16 * LANES, LANES), jnp.bfloat16),
             pltpu.VMEM((length // per, per, LANES, LANES), jnp.float32),
             pltpu.VMEM((16, 8, LANES), jnp.float32),
             pltpu.VMEM((LANES, LANES), jnp.float32),

time: 75.8 us -> 74.9 us (0.988)
  Pallas kernels: 44.4 us -> 43.5 us
    pallas_call x1, Pallas kernels: 4.99 us -> 4.1 us  [column_scan(): pl.pallas_call(kernel, out_shape=jax.ShapeDtypeStruct(columns.shape, jnp....]
where the time goes in v9:
time: 74.9 us; the launch traced here: 74.3 us
  Pallas kernels  43.5 us (58%)
  starting transfers between devices  21.5 us (29%)
  local copies, waits for them, and re-layouts  4.78 us (6%)
  other arithmetic  2.39 us (3%)
  waiting for transfers between devices  1.93 us (3%)
    pallas_call x2, Pallas kernels, row_scan(): pl.pallas_call(functools.partial(row_scan_kernel, (rows, cols, flip, batc...  28.5 us
    pallas_call x1, Pallas kernels, cost_volume(): pl.pallas_call(functools.partial(cost_kernel, (rows, cols, total_rows, to...  9.28 us
    all_to_all x1, starting transfers between devices, per_device(): lax.all_to_all(grouped, 'rows', split_axis=0, concat_axis=0, tiled=True)  8.19 us
    all_to_all x1, starting transfers between devices, per_device(): lax.all_to_all(column_sum.reshape(groups, rows, per_group, DISP), 'rows',...  6.39 us
    ppermute x1, starting transfers between devices, neighbours(): lax.ppermute(pair, row_axis, [(i, i + 1) for i in range(groups - 1)])  5.47 us
    pallas_call x1, Pallas kernels, column_scan(): pl.pallas_call(kernel, out_shape=jax.ShapeDtypeStruct(columns.shape, jnp....  4.1 us
    unnamed x14, local copies, waits for them, and re-layouts  3.79 us
  transfers between devices with their start and end apart: 6, of which 3 were waited for; matrix products, arithmetic and copies ran while one was open for 2% of the time, Pallas kernels for 45%

profile of v9, /device:TPU:0, one launch (start us, length us, event | category | flops | bytes accessed | tf_op | source)
XLA Modules:
  0.0 74.3 jit_solution(12187081074258807617)
XLA Ops:
  0.0 0.7 fusion.4
  0.7 1.3 %collective-permute-start.1 = (bf16[2,4,512]{2,1,0:T(4,128)(2,1)S(1)}, bf16[2,4,512]{2,1,0:T(4,128)(2,1)S(1)}, u32[]{:S(2)}, u32[]{:S(2)}) collective-permute-start(bf16[2,4,512]{2,1,0:T(4,128)(2,1)S(1)} %pad_maximum_fusion.3), channel_id=1, source_target_pairs={{2,0},{4,2},{6,4},{8,6},{10,8},{12,10},{14,12},{16,14},{18,16},{20... | collective-permute-start | bytes 24584 | tf_op jit(solution)/shard_map/ppermute | solution.py:581
  2.0 5.5 %collective-permute-start = (bf16[2,4,512]{2,1,0:T(4,128)(2,1)S(1)}, bf16[2,4,512]{2,1,0:T(4,128)(2,1)S(1)}, u32[]{:S(2)}, u32[]{:S(2)}) collective-permute-start(bf16[2,4,512]{2,1,0:T(4,128)(2,1)S(1)} %pad_maximum_fusion.3), channel_id=1, source_target_pairs={{0,2},{2,4},{4,6},{6,8},{8,10},{10,12},{12,14},{14,16},{16,18},{18... | collective-permute-start | bytes 24584 | tf_op jit(solution)/shard_map/ppermute | solution.py:580
  7.5 0.7 fusion.6
  8.2 0.7 convert_bitcast_fusion
  8.9 0.1 tile.10.first_ref
  9.0 0.0 copy-start
  9.0 1.0 %copy-done = bf16[3,64,64,3,3]{2,1,4,3,0:T(8,128)(2,1)S(1)} copy-done((bf16[3,64,64,3,3]{2,1,4,3,0:T(8,128)(2,1)S(1)}, bf16[3,64,64,3,3]{2,1,4,3,0:T(8,128)(2,1)}, u32[]{:S(2)}) %copy-start) | copy-done | bytes 221208
  10.0 0.5 shard_map.55
  10.5 0.0 collective-permute-done.1
  10.6 0.0 collective-permute-done
  10.6 0.1 collective-permute-start.2
  10.7 0.1 pad_add_fusion.where_ref.place_ref
  10.8 0.0 copy-start.1
  10.8 0.1 copy.14.mask_ref
  10.9 0.9 %collective-permute-done.2 = bf16[2,12,512]{2,1,0:T(8,128)(2,1)S(1)} collective-permute-done((bf16[2,12,512]{2,1,0:T(8,128)(2,1)S(1)}, bf16[2,12,512]{2,1,0:T(8,128)(2,1)S(1)}, u32[]{:S(2)}, u32[]{:S(2)}) %collective-permute-start.2) | collective-permute-done | bytes 24608 | tf_op jit(solution)/shard_map/ppermute | solution.py:584
  11.9 0.1 fusion.3
  12.0 0.1 dynamic-slice_bitcast_fusion
  12.1 0.5 reverse
  12.6 0.1 slice.40
  12.7 0.1 dynamic-slice_bitcast_fusion.1
  12.8 0.1 fusion.9
  12.8 0.1 fusion.8
  13.0 0.1 copy.12
  13.2 0.2 copy.13
  13.4 9.3 %shard_map.56 = (f32[4,512,128]{2,1,0:T(8,128)S(1)}, bf16[16,128,128]{2,1,0:T(8,128)(2,1)}) custom-call(s32[3]{0:T(128)S(1)} %pad_add_fusion.where_ref.place_ref, bf16[560,128]{1,0:T(8,128)(2,1)S(1)} %pad_bitcast_fusion.1.left_ref, bf16[688,128]{1,0:T(8,128)(2,1)S(1)} %pad_bitcast_fusion.right_ref, bf16[512,256]{1,0:T(8,128)(2,1)S(1)} %copy.14.mask_ref, ...), custom_call_target="tpu_custom_call" | custom-call | flops 8000000000 | bytes 6000000 | tf_op jit(solution)/shard_map/pallas_call | solution.py:154
  22.7 0.0 copy-done.1
  22.7 0.0 copy-start.3
  22.7 1.0 %copy-done.3 = f32[4,512,128]{2,1,0:T(8,128)} copy-done((f32[4,512,128]{2,1,0:T(8,128)}, f32[4,512,128]{2,1,0:T(8,128)S(1)}, u32[]{:S(2)}) %copy-start.3) | copy-done | bytes 1048600
  23.7 8.2 %all-to-all-start = ((bf16[16,4,32,128]{3,2,1,0:T(8,128)(2,1)}), bf16[16,4,32,128]{3,2,1,0:T(8,128)(2,1)S(1)}, u32[]{:S(2)}, u32[]{:S(2)}) async-start(bf16[16,4,32,128]{3,2,1,0:T(8,128)(2,1)} %bitcast.13), calls=%async_computation | async-start | bytes 1048576 | tf_op jit(solution)/shard_map/all_to_all | solution.py:629
  31.9 14.8 %shard_map.57 = (f32[4,512,128]{2,1,0:T(8,128)}, f32[16,8,128]{2,1,0:T(8,128)}) custom-call(s32[3]{0:T(128)} %copy-done.1, f32[4,512,128]{2,1,0:T(8,128)} %copy-done.3), custom_call_target="tpu_custom_call" | custom-call | flops 2000000000 | bytes 30000000 | tf_op jit(solution)/shard_map/pallas_call | solution.py:338
  46.7 0.0 copy-start.2
  46.7 0.0 copy-start.4
  46.7 0.1 collective-permute-start.3
  46.8 0.5 all-to-all-done
  47.3 4.1 %shard_map.58 = bf16[64,32,128]{2,1,0:T(8,128)(2,1)} custom-call(bf16[64,32,128]{2,1,0:T(8,128)(2,1)S(1)} %bitcast.25), custom_call_target="tpu_custom_call" | custom-call | flops 200000000 | bytes 2000000 | tf_op jit(solution)/shard_map/pallas_call | solution.py:502
  51.4 0.0 collective-permute-done.3.rest_0_
  51.4 6.4 %all-to-all-start.1 = ((bf16[16,4,32,128]{3,2,1,0:T(8,128)(2,1)}), bf16[16,4,32,128]{3,2,1,0:T(8,128)(2,1)S(1)}, u32[]{:S(2)}, u32[]{:S(2)}) async-start(bf16[16,4,32,128]{3,2,1,0:T(8,128)(2,1)} %bitcast.15), calls=%async_computation.1 | async-start | bytes 1048576 | tf_op jit(solution)/shard_map/all_to_all | solution.py:636
  57.8 0.0 copy-done.2
  57.8 0.0 copy-done.4
  57.8 0.0 copy-start.5
  57.8 1.2 %copy-done.5 = f32[4,512,128]{2,1,0:T(8,128)S(1)} copy-done((f32[4,512,128]{2,1,0:T(8,128)S(1)}, f32[4,512,128]{2,1,0:T(8,128)}, u32[]{:S(2)}) %copy-start.5) | copy-done | bytes 1048600
  59.0 13.7 %shard_map.59 = (f32[4,512,128]{2,1,0:T(8,128)S(1)}, f32[16,8,128]{2,1,0:T(8,128)}) custom-call(s32[3]{0:T(128)S(1)} %copy-done.2, f32[4,512,128]{2,1,0:T(8,128)S(1)} %copy-done.4, f32[16,8,128]{2,1,0:T(8,128)S(1)} %collective-permute-done.3.rest_0_, f32[4,512,128]{2,1,0:T(8,128)S(1)} %copy-done.5), custom_call_target="tpu_custom_call" | custom-call | flops 2000000000 | bytes 30000000 | tf_op jit(solution)/shard_map/pallas_call | solution.py:338
  72.8 0.5 all-to-all-done.1.down_ref
  73.2 1.1 %shard_map.60 = f32[4,512,128]{2,1,0:T(8,128)} custom-call(f32[4,512,128]{2,1,0:T(8,128)S(1)} %get-tuple-element.31.across_ref, bf16[16,4,32,128]{3,2,1,0:T(8,128)(2,1)S(1)} %all-to-all-done.1.down_ref), custom_call_target="tpu_custom_call" | custom-call | flops 300000 | bytes 2600000 | tf_op jit(solution)/shard_map/pallas_call | solution.py:524
  (11 shorter events, 0.2 us)
Async XLA Ops:
  0.7 9.8 %collective-permute-start.1 = (bf16[2,4,512]{2,1,0:T(4,128)(2,1)S(1)}, bf16[2,4,512]{2,1,0:T(4,128)(2,1)S(1)}, u32[]{:S(2)}, u32[]{:S(2)}) collective-permute-start(bf16[2,4,512]{2,1,0:T(4,128)(2,1)S(1)} %pad_maximum_fusion.3), channel_id=1, source_target_pairs={{2,0},{4,2},{6,4},{8,6},{10,8},{12,10},{14,12},{16,14},{18,16},{20... | collective-permute-start | bytes 24584 | tf_op jit(solution)/shard_map/ppermute | solution.py:581
  2.0 8.5 %collective-permute-start = (bf16[2,4,512]{2,1,0:T(4,128)(2,1)S(1)}, bf16[2,4,512]{2,1,0:T(4,128)(2,1)S(1)}, u32[]{:S(2)}, u32[]{:S(2)}) collective-permute-start(bf16[2,4,512]{2,1,0:T(4,128)(2,1)S(1)} %pad_maximum_fusion.3), channel_id=1, source_target_pairs={{0,2},{2,4},{4,6},{6,8},{8,10},{10,12},{12,14},{14,16},{16,18},{18... | collective-permute-start | bytes 24584 | tf_op jit(solution)/shard_map/ppermute | solution.py:580
  9.0 1.0 %copy-start = (bf16[3,64,64,3,3]{2,1,4,3,0:T(8,128)(2,1)S(1)}, bf16[3,64,64,3,3]{2,1,4,3,0:T(8,128)(2,1)}, u32[]{:S(2)}) copy-start(bf16[3,64,64,3,3]{2,1,4,3,0:T(8,128)(2,1)} %param.9) | copy-start | bytes 663556
  10.6 1.3 %collective-permute-start.2 = (bf16[2,12,512]{2,1,0:T(8,128)(2,1)S(1)}, bf16[2,12,512]{2,1,0:T(8,128)(2,1)S(1)}, u32[]{:S(2)}, u32[]{:S(2)}) collective-permute-start(bf16[2,12,512]{2,1,0:T(8,128)(2,1)S(1)} %pad_maximum_fusion.2), channel_id=1, source_target_pairs={{0,1},{1,0},{2,3},{3,2},{4,5},{5,4},{6,7},{7,6},{8,9},{9,8},{10,11... | collective-permute-start | bytes 73736 | tf_op jit(solution)/shard_map/ppermute | solution.py:584
  10.8 11.9 %copy-start.1 = (s32[3]{0:T(128)}, s32[3]{0:T(128)S(1)}, u32[]{:S(2)}) copy-start(s32[3]{0:T(128)S(1)} %pad_add_fusion.where_ref.place_ref) | copy-start | bytes 40
  22.7 1.0 %copy-start.3 = (f32[4,512,128]{2,1,0:T(8,128)}, f32[4,512,128]{2,1,0:T(8,128)S(1)}, u32[]{:S(2)}) copy-start(f32[4,512,128]{2,1,0:T(8,128)S(1)} %get-tuple-element.25.cost_hbm) | copy-start | bytes 3145732
  23.7 23.6 %all-to-all-start = ((bf16[16,4,32,128]{3,2,1,0:T(8,128)(2,1)}), bf16[16,4,32,128]{3,2,1,0:T(8,128)(2,1)S(1)}, u32[]{:S(2)}, u32[]{:S(2)}) async-start(bf16[16,4,32,128]{3,2,1,0:T(8,128)(2,1)} %bitcast.13), calls=%async_computation | async-start | bytes 1048576 | tf_op jit(solution)/shard_map/all_to_all | solution.py:629
  46.7 11.1 %copy-start.2 = (s32[3]{0:T(128)S(1)}, s32[3]{0:T(128)}, u32[]{:S(2)}) copy-start(s32[3]{0:T(128)} %copy-done.1) | copy-start | bytes 40
  46.7 11.1 %copy-start.4 = (f32[4,512,128]{2,1,0:T(8,128)S(1)}, f32[4,512,128]{2,1,0:T(8,128)}, u32[]{:S(2)}) copy-start(f32[4,512,128]{2,1,0:T(8,128)} %copy-done.3) | copy-start | bytes 3145732
  46.7 4.7 %collective-permute-start.3 = (f32[16,8,128]{2,1,0:T(8,128)}, f32[16,8,128]{2,1,0:T(8,128)S(1)}, u32[]{:S(2)}, u32[]{:S(2)}) collective-permute-start(f32[16,8,128]{2,1,0:T(8,128)} %get-tuple-element.27), channel_id=1, source_target_pairs={{0,1},{1,0},{2,3},{3,2},{4,5},{5,4},{6,7},{7,6},{8,9},{9,8},{10,11... | collective-permute-start | bytes 196616 | tf_op jit(solution)/shard_map/ppermute | solution.py:633
  51.4 21.9 %all-to-all-start.1 = ((bf16[16,4,32,128]{3,2,1,0:T(8,128)(2,1)}), bf16[16,4,32,128]{3,2,1,0:T(8,128)(2,1)S(1)}, u32[]{:S(2)}, u32[]{:S(2)}) async-start(bf16[16,4,32,128]{3,2,1,0:T(8,128)(2,1)} %bitcast.15), calls=%async_computation.1 | async-start | bytes 1048576 | tf_op jit(solution)/shard_map/all_to_all | solution.py:636
  57.8 1.2 %copy-start.5 = (f32[4,512,128]{2,1,0:T(8,128)S(1)}, f32[4,512,128]{2,1,0:T(8,128)}, u32[]{:S(2)}) copy-start(f32[4,512,128]{2,1,0:T(8,128)} %get-tuple-element.30.rest_1_) | copy-start | bytes 3145732

commit v10 on v9

--- a/solution.py
+++ b/solution.py
@@ -208,7 +208,7 @@
         pick_ref[pair] = jnp.where(k == wanted, 1.0, 0.0).astype(jnp.bfloat16)
         return carry
 
-    lax.fori_loop(0, width // 2, build_pick, 0)
+    lax.fori_loop(0, width // 2, build_pick, 0, unroll=4)
 
     def split(index, target):
         start = chunk_start(jnp.minimum(index, count - 1))
@@ -287,11 +287,11 @@
         split(batch + slot, split_b.at[pl.ds(slot * LANES, LANES)])
 
     def first(group, carry):
-        for k in range(4):
-            spread(split_a, even_ref, group * 4 + k)
+        for k in range(8):
+            spread(split_a, even_ref, group * 8 + k)
         return carry
 
-    lax.fori_loop(0, width // 8, first, 0)
+    lax.fori_loop(0, width // 16, first, 0)
 
     for index in range(2 * batch, count):
         copy_in(index).wait()

time: 74.9 us -> 74.6 us (level)
  waiting for transfers between devices: 1.93 us -> 2.73 us
  Pallas kernels: 43.5 us -> 42.7 us
    pallas_call x2, Pallas kernels: 28.5 us -> 27.7 us  [row_scan(): pl.pallas_call(functools.partial(row_scan_kernel, (rows, cols, flip, batc...]
  transfers between devices with their start and end apart: 6 -> 6, of which waited for: 3 -> 3; matrix products, arithmetic and copies ran while one was open for 2% -> 2% of each run, Pallas kernels for 45% -> 44%
where the time goes in v10:
time: 74.6 us; the launch traced here: 74 us
  Pallas kernels  42.7 us (57%)
  starting transfers between devices  21.2 us (28%)
  local copies, waits for them, and re-layouts  4.78 us (6%)
  waiting for transfers between devices  2.73 us (4%)
  other arithmetic  2.39 us (3%)
    pallas_call x2, Pallas kernels, row_scan(): pl.pallas_call(functools.partial(row_scan_kernel, (rows, cols, flip, batc...  27.7 us
    pallas_call x1, Pallas kernels, cost_volume(): pl.pallas_call(functools.partial(cost_kernel, (rows, cols, total_rows, to...  9.28 us
    all_to_all x1, starting transfers between devices, per_device(): lax.all_to_all(grouped, 'rows', split_axis=0, concat_axis=0, tiled=True)  8.19 us
    all_to_all x1, starting transfers between devices, per_device(): lax.all_to_all(column_sum.reshape(groups, rows, per_group, DISP), 'rows',...  6.07 us
    ppermute x1, starting transfers between devices, neighbours(): lax.ppermute(pair, row_axis, [(i, i + 1) for i in range(groups - 1)])  5.47 us
    pallas_call x1, Pallas kernels, column_scan(): pl.pallas_call(kernel, out_shape=jax.ShapeDtypeStruct(columns.shape, jnp....  4.1 us
    unnamed x14, local copies, waits for them, and re-layouts  3.79 us
  transfers between devices with their start and end apart: 6, of which 3 were waited for; matrix products, arithmetic and copies ran while one was open for 2% of the time, Pallas kernels for 44%

profile of v10, /device:TPU:0, one launch (start us, length us, event | category | flops | bytes accessed | tf_op | source)
XLA Modules:
  0.0 74.0 jit_solution(15683720288230029804)
XLA Ops:
  0.0 0.7 fusion.4
  0.7 1.3 %collective-permute-start.1 = (bf16[2,4,512]{2,1,0:T(4,128)(2,1)S(1)}, bf16[2,4,512]{2,1,0:T(4,128)(2,1)S(1)}, u32[]{:S(2)}, u32[]{:S(2)}) collective-permute-start(bf16[2,4,512]{2,1,0:T(4,128)(2,1)S(1)} %pad_maximum_fusion.3), channel_id=1, source_target_pairs={{2,0},{4,2},{6,4},{8,6},{10,8},{12,10},{14,12},{16,14},{18,16},{20... | collective-permute-start | bytes 24584 | tf_op jit(solution)/shard_map/ppermute | solution.py:581
  2.0 5.5 %collective-permute-start = (bf16[2,4,512]{2,1,0:T(4,128)(2,1)S(1)}, bf16[2,4,512]{2,1,0:T(4,128)(2,1)S(1)}, u32[]{:S(2)}, u32[]{:S(2)}) collective-permute-start(bf16[2,4,512]{2,1,0:T(4,128)(2,1)S(1)} %pad_maximum_fusion.3), channel_id=1, source_target_pairs={{0,2},{2,4},{4,6},{6,8},{8,10},{10,12},{12,14},{14,16},{16,18},{18... | collective-permute-start | bytes 24584 | tf_op jit(solution)/shard_map/ppermute | solution.py:580
  7.5 0.7 fusion.6
  8.2 0.7 convert_bitcast_fusion
  8.9 0.1 tile.10.first_ref
  9.0 0.0 copy-start
  9.0 1.0 %copy-done = bf16[3,64,64,3,3]{2,1,4,3,0:T(8,128)(2,1)S(1)} copy-done((bf16[3,64,64,3,3]{2,1,4,3,0:T(8,128)(2,1)S(1)}, bf16[3,64,64,3,3]{2,1,4,3,0:T(8,128)(2,1)}, u32[]{:S(2)}) %copy-start) | copy-done | bytes 221208
  10.0 0.5 shard_map.55
  10.5 0.0 collective-permute-done.1
  10.6 0.0 collective-permute-done
  10.6 0.1 collective-permute-start.2
  10.7 0.1 pad_add_fusion.where_ref.place_ref
  10.8 0.0 copy-start.1
  10.8 0.1 copy.14.mask_ref
  10.9 0.9 %collective-permute-done.2 = bf16[2,12,512]{2,1,0:T(8,128)(2,1)S(1)} collective-permute-done((bf16[2,12,512]{2,1,0:T(8,128)(2,1)S(1)}, bf16[2,12,512]{2,1,0:T(8,128)(2,1)S(1)}, u32[]{:S(2)}, u32[]{:S(2)}) %collective-permute-start.2) | collective-permute-done | bytes 24608 | tf_op jit(solution)/shard_map/ppermute | solution.py:584
  11.9 0.1 fusion.3
  12.0 0.1 dynamic-slice_bitcast_fusion
  12.1 0.5 reverse
  12.6 0.1 slice.40
  12.7 0.1 dynamic-slice_bitcast_fusion.1
  12.8 0.1 fusion.9
  12.8 0.1 fusion.8
  13.0 0.1 copy.12
  13.2 0.2 copy.13
  13.4 9.3 %shard_map.56 = (f32[4,512,128]{2,1,0:T(8,128)S(1)}, bf16[16,128,128]{2,1,0:T(8,128)(2,1)}) custom-call(s32[3]{0:T(128)S(1)} %pad_add_fusion.where_ref.place_ref, bf16[560,128]{1,0:T(8,128)(2,1)S(1)} %pad_bitcast_fusion.1.left_ref, bf16[688,128]{1,0:T(8,128)(2,1)S(1)} %pad_bitcast_fusion.right_ref, bf16[512,256]{1,0:T(8,128)(2,1)S(1)} %copy.14.mask_ref, ...), custom_call_target="tpu_custom_call" | custom-call | flops 8000000000 | bytes 6000000 | tf_op jit(solution)/shard_map/pallas_call | solution.py:154
  22.7 0.0 copy-done.1
  22.7 0.0 copy-start.3
  22.7 1.0 %copy-done.3 = f32[4,512,128]{2,1,0:T(8,128)} copy-done((f32[4,512,128]{2,1,0:T(8,128)}, f32[4,512,128]{2,1,0:T(8,128)S(1)}, u32[]{:S(2)}) %copy-start.3) | copy-done | bytes 1048600
  23.7 8.2 %all-to-all-start = ((bf16[16,4,32,128]{3,2,1,0:T(8,128)(2,1)}), bf16[16,4,32,128]{3,2,1,0:T(8,128)(2,1)S(1)}, u32[]{:S(2)}, u32[]{:S(2)}) async-start(bf16[16,4,32,128]{3,2,1,0:T(8,128)(2,1)} %bitcast.13), calls=%async_computation | async-start | bytes 1048576 | tf_op jit(solution)/shard_map/all_to_all | solution.py:629
  31.9 14.5 %shard_map.57 = (f32[4,512,128]{2,1,0:T(8,128)}, f32[16,8,128]{2,1,0:T(8,128)}) custom-call(s32[3]{0:T(128)} %copy-done.1, f32[4,512,128]{2,1,0:T(8,128)} %copy-done.3), custom_call_target="tpu_custom_call" | custom-call | flops 2000000000 | bytes 30000000 | tf_op jit(solution)/shard_map/pallas_call | solution.py:338
  46.3 0.0 copy-start.2
  46.3 0.0 copy-start.4
  46.4 0.1 collective-permute-start.3
  46.4 0.8 %all-to-all-done = bf16[16,4,32,128]{3,2,1,0:T(8,128)(2,1)S(1)} async-done(((bf16[16,4,32,128]{3,2,1,0:T(8,128)(2,1)}), bf16[16,4,32,128]{3,2,1,0:T(8,128)(2,1)S(1)}, u32[]{:S(2)}, u32[]{:S(2)}) %all-to-all-start) | async-done | bytes 524320 | tf_op jit(solution)/shard_map/all_to_all | solution.py:629
  47.3 4.1 %shard_map.58 = bf16[64,32,128]{2,1,0:T(8,128)(2,1)} custom-call(bf16[64,32,128]{2,1,0:T(8,128)(2,1)S(1)} %bitcast.25), custom_call_target="tpu_custom_call" | custom-call | flops 200000000 | bytes 2000000 | tf_op jit(solution)/shard_map/pallas_call | solution.py:502
  51.4 0.0 collective-permute-done.3.rest_0_
  51.4 6.1 %all-to-all-start.1 = ((bf16[16,4,32,128]{3,2,1,0:T(8,128)(2,1)}), bf16[16,4,32,128]{3,2,1,0:T(8,128)(2,1)S(1)}, u32[]{:S(2)}, u32[]{:S(2)}) async-start(bf16[16,4,32,128]{3,2,1,0:T(8,128)(2,1)} %bitcast.15), calls=%async_computation.1 | async-start | bytes 1048576 | tf_op jit(solution)/shard_map/all_to_all | solution.py:636
  57.4 0.0 copy-done.2
  57.5 0.0 copy-done.4
  57.5 0.0 copy-start.5
  57.5 1.2 %copy-done.5 = f32[4,512,128]{2,1,0:T(8,128)S(1)} copy-done((f32[4,512,128]{2,1,0:T(8,128)S(1)}, f32[4,512,128]{2,1,0:T(8,128)}, u32[]{:S(2)}) %copy-start.5) | copy-done | bytes 1048600
  58.7 13.3 %shard_map.59 = (f32[4,512,128]{2,1,0:T(8,128)S(1)}, f32[16,8,128]{2,1,0:T(8,128)}) custom-call(s32[3]{0:T(128)S(1)} %copy-done.2, f32[4,512,128]{2,1,0:T(8,128)S(1)} %copy-done.4, f32[16,8,128]{2,1,0:T(8,128)S(1)} %collective-permute-done.3.rest_0_, f32[4,512,128]{2,1,0:T(8,128)S(1)} %copy-done.5), custom_call_target="tpu_custom_call" | custom-call | flops 2000000000 | bytes 30000000 | tf_op jit(solution)/shard_map/pallas_call | solution.py:338
  72.0 0.9 %all-to-all-done.1.down_ref = bf16[16,4,32,128]{3,2,1,0:T(8,128)(2,1)S(1)} async-done(((bf16[16,4,32,128]{3,2,1,0:T(8,128)(2,1)}), bf16[16,4,32,128]{3,2,1,0:T(8,128)(2,1)S(1)}, u32[]{:S(2)}, u32[]{:S(2)}) %all-to-all-start.1) | async-done | bytes 524320 | tf_op jit(solution)/shard_map/all_to_all | solution.py:636
  72.9 1.1 %shard_map.60 = f32[4,512,128]{2,1,0:T(8,128)} custom-call(f32[4,512,128]{2,1,0:T(8,128)S(1)} %get-tuple-element.31.across_ref, bf16[16,4,32,128]{3,2,1,0:T(8,128)(2,1)S(1)} %all-to-all-done.1.down_ref), custom_call_target="tpu_custom_call" | custom-call | flops 300000 | bytes 2600000 | tf_op jit(solution)/shard_map/pallas_call | solution.py:524
  (11 shorter events, 0.2 us)
Async XLA Ops:
  0.7 9.8 %collective-permute-start.1 = (bf16[2,4,512]{2,1,0:T(4,128)(2,1)S(1)}, bf16[2,4,512]{2,1,0:T(4,128)(2,1)S(1)}, u32[]{:S(2)}, u32[]{:S(2)}) collective-permute-start(bf16[2,4,512]{2,1,0:T(4,128)(2,1)S(1)} %pad_maximum_fusion.3), channel_id=1, source_target_pairs={{2,0},{4,2},{6,4},{8,6},{10,8},{12,10},{14,12},{16,14},{18,16},{20... | collective-permute-start | bytes 24584 | tf_op jit(solution)/shard_map/ppermute | solution.py:581
  2.0 8.5 %collective-permute-start = (bf16[2,4,512]{2,1,0:T(4,128)(2,1)S(1)}, bf16[2,4,512]{2,1,0:T(4,128)(2,1)S(1)}, u32[]{:S(2)}, u32[]{:S(2)}) collective-permute-start(bf16[2,4,512]{2,1,0:T(4,128)(2,1)S(1)} %pad_maximum_fusion.3), channel_id=1, source_target_pairs={{0,2},{2,4},{4,6},{6,8},{8,10},{10,12},{12,14},{14,16},{16,18},{18... | collective-permute-start | bytes 24584 | tf_op jit(solution)/shard_map/ppermute | solution.py:580
  9.0 1.0 %copy-start = (bf16[3,64,64,3,3]{2,1,4,3,0:T(8,128)(2,1)S(1)}, bf16[3,64,64,3,3]{2,1,4,3,0:T(8,128)(2,1)}, u32[]{:S(2)}) copy-start(bf16[3,64,64,3,3]{2,1,4,3,0:T(8,128)(2,1)} %param.9) | copy-start | bytes 663556
  10.6 1.3 %collective-permute-start.2 = (bf16[2,12,512]{2,1,0:T(8,128)(2,1)S(1)}, bf16[2,12,512]{2,1,0:T(8,128)(2,1)S(1)}, u32[]{:S(2)}, u32[]{:S(2)}) collective-permute-start(bf16[2,12,512]{2,1,0:T(8,128)(2,1)S(1)} %pad_maximum_fusion.2), channel_id=1, source_target_pairs={{0,1},{1,0},{2,3},{3,2},{4,5},{5,4},{6,7},{7,6},{8,9},{9,8},{10,11... | collective-permute-start | bytes 73736 | tf_op jit(solution)/shard_map/ppermute | solution.py:584
  10.8 11.9 %copy-start.1 = (s32[3]{0:T(128)}, s32[3]{0:T(128)S(1)}, u32[]{:S(2)}) copy-start(s32[3]{0:T(128)S(1)} %pad_add_fusion.where_ref.place_ref) | copy-start | bytes 40
  22.7 1.0 %copy-start.3 = (f32[4,512,128]{2,1,0:T(8,128)}, f32[4,512,128]{2,1,0:T(8,128)S(1)}, u32[]{:S(2)}) copy-start(f32[4,512,128]{2,1,0:T(8,128)S(1)} %get-tuple-element.25.cost_hbm) | copy-start | bytes 3145732
  23.7 23.6 %all-to-all-start = ((bf16[16,4,32,128]{3,2,1,0:T(8,128)(2,1)}), bf16[16,4,32,128]{3,2,1,0:T(8,128)(2,1)S(1)}, u32[]{:S(2)}, u32[]{:S(2)}) async-start(bf16[16,4,32,128]{3,2,1,0:T(8,128)(2,1)} %bitcast.13), calls=%async_computation | async-start | bytes 1048576 | tf_op jit(solution)/shard_map/all_to_all | solution.py:629
  46.3 11.1 %copy-start.2 = (s32[3]{0:T(128)S(1)}, s32[3]{0:T(128)}, u32[]{:S(2)}) copy-start(s32[3]{0:T(128)} %copy-done.1) | copy-start | bytes 40
  46.3 11.1 %copy-start.4 = (f32[4,512,128]{2,1,0:T(8,128)S(1)}, f32[4,512,128]{2,1,0:T(8,128)}, u32[]{:S(2)}) copy-start(f32[4,512,128]{2,1,0:T(8,128)} %copy-done.3) | copy-start | bytes 3145732
  46.4 5.0 %collective-permute-start.3 = (f32[16,8,128]{2,1,0:T(8,128)}, f32[16,8,128]{2,1,0:T(8,128)S(1)}, u32[]{:S(2)}, u32[]{:S(2)}) collective-permute-start(f32[16,8,128]{2,1,0:T(8,128)} %get-tuple-element.27), channel_id=1, source_target_pairs={{0,1},{1,0},{2,3},{3,2},{4,5},{5,4},{6,7},{7,6},{8,9},{9,8},{10,11... | collective-permute-start | bytes 196616 | tf_op jit(solution)/shard_map/ppermute | solution.py:633
  51.4 21.5 %all-to-all-start.1 = ((bf16[16,4,32,128]{3,2,1,0:T(8,128)(2,1)}), bf16[16,4,32,128]{3,2,1,0:T(8,128)(2,1)S(1)}, u32[]{:S(2)}, u32[]{:S(2)}) async-start(bf16[16,4,32,128]{3,2,1,0:T(8,128)(2,1)} %bitcast.15), calls=%async_computation.1 | async-start | bytes 1048576 | tf_op jit(solution)/shard_map/all_to_all | solution.py:636
  57.5 1.2 %copy-start.5 = (f32[4,512,128]{2,1,0:T(8,128)S(1)}, f32[4,512,128]{2,1,0:T(8,128)}, u32[]{:S(2)}) copy-start(f32[4,512,128]{2,1,0:T(8,128)} %get-tuple-element.30.rest_1_) | copy-start | bytes 3145732
